TPU v7x, 32 devices: a whole 2x2x4 slice. The times are simulated.
32 devices in a mesh: dp: 2 (over x), row: 4 (over y, core), col: 4 (over z).
Axes of the slice: x: 2, y: 2, z: 4, core: 2. Of those that a mesh axis runs over, the one named last changes fastest.
Arguments:
- tokens: bfloat16 [768, 8192], P('col', ('dp', 'row')), may hold values from -6 to 6
- cotangent: bfloat16 [768, 8192], P('col', ('dp', 'row')), may hold values from -6 to 6
- segment_ids: int32 [8192], P('dp'), may hold values from 0 to 5, as said below
- doc_times: int32 [8, 7], P('dp'), may hold values from 0 to 255
- time_table: float32 [256, 128], replicated, may hold values from -6 to 6
- attn_gain: bfloat16 [768], P('col'), may hold values from 0.5 to 1.5
- mlp_gain: bfloat16 [768], P('col'), may hold values from 0.5 to 1.5
- mod_weight: bfloat16 [6, 768, 128], P(None, 'col'), may hold values from -0.25 to 0.25
- mod_bias: bfloat16 [6, 768], P(None, 'col'), may hold values from -4 to 4
- qkv_weight: bfloat16 [768, 3, 768], P('col', None, 'row'), may hold values from -0.21875 to 0.21875
- proj_weight: bfloat16 [768, 768], P('row', 'col'), may hold values from -3 to 3
- up_weight: bfloat16 [768, 3072], P('col', 'row'), may hold values from -2 to 2
- up_bias: bfloat16 [3072], P('row'), may hold values from -4 to 4
- down_weight: bfloat16 [768, 3072], P('col', 'row'), may hold values from -0.109375 to 0.109375
- down_bias: bfloat16 [768], P('col'), may hold values from -4 to 4
Outputs:
- block_output: bfloat16 [768, 8192], P('col', ('dp', 'row'))
- tokens_grad: bfloat16 [768, 8192], P('col', ('dp', 'row'))
- table_grad: float32 [256, 128], replicated
- attn_gain_grad: float32 [768], P('col')
- mlp_gain_grad: float32 [768], P('col')
- mod_weight_grad: float32 [6, 768, 128], P(None, 'col')
- mod_bias_grad: float32 [6, 768], P(None, 'col')
- qkv_weight_grad: float32 [768, 3, 768], P('col', None, 'row')
- proj_weight_grad: float32 [768, 768], P('row', 'col')
- up_weight_grad: float32 [768, 3072], P('col', 'row')
- up_bias_grad: float32 [3072], P('row')
- down_weight_grad: float32 [768, 3072], P('col', 'row')
- down_bias_grad: float32 [768], P('col')
- stream_rms: float32 [3], replicated
Inputs may be any that keep to these rules, and one draw needn't show every extreme that they name: `segment_ids`: each sequence of 1024 tokens holds whole documents of 200 to min(2000, 1024) tokens with ids 1, 2, 3, ... in order, each a contiguous run, followed by padding with id 0; the first document always fits.
All inputs are finite; a program needn't handle non-finite values.
Results may differ from a plain program's by a relative error of at most 0.023.
Values may be sent and summed in bfloat16 or wider, within the bound.
No kernel may reach another device: no remote copies, remote signals or barrier semaphores. Data moves between devices by JAX's collectives and lax.ppermute only.
A program may use at most 192 MiB of HBM per device.

v0:
```python
import jax
import jax.numpy as jnp
from jax import lax
from jax.sharding import PartitionSpec as P

HEAD_DIM = 64
SEQ = 1024


PRECISE = lax.Precision.HIGHEST
EPSILON = 1e-05
MASK_FILL = -1e30


def doc_positions(seg_rows):
    length = seg_rows.shape[1]
    places = jnp.arange(length, dtype=jnp.int32)[None, :]
    fresh_start = (places == 0) | (seg_rows != jnp.roll(seg_rows, 1, axis=1))
    starts = lax.cummax(jnp.where(fresh_start, places, 0), axis=1)
    return (places - starts).astype(jnp.float32)


def rope_tables(positions, head_size):
    half_size = head_size // 2
    inverse_freq = 1.0 / 10000.0 ** (jnp.arange(half_size, dtype=jnp.float32) * 2.0 / head_size)
    angles = positions[:, None] * inverse_freq[None, :]
    cosine_table = jnp.cos(angles)
    sine_table = jnp.sin(angles)
    return (
        jnp.concatenate([cosine_table, cosine_table], 1),
        jnp.concatenate([sine_table, sine_table], 1),
    )


def rotate(vectors, cosine_table, sine_table):
    half_size = vectors.shape[-1] // 2
    turned = jnp.concatenate([-vectors[..., half_size:], vectors[..., :half_size]], -1)
    return vectors * cosine_table[:, None, :] + turned * sine_table[:, None, :]


def rotate_back(grads, cosine_table, sine_table):
    half_size = grads.shape[-1] // 2
    scaled = grads * sine_table[:, None, :]
    turned_back = jnp.concatenate([scaled[..., half_size:], -scaled[..., :half_size]], -1)
    return grads * cosine_table[:, None, :] + turned_back


def gelu_back(hidden_pre, hidden_grad):

    def activation(inner):
        return jax.nn.gelu(inner, approximate=True)

    return jax.vjp(activation, hidden_pre)[1](hidden_grad)[0]


def col_totals(first, second):
    return lax.psum((jnp.sum(first, axis=1), jnp.sum(second, axis=1)), "col")


def normalize(stream, width):
    row_total, squares = col_totals(stream, stream * stream)
    center = row_total / width
    spread = squares / width - center * center
    inverse = lax.rsqrt(spread + EPSILON)
    return ((stream - center[:, None]) * inverse[:, None], inverse)


def normalize_back(grad_normed, normed, inverse, width):
    row_total, row_along = col_totals(grad_normed, grad_normed * normed)
    return inverse[:, None] * (
        grad_normed - row_total[:, None] / width - normed * (row_along[:, None] / width)
    )


def gather_rows(values):
    return lax.all_gather(values, "row", axis=0, tiled=True)


def gather_cols(values):
    return lax.all_gather(values, "col", axis=0, tiled=True)


def sum_cols(left, right, contract, rows):

    def partial_term(offset, amount):
        return lax.dot_general(
            left, right, (((1,), (contract,)), ((), ())), preferred_element_type=jnp.float32
        )

    return lax.psum_scatter(
        partial_term(jnp.int32(0), lax.axis_size("col") * rows),
        "col",
        scatter_dimension=0,
        tiled=True,
    )


def sum_rows_from(partial_term, rows):
    return lax.psum_scatter(
        partial_term(jnp.int32(0), rows * lax.axis_size("row")).astype(jnp.bfloat16),
        "row",
        scatter_dimension=0,
        tiled=True,
    ).astype(jnp.float32)


def sum_rows(left, right, contract, rows):

    def partial_term(offset, amount):
        return lax.dot_general(
            left, right, (((1,), (contract,)), ((), ())), preferred_element_type=jnp.float32
        )

    return sum_rows_from(partial_term, rows)


def weight_product(left, right):
    return lax.dot_general(
        left, right, (((0,), (0,)), ((), ())), preferred_element_type=jnp.float32
    )


def block_forward(queries, key_vecs, value_vecs, seg_query, seg_keys):
    score_scale = HEAD_DIM ** (-0.5)
    scores = (
        jnp.einsum("qhd,khd->hqk", queries, key_vecs, preferred_element_type=jnp.float32)
        * score_scale
    )
    allowed = (seg_query[:, None] == seg_keys[None, :]) & (seg_keys[None, :] != 0)
    masked = jnp.where(allowed[None], scores, MASK_FILL)
    largest = jnp.max(masked, axis=-1)
    exponent = jnp.where(allowed[None], jnp.exp(masked - largest[..., None]), 0.0)
    padding = (seg_query == 0).astype(jnp.float32)
    denominator = jnp.sum(exponent, axis=-1) + padding[None, :]
    probability = exponent / denominator[..., None]
    mixed_out = jnp.einsum(
        "hqk,khd->qhd",
        probability.astype(jnp.bfloat16),
        value_vecs,
        preferred_element_type=jnp.float32,
    )
    return (mixed_out, largest + jnp.log(denominator))


def block_backward(queries, key_vecs, value_vecs, seg_query, seg_keys, logsum, grad_mixed):
    score_scale = HEAD_DIM ** (-0.5)
    scores = (
        jnp.einsum("qhd,khd->hqk", queries, key_vecs, preferred_element_type=jnp.float32)
        * score_scale
    )
    allowed = (seg_query[:, None] == seg_keys[None, :]) & (seg_keys[None, :] != 0)
    masked = jnp.where(allowed[None], scores, MASK_FILL)
    probability = jnp.where(allowed[None], jnp.exp(masked - logsum[..., None]), 0.0)
    grad_probs = jnp.einsum(
        "qhd,khd->hqk", grad_mixed, value_vecs, preferred_element_type=jnp.float32
    )
    value_grad = jnp.einsum(
        "hqk,qhd->khd",
        probability.astype(jnp.bfloat16),
        grad_mixed,
        preferred_element_type=jnp.float32,
    )
    inner_sum = jnp.sum(probability * grad_probs, axis=-1)
    score_grad = (probability * (grad_probs - inner_sum[..., None])).astype(jnp.bfloat16)
    query_grad = (
        jnp.einsum("hqk,khd->qhd", score_grad, key_vecs, preferred_element_type=jnp.float32)
        * score_scale
    )
    key_grad = (
        jnp.einsum("hqk,qhd->khd", score_grad, queries, preferred_element_type=jnp.float32)
        * score_scale
    )
    return (query_grad, key_grad, value_grad)


def attention_forward(queries, key_vecs, value_vecs, seg_blocks):
    block_rows = min(512, SEQ)
    block_total = SEQ // block_rows

    def one_sequence(packed):
        query_seq, key_seq, value_seq, seg_seq = packed

        def one_block(block_index):
            query_rows = lax.dynamic_slice_in_dim(
                query_seq, block_index * block_rows, block_rows, 0
            )
            seg_query = lax.dynamic_slice_in_dim(seg_seq, block_index * block_rows, block_rows, 0)
            return block_forward(query_rows, key_seq, value_seq, seg_query, seg_seq)

        mixed_out, logsum = lax.map(one_block, jnp.arange(block_total))
        return (mixed_out.reshape(query_seq.shape), logsum)

    return lax.map(one_sequence, (queries, key_vecs, value_vecs, seg_blocks))


def attention_backward(queries, key_vecs, value_vecs, seg_blocks, logsum, grad_mixed):
    block_rows = min(512, SEQ)
    block_total = SEQ // block_rows

    def one_sequence(packed):
        query_seq, key_seq, value_seq, seg_seq, logsum_seq, grad_seq = packed

        def one_block(running, block_index):
            key_total, value_total = running
            query_rows = lax.dynamic_slice_in_dim(
                query_seq, block_index * block_rows, block_rows, 0
            )
            seg_query = lax.dynamic_slice_in_dim(seg_seq, block_index * block_rows, block_rows, 0)
            grad_rows = lax.dynamic_slice_in_dim(grad_seq, block_index * block_rows, block_rows, 0)
            query_grad, key_grad, value_grad = block_backward(
                query_rows,
                key_seq,
                value_seq,
                seg_query,
                seg_seq,
                logsum_seq[block_index],
                grad_rows,
            )
            return ((key_total + key_grad, value_total + value_grad), query_grad)

        empty_grads = jnp.zeros(key_seq.shape, jnp.float32)
        totals, query_parts = lax.scan(
            one_block, (empty_grads, empty_grads), jnp.arange(block_total)
        )
        return (query_parts.reshape(query_seq.shape), totals[0], totals[1])

    return lax.map(one_sequence, (queries, key_vecs, value_vecs, seg_blocks, logsum, grad_mixed))


def per_device(
    tokens,
    cotangent,
    segment_ids,
    doc_times,
    time_table,
    attn_gain,
    mlp_gain,
    mod_weight,
    mod_bias,
    qkv_weight,
    proj_weight,
    up_weight,
    up_bias,
    down_weight,
    down_bias,
):
    col_count = lax.axis_size("col")
    row_index = lax.axis_index("row")
    col_index = lax.axis_index("col")
    group_rows = segment_ids.shape[0]
    first_rows = tokens.shape[1]
    second_rows = group_rows // col_count
    width_local = tokens.shape[0]
    width = width_local * col_count
    head_width = qkv_weight.shape[2]
    heads_local = head_width // HEAD_DIM
    seq_local = second_rows // SEQ
    slot_count = doc_times.shape[1]
    doc_count = doc_times.shape[0] * slot_count
    cond_width = mod_weight.shape[2]
    doc_embed = jnp.take(time_table, doc_times.reshape(-1), axis=0)
    mod_full = (
        mod_weight.astype(jnp.float32).transpose(2, 0, 1).reshape(cond_width, 6 * width_local)
    )
    doc_mods = jnp.dot(doc_embed, mod_full, precision=PRECISE) + mod_bias.astype(
        jnp.float32
    ).reshape(-1)
    first_segs = lax.dynamic_slice_in_dim(segment_ids, row_index * first_rows, first_rows, 0)
    first_places = row_index * first_rows + jnp.arange(first_rows, dtype=jnp.int32)
    doc_slots = first_places // SEQ * slot_count + first_segs
    selector = (doc_slots[:, None] == jnp.arange(doc_count, dtype=jnp.int32)[None, :]).astype(
        jnp.float32
    )
    token_mods = jnp.dot(selector, doc_mods, precision=PRECISE).reshape(first_rows, 6, width_local)
    shift_one = token_mods[:, 0]
    scale_one = token_mods[:, 1]
    gate_one = token_mods[:, 2]
    shift_two = token_mods[:, 3]
    scale_two = token_mods[:, 4]
    gate_two = token_mods[:, 5]
    stream = tokens.T.astype(jnp.float32)
    normed_one, inverse_one = normalize(stream, width)
    gain_one = attn_gain.astype(jnp.float32)
    scaled_one = normed_one * gain_one
    input_one = (scaled_one * (1.0 + scale_one) + shift_one).astype(jnp.bfloat16)
    rows_one = gather_rows(input_one)
    qkv_flat = qkv_weight.reshape(width_local, 3 * head_width)
    projected = sum_cols(rows_one, qkv_flat, 0, second_rows)
    second_segs = lax.dynamic_slice_in_dim(segment_ids, col_index * second_rows, second_rows, 0)
    seg_blocks = second_segs.reshape(seq_local, SEQ)
    cosine_table, sine_table = rope_tables(doc_positions(seg_blocks).reshape(-1), HEAD_DIM)
    split_heads = projected.reshape(second_rows, 3, heads_local, HEAD_DIM)
    queries = rotate(split_heads[:, 0], cosine_table, sine_table).astype(jnp.bfloat16)
    key_vecs = rotate(split_heads[:, 1], cosine_table, sine_table).astype(jnp.bfloat16)
    value_vecs = split_heads[:, 2].astype(jnp.bfloat16)
    seq_shape = (seq_local, SEQ, heads_local, HEAD_DIM)
    query_seqs = queries.reshape(seq_shape)
    key_seqs = key_vecs.reshape(seq_shape)
    value_seqs = value_vecs.reshape(seq_shape)
    mixed_out, logsum = attention_forward(query_seqs, key_seqs, value_seqs, seg_blocks)
    mixed_low = mixed_out.reshape(second_rows, head_width).astype(jnp.bfloat16)
    mixed_rows = gather_cols(mixed_low)
    attn_out = sum_rows(mixed_rows, proj_weight, 0, first_rows)
    middle = stream + gate_one * attn_out
    normed_two, inverse_two = normalize(middle, width)
    gain_two = mlp_gain.astype(jnp.float32)
    scaled_two = normed_two * gain_two
    input_two = (scaled_two * (1.0 + scale_two) + shift_two).astype(jnp.bfloat16)
    rows_two = gather_rows(input_two)
    hidden_pre = sum_cols(rows_two, up_weight, 0, second_rows) + up_bias.astype(jnp.float32)
    hidden_low = jax.nn.gelu(hidden_pre, approximate=True).astype(jnp.bfloat16)
    hidden_rows = gather_cols(hidden_low)
    mlp_out = sum_rows(hidden_rows, down_weight, 1, first_rows) + down_bias.astype(jnp.float32)
    result = middle + gate_two * mlp_out
    block_output = result.T.astype(jnp.bfloat16)
    valid_rows = (first_segs != 0).astype(jnp.float32)[:, None]
    attn_term = gate_one * attn_out
    mlp_term = gate_two * mlp_out
    stat_terms = jnp.stack(
        [
            jnp.sum(valid_rows * result * result),
            jnp.sum(valid_rows * attn_term * attn_term),
            jnp.sum(valid_rows * mlp_term * mlp_term),
            jnp.sum(valid_rows) * width_local,
        ]
    )
    grad_result = cotangent.T.astype(jnp.float32)
    grad_gate_two = grad_result * mlp_out
    grad_branch = (grad_result * gate_two).astype(jnp.bfloat16)
    branch_rows = gather_rows(grad_branch)
    downbias_part = jnp.sum(branch_rows.astype(jnp.float32), axis=0)
    down_grad_part = weight_product(branch_rows, hidden_rows)
    hidden_grad = sum_cols(branch_rows, down_weight, 0, second_rows)
    pre_grad = gelu_back(hidden_pre, hidden_grad).astype(jnp.bfloat16)
    pre_rows = gather_cols(pre_grad)
    upbias_part = jnp.sum(pre_rows.astype(jnp.float32), axis=0)
    up_grad_part = weight_product(rows_two, pre_rows)
    input_grad_two = sum_rows(pre_rows, up_weight, 1, first_rows)
    grad_scaled_two = input_grad_two * (1.0 + scale_two)
    gain_two_part = jnp.sum(grad_scaled_two * normed_two, axis=0)
    grad_middle = grad_result + normalize_back(
        grad_scaled_two * gain_two, normed_two, inverse_two, width
    )
    grad_gate_one = grad_middle * attn_out
    grad_attn = (grad_middle * gate_one).astype(jnp.bfloat16)
    attn_rows = gather_rows(grad_attn)
    proj_grad_part = weight_product(mixed_rows, attn_rows)
    grad_mixed = sum_cols(attn_rows, proj_weight, 1, second_rows).astype(jnp.bfloat16)
    query_grad, key_grad, value_grad = attention_backward(
        query_seqs, key_seqs, value_seqs, seg_blocks, logsum, grad_mixed.reshape(seq_shape)
    )
    head_shape = (second_rows, heads_local, HEAD_DIM)
    query_back = rotate_back(query_grad.reshape(head_shape), cosine_table, sine_table)
    key_back = rotate_back(key_grad.reshape(head_shape), cosine_table, sine_table)
    qkv_grad_low = (
        jnp.stack([query_back, key_back, value_grad.reshape(head_shape)], axis=1)
        .reshape(second_rows, 3 * head_width)
        .astype(jnp.bfloat16)
    )
    qkv_rows = gather_cols(qkv_grad_low)
    qkv_grad_part = weight_product(rows_one, qkv_rows).reshape(width_local, 3, head_width)
    input_grad_one = sum_rows(qkv_rows, qkv_flat, 1, first_rows)
    grad_scaled_one = input_grad_one * (1.0 + scale_one)
    gain_one_part = jnp.sum(grad_scaled_one * normed_one, axis=0)
    grad_stream = grad_middle + normalize_back(
        grad_scaled_one * gain_one, normed_one, inverse_one, width
    )
    tokens_grad = grad_stream.T.astype(jnp.bfloat16)
    token_mod_grads = jnp.stack(
        [
            input_grad_one,
            input_grad_one * scaled_one,
            grad_gate_one,
            input_grad_two,
            input_grad_two * scaled_two,
            grad_gate_two,
        ],
        axis=1,
    ).reshape(first_rows, 6 * width_local)
    doc_mod_grads = lax.dot_general(
        selector, token_mod_grads, (((0,), (0,)), ((), ())), precision=PRECISE
    )
    mod_bias_part = jnp.sum(doc_mod_grads, axis=0).reshape(6, width_local)
    mod_weight_part = (
        lax.dot_general(doc_embed, doc_mod_grads, (((0,), (0,)), ((), ())), precision=PRECISE)
        .reshape(cond_width, 6, width_local)
        .transpose(1, 2, 0)
    )
    embed_grads = lax.dot_general(
        doc_mod_grads, mod_full, (((1,), (1,)), ((), ())), precision=PRECISE
    )
    time_select = (
        doc_times.reshape(-1)[:, None] == jnp.arange(time_table.shape[0], dtype=jnp.int32)[None, :]
    ).astype(jnp.float32)
    table_part = lax.dot_general(
        time_select, embed_grads, (((0,), (0,)), ((), ())), precision=PRECISE
    )
    small_sums = (
        lax.psum(gain_one_part.astype(jnp.bfloat16), ("dp", "row")).astype(jnp.float32),
        lax.psum(gain_two_part.astype(jnp.bfloat16), ("dp", "row")).astype(jnp.float32),
        lax.psum(mod_weight_part.astype(jnp.bfloat16), ("dp", "row")).astype(jnp.float32),
        lax.psum(mod_bias_part.astype(jnp.bfloat16), ("dp", "row")).astype(jnp.float32),
    )
    weight_sums = (
        lax.psum(qkv_grad_part.astype(jnp.bfloat16), "dp").astype(jnp.float32),
        lax.psum(proj_grad_part.astype(jnp.bfloat16), "dp").astype(jnp.float32),
        lax.psum(up_grad_part.astype(jnp.bfloat16), "dp").astype(jnp.float32),
        lax.psum(down_grad_part.astype(jnp.bfloat16), "dp").astype(jnp.float32),
        lax.psum(upbias_part.astype(jnp.bfloat16), "dp").astype(jnp.float32),
        lax.psum(downbias_part.astype(jnp.bfloat16), "dp").astype(jnp.float32),
    )
    global_totals = lax.psum((table_part, stat_terms), ("dp", "row", "col"))
    stream_rms = jnp.sqrt(global_totals[1][:3] / global_totals[1][3])
    return (
        block_output,
        tokens_grad,
        global_totals[0],
        small_sums[0],
        small_sums[1],
        small_sums[2],
        small_sums[3],
        weight_sums[0],
        weight_sums[1],
        weight_sums[2],
        weight_sums[4],
        weight_sums[3],
        weight_sums[5],
        stream_rms,
    )


def solution(mesh):
    return jax.shard_map(
        per_device,
        mesh=mesh,
        in_specs=(
            P("col", ("dp", "row")),
            P("col", ("dp", "row")),
            P("dp"),
            P("dp", None),
            P(),
            P("col"),
            P("col"),
            P(None, "col", None),
            P(None, "col"),
            P("col", None, "row"),
            P("row", "col"),
            P("col", "row"),
            P("row"),
            P("col", "row"),
            P("col"),
        ),
        out_specs=(
            P("col", ("dp", "row")),
            P("col", ("dp", "row")),
            P(),
            P("col"),
            P("col"),
            P(None, "col", None),
            P(None, "col"),
            P("col", None, "row"),
            P("row", "col"),
            P("col", "row"),
            P("row"),
            P("col", "row"),
            P("col"),
            P(),
        ),
        check_vma=False,
    )
```

profile of v0, /device:TPU:0, one launch (start us, length us, event | category | flops | bytes accessed | tf_op | source)
XLA Modules:
  0.0 1624.2 jit_solution(11695370097616547429)
XLA Ops:
  12.5 13.7 all-reduce.3
  37.0 17.7 %all-gather.9.cloned.1.call-done = bf16[4096,192]{0,1:T(8,128)(2,1)} async-done(((bf16[1024,192]{0,1:T(8,128)(2,1)}), bf16[4096,192]{0,1:T(8,128)(2,1)}) %all-gather.9.cloned.1.call-update) | async-done | bytes 1572880 | tf_op jit(solution)/shard_map/all_gather | solution.py:76
  54.7 6.4 fusion.120
  63.9 158.7 %reduce-scatter.9.cloned.1.call-done = f32[1024,576]{0,1:T(8,128)} async-done(((f32[4096,576]{0,1:T(8,128)}), f32[1024,576]{0,1:T(8,128)}) %reduce-scatter.9.cloned.1.call-update) | async-done | bytes 2359312 | tf_op jit(solution)/shard_map/reduce_scatter | solution.py:90
  226.4 17.4 %while.47 = (s32[]{:T(128)}, bf16[2,512,3,64]{1,3,2,0:T(8,128)(2,1)}, f32[2,3,512]{2,1,0:T(4,128)S(1)}, s32[2]{0:T(128)S(1)}, s32[1024]{0:T(1024)S(1)}, /*index=...) while((s32[]{:T(128)}, ...), condition=%wide.region_10.11_spmd, body=%wide.region_7.10_spmd.sunk | while | flops 425725440 | bytes 25587968 | solution.py:190
  246.4 38.0 %all-gather.11.cloned.1.call-done = bf16[4096,192]{0,1:T(8,128)(2,1)} async-done(((bf16[1024,192]{0,1:T(8,128)(2,1)}), bf16[4096,192]{0,1:T(8,128)(2,1)}) %all-gather.11.cloned.1.call-update) | async-done | bytes 1572880 | tf_op jit(solution)/shard_map/all_gather | solution.py:80
  287.9 26.9 %reduce-scatter.11.cloned.1.call-done = bf16[1024,192]{0,1:T(8,128)(2,1)} async-done(((bf16[4096,192]{0,1:T(8,128)(2,1)}), bf16[1024,192]{0,1:T(8,128)(2,1)}) %reduce-scatter.11.cloned.1.call-update) | async-done | bytes 393232 | tf_op jit(solution)/shard_map/reduce_scatter | solution.py:99
  316.3 12.0 all-reduce.2
  331.7 16.4 %all-gather.13.cloned.1.call-done = bf16[4096,192]{0,1:T(8,128)(2,1)} async-done(((bf16[1024,192]{0,1:T(8,128)(2,1)}), bf16[4096,192]{0,1:T(8,128)(2,1)}) %all-gather.13.cloned.1.call-update) | async-done | bytes 1572880 | tf_op jit(solution)/shard_map/all_gather | solution.py:76
  348.1 7.8 fusion.117
  356.0 13.9 all-gather.17.cloned.1.call-done
  369.9 7.8 fusion.118
  378.3 205.9 %reduce-scatter.13.cloned.1.call-done = f32[1024,768]{1,0:T(8,128)} async-done(((f32[4096,768]{1,0:T(8,128)}), f32[1024,768]{1,0:T(8,128)}) %reduce-scatter.13.cloned.1.call-update) | async-done | bytes 3145744 | tf_op jit(solution)/shard_map/reduce_scatter | solution.py:90
  584.2 215.4 %reduce-scatter.17.cloned.1.call-done = f32[1024,768]{1,0:T(8,128)} async-done(((f32[4096,768]{1,0:T(8,128)}), f32[1024,768]{1,0:T(8,128)}) %reduce-scatter.17.cloned.1.call-update) | async-done | bytes 3145744 | tf_op jit(solution)/shard_map/reduce_scatter | solution.py:90
  805.8 115.9 %all-gather.15.cloned.1.call-done = bf16[4096,768]{1,0:T(8,128)(2,1)} async-done(((bf16[1024,768]{1,0:T(8,128)(2,1)}), bf16[4096,768]{1,0:T(8,128)(2,1)}) %all-gather.15.cloned.1.call-update) | async-done | bytes 6291472 | tf_op jit(solution)/shard_map/all_gather | solution.py:80
  921.7 6.1 convolution_convert_fusion.2
  927.9 108.9 %all-gather.19.cloned.1.call-done = bf16[4096,768]{1,0:T(8,128)(2,1)} async-done(((bf16[1024,768]{1,0:T(8,128)(2,1)}), bf16[4096,768]{1,0:T(8,128)(2,1)}) %all-gather.19.cloned.1.call-update) | async-done | bytes 6291472 | tf_op jit(solution)/shard_map/all_gather | solution.py:80
  1036.8 6.1 convolution_convert_fusion.1
  1044.3 21.6 %reduce-scatter.15.cloned.1.call-done = bf16[1024,192]{0,1:T(8,128)(2,1)} async-done(((bf16[4096,192]{0,1:T(8,128)(2,1)}), bf16[1024,192]{0,1:T(8,128)(2,1)}) %reduce-scatter.15.cloned.1.call-update) | async-done | bytes 393232 | tf_op jit(solution)/shard_map/reduce_scatter | solution.py:99
  1065.9 30.6 %reduce-scatter.19.cloned.1.call-done = bf16[1024,192]{0,1:T(8,128)(2,1)} async-done(((bf16[4096,192]{0,1:T(8,128)(2,1)}), bf16[1024,192]{0,1:T(8,128)(2,1)}) %reduce-scatter.19.cloned.1.call-update) | async-done | bytes 393232 | tf_op jit(solution)/shard_map/reduce_scatter | solution.py:99
  1100.4 11.8 all-reduce.1
  1115.2 17.0 %all-gather.21.cloned.1.call-done = bf16[4096,192]{0,1:T(8,128)(2,1)} async-done(((bf16[1024,192]{0,1:T(8,128)(2,1)}), bf16[4096,192]{0,1:T(8,128)(2,1)}) %all-gather.21.cloned.1.call-update) | async-done | bytes 1572880 | tf_op jit(solution)/shard_map/all_gather | solution.py:76
  1136.4 59.9 %reduce-scatter.21.cloned.1.call-done = f32[1024,192]{0,1:T(8,128)} async-done(((f32[4096,192]{0,1:T(8,128)}), f32[1024,192]{0,1:T(8,128)}) %reduce-scatter.21.cloned.1.call-update) | async-done | bytes 786448 | tf_op jit(solution)/shard_map/reduce_scatter | solution.py:90
  1198.2 42.9 %while.48 = (s32[]{:T(128)}, f32[1024,3,64]{0,2,1:T(8,128)S(1)}, f32[1024,3,64]{0,2,1:T(8,128)S(1)}, f32[2,512,3,64]{1,0,3,2:T(2,128)}, s32[2]{0:T(128)S(1)}, /*...) while((s32[]{:T(128)}, f32[1024,3,64]{0,2,1:T(8,128)S(1)}, ...), condition=%wide.region_27.28_spmd.clone, body=%wide.region_25.27_spmd.clone.sunk | while | flops 1024491008 | bytes 58507604 | solution.py:222
  1211.6 8.1 dynamic_update_slice.31
  1233.1 8.1 dynamic_update_slice.31
  1261.1 77.3 %all-gather.23.cloned.1.call-done = bf16[4096,576]{0,1:T(8,128)(2,1)} async-done(((bf16[1024,576]{0,1:T(8,128)(2,1)}), bf16[4096,576]{0,1:T(8,128)(2,1)}) %all-gather.23.cloned.1.call-update) | async-done | bytes 4718608 | tf_op jit(solution)/shard_map/all_gather | solution.py:80
  1363.2 39.0 %psum.159 = f32[4]{0:T(128)S(1)} all-reduce(f32[4]{0:T(128)S(1)} %pad_maximum_fusion.3), channel_id=1, replica_groups=mesh['dp'=2,'row'=4,'col'=4] {'dp','row','col'}, use_global_device_ids=true, to_apply=%region_53.54 | all-reduce | flops 4 | bytes 32 | tf_op jit(solution)/shard_map/psum | solution.py:412
  1422.0 11.9 all-reduce
  1438.8 12.0 all-reduce.4
  1452.6 33.6 %all-reduce.13.cloned.1.call-done = bf16[6,192,128]{2,1,0:T(8,128)(2,1)} async-done(((bf16[6,192,128]{2,1,0:T(8,128)(2,1)}), bf16[6,192,128]{2,1,0:T(8,128)(2,1)}) %all-reduce.13.cloned.1.call-update) | async-done | bytes 294928 | tf_op jit(solution)/shard_map/psum | solution.py:401
  1488.1 127.8 %all-reduce.11.cloned.1.call-done = f32[256,128]{1,0:T(8,128)} async-done(((f32[256,128]{1,0:T(8,128)}), f32[256,128]{1,0:T(8,128)}) %all-reduce.11.cloned.1.call-update) | async-done | bytes 131088 | tf_op jit(solution)/shard_map/psum | solution.py:412
  (301 shorter events, 165.3 us)
Async XLA Ops:
  7.2 362.7 %copy-start = (bf16[192,768]{1,0:T(8,128)(2,1)S(1)}, bf16[192,768]{1,0:T(8,128)(2,1)}, u32[]{:S(2)}) copy-start(bf16[192,768]{1,0:T(8,128)(2,1)} %param.32) | copy-start | bytes 884740
  7.2 47.5 %all-gather.9.cloned.1.call-start = ((), (), s32[]{:S(2)}) async-start(), calls=%async_computation.8 | async-start | bytes 1966080 | tf_op jit(solution)/shard_map/all_gather | solution.py:76
  36.7 185.9 %reduce-scatter.9.cloned.1.call-start = ((), (), s32[]{:S(2)}) async-start(), calls=%async_computation.9 | async-start | bytes 11796480 | tf_op jit(solution)/shard_map/reduce_scatter | solution.py:90
  61.2 223.2 %all-gather.11.cloned.1.call-start = ((), (), s32[]{:S(2)}) async-start(), calls=%async_computation.10 | async-start | bytes 1966080 | tf_op jit(solution)/shard_map/all_gather | solution.py:80
  63.9 161.7 %copy-start.16 = (f32[1024,64]{0,1:T(8,128)}, f32[1024,64]{0,1:T(8,128)S(1)}, u32[]{:S(2)}) copy-start(f32[1024,64]{0,1:T(8,128)S(1)} %get-tuple-element.330) | copy-start | bytes 786436
  63.9 161.7 %copy-start.22 = (f32[1024,64]{0,1:T(8,128)}, f32[1024,64]{0,1:T(8,128)S(1)}, u32[]{:S(2)}) copy-start(f32[1024,64]{0,1:T(8,128)S(1)} %get-tuple-element.331) | copy-start | bytes 786436
  243.8 112.1 %copy-start.6 = (bf16[1024,3,64]{0,2,1:T(8,128)(2,1)}, bf16[1024,3,64]{0,2,1:T(8,128)(2,1)S(1)}, u32[]{:S(2)}) copy-start(bf16[1024,3,64]{0,2,1:T(8,128)(2,1)S(1)} %get-tuple-element.591) | copy-start | bytes 1179652
  246.3 82.0 %copy-start.18 = (bf16[192,1024]{1,0:T(8,128)(2,1)S(1)}, bf16[192,1024]{1,0:T(8,128)(2,1)}, u32[]{:S(2)}) copy-start(bf16[192,1024]{1,0:T(8,128)(2,1)} %param.20) | copy-start | bytes 1179652
  246.3 68.5 %reduce-scatter.11.cloned.1.call-start = ((), (), s32[]{:S(2)}) async-start(), calls=%async_computation.11 | async-start | bytes 1966080 | tf_op jit(solution)/shard_map/reduce_scatter | solution.py:99
  287.6 60.5 %all-gather.13.cloned.1.call-start = ((), (), s32[]{:S(2)}) async-start(), calls=%async_computation.12 | async-start | bytes 1966080 | tf_op jit(solution)/shard_map/all_gather | solution.py:76
  316.3 796.0 %copy-start.2 = (f32[1024,192]{0,1:T(8,128)}, f32[1024,192]{0,1:T(8,128)S(1)}, u32[]{:S(2)}) copy-start(f32[1024,192]{0,1:T(8,128)S(1)} %get-tuple-element.294) | copy-start | bytes 2359300
  331.0 38.8 %all-gather.17.cloned.1.call-start = ((), (), s32[]{:S(2)}) async-start(), calls=%async_computation.16 | async-start | bytes 1966080 | tf_op jit(solution)/shard_map/all_gather | solution.py:76
  331.6 252.6 %reduce-scatter.13.cloned.1.call-start = ((), (), s32[]{:S(2)}) async-start(), calls=%async_computation.13 | async-start | bytes 15728640 | tf_op jit(solution)/shard_map/reduce_scatter | solution.py:90
  355.9 443.7 %reduce-scatter.17.cloned.1.call-start = ((), (), s32[]{:S(2)}) async-start(), calls=%async_computation.17 | async-start | bytes 15728640 | tf_op jit(solution)/shard_map/reduce_scatter | solution.py:90
  377.7 544.0 %all-gather.15.cloned.1.call-start = ((), (), s32[]{:S(2)}) async-start(), calls=%async_computation.14 | async-start | bytes 7864320 | tf_op jit(solution)/shard_map/all_gather | solution.py:80
  805.1 231.7 %all-gather.19.cloned.1.call-start = ((), (), s32[]{:S(2)}) async-start(), calls=%async_computation.18 | async-start | bytes 7864320 | tf_op jit(solution)/shard_map/all_gather | solution.py:80
  805.7 260.2 %reduce-scatter.15.cloned.1.call-start = ((), (), s32[]{:S(2)}) async-start(), calls=%async_computation.15 | async-start | bytes 1966080 | tf_op jit(solution)/shard_map/reduce_scatter | solution.py:99
  927.8 115.2 %copy-start.53 = (bf16[192]{0:T(256)(128)(2,1)S(1)}, bf16[192]{0:T(256)(128)(2,1)}, u32[]{:S(2)}) copy-start(bf16[192]{0:T(256)(128)(2,1)} %param.33) | copy-start | bytes 1156
  927.8 168.7 %copy-start.20 = (bf16[1024,192]{0,1:T(8,128)(2,1)S(1)}, bf16[1024,192]{0,1:T(8,128)(2,1)}, u32[]{:S(2)}) copy-start(bf16[1024,192]{0,1:T(8,128)(2,1)} %reduce-scatter.11.cloned.1.call-done) | copy-start | bytes 1179652
  927.9 168.7 %reduce-scatter.19.cloned.1.call-start = ((), (), s32[]{:S(2)}) async-start(), calls=%async_computation.19 | async-start | bytes 1966080 | tf_op jit(solution)/shard_map/reduce_scatter | solution.py:99
  1042.9 89.3 %all-gather.21.cloned.1.call-start = ((), (), s32[]{:S(2)}) async-start(), calls=%async_computation.20 | async-start | bytes 1966080 | tf_op jit(solution)/shard_map/all_gather | solution.py:76
  1115.1 81.1 %reduce-scatter.21.cloned.1.call-start = ((), (), s32[]{:S(2)}) async-start(), calls=%async_computation.21 | async-start | bytes 3932160 | tf_op jit(solution)/shard_map/reduce_scatter | solution.py:90
  1135.9 202.5 %all-gather.23.cloned.1.call-start = ((), (), s32[]{:S(2)}) async-start(), calls=%async_computation.22 | async-start | bytes 5898240 | tf_op jit(solution)/shard_map/all_gather | solution.py:80
  1248.8 155.1 %all-reduce.15.cloned.1.call-start = ((), (), s32[]{:S(2)}) async-start(), calls=%async_computation.26 | async-start | bytes 1966080 | tf_op jit(solution)/shard_map/psum | solution.py:405
  1259.9 78.5 %copy-start.27 = (bf16[4096,192]{0,1:T(8,128)(2,1)S(1)}, bf16[4096,192]{0,1:T(8,128)(2,1)}, u32[]{:S(2)}) copy-start(bf16[4096,192]{0,1:T(8,128)(2,1)} %all-gather.9.cloned.1.call-done) | copy-start | bytes 4718596
  1261.1 84.1 %copy-start.26 = (bf16[192,3,192]{0,2,1:T(8,128)(2,1)S(1)}, bf16[192,3,192]{0,2,1:T(8,128)(2,1)}, u32[]{:S(2)}) copy-start(bf16[192,3,192]{0,2,1:T(8,128)(2,1)} %copy-done.25) | copy-start | bytes 663556
  1345.1 68.6 %reduce-scatter.23.cloned.1.call-start = ((), (), s32[]{:S(2)}) async-start(), calls=%async_computation.23 | async-start | bytes 1966080 | tf_op jit(solution)/shard_map/reduce_scatter | solution.py:99
  1350.1 136.1 %all-reduce.13.cloned.1.call-start = ((), (), s32[]{:S(2)}) async-start(), calls=%async_computation.25 | async-start | bytes 589824 | tf_op jit(solution)/shard_map/psum | solution.py:401
  1354.9 61.2 %copy-start.11 = (f32[1024,192]{0,1:T(8,128)S(1)}, f32[1024,192]{0,1:T(8,128)}, u32[]{:S(2)}) copy-start(f32[1024,192]{0,1:T(8,128)} %get-tuple-element.293) | copy-start | bytes 2359300
  1354.9 61.2 %copy-start.21 = (bf16[1024,192]{0,1:T(8,128)(2,1)S(1)}, bf16[1024,192]{0,1:T(8,128)(2,1)}, u32[]{:S(2)}) copy-start(bf16[1024,192]{0,1:T(8,128)(2,1)} %reduce-scatter.11.cloned.1.call-done) | copy-start | bytes 1179652
  1419.7 197.8 %copy-start.1 = (bf16[192,768]{1,0:T(8,128)(2,1)S(1)}, bf16[192,768]{1,0:T(8,128)(2,1)}, u32[]{:S(2)}) copy-start(bf16[192,768]{1,0:T(8,128)(2,1)} %param.32) | copy-start | bytes 884740
  1435.8 180.1 %all-reduce.11.cloned.1.call-start = ((), (), s32[]{:S(2)}) async-start(), calls=%async_computation.24 | async-start | bytes 262144 | tf_op jit(solution)/shard_map/psum | solution.py:412
  (45 other events, 669.3 us)
Sparse Core Ops, SparseCore 0:
  36.8 17.8 all-gather.8
  61.3 161.2 reduce-scatter.8
  246.4 37.9 all-gather.10
  287.7 27.0 reduce-scatter.10
  331.1 16.9 all-gather.12
  350.2 19.6 all-gather.16
  372.3 211.8 reduce-scatter.12
  586.7 212.8 reduce-scatter.16
  805.3 116.3 all-gather.14
  923.2 113.5 all-gather.18
  1039.5 26.3 reduce-scatter.14
  1068.3 28.1 reduce-scatter.18
  1115.3 16.9 all-gather.20
  1136.0 60.2 reduce-scatter.20
  1248.9 89.4 all-gather.22
  1345.2 37.7 all-reduce.14
  1385.4 28.1 reduce-scatter.22
  1435.9 50.3 all-reduce.12
  1493.3 122.5 all-reduce.10
where the time goes:
time: 1640 us; the launch traced here: 1620 us
  waiting for transfers between devices  1290 us (79%)
  blocking collectives  105 us (6%)
  matrix products  98.2 us (6%)
  other arithmetic  62.4 us (4%)
  local copies, waits for them, and re-layouts  43.9 us (3%)
    reduce_scatter x4, waiting for transfers between devices, sum_cols(): lax.psum_scatter(partial_term(jnp.int32(0), lax.axis_size('col') * rows),...  640 us
    all_gather x4, waiting for transfers between devices, gather_cols(): return lax.all_gather(values, 'col', axis=0, tiled=True)  340 us
    psum x1, waiting for transfers between devices, per_device(): global_totals = lax.psum((table_part, stat_terms), ('dp', 'row', 'col'))  128 us
    reduce_scatter x4, waiting for transfers between devices, sum_rows_from(): lax.psum_scatter(partial_term(jnp.int32(0), rows * lax.axis_size('row'))....  81.7 us
    all_gather x4, waiting for transfers between devices, gather_rows(): return lax.all_gather(values, 'row', axis=0, tiled=True)  65.1 us
    psum x4, blocking collectives, col_totals(): return lax.psum((jnp.sum(first, axis=1), jnp.sum(second, axis=1)), 'col')  49.3 us
    dot_general x8, matrix products, partial_term(): lax.dot_general(left, right, (((1,), (contract,)), ((), ())), preferred_e...  46 us
    psum x1, blocking collectives, per_device(): global_totals = lax.psum((table_part, stat_terms), ('dp', 'row', 'col'))  39 us
  transfers between devices with their start and end apart: 19, of which 18 were waited for; matrix products, arithmetic and copies ran while one was open for 4% of the time, Pallas kernels for 0%

commit v1 on v0

v1 whole, which is shorter than its diff:
```python
import jax
import jax.numpy as jnp
from jax import lax
from jax.sharding import PartitionSpec as P

HEAD_DIM = 64
SEQ = 1024

PRECISE = lax.Precision.HIGHEST
EPSILON = 1e-05
MASK_FILL = -1e30
LOW = jnp.bfloat16
FULL = jnp.float32


def swap(values, axis, bit):
    count = lax.axis_size(axis)
    return lax.ppermute(values, axis, [(i, i ^ bit) for i in range(count)])


def row_bits():
    count = lax.axis_size("row")
    bits = []
    bit = 1
    while bit < count:
        bits.append(bit)
        bit *= 2
    return bits


def gather_rows(values):
    for bit in reversed(row_bits()):
        values = jnp.concatenate([values, swap(values, "row", bit)], 0)
    return values


def xor_order():
    order = [0]
    for bit in reversed(row_bits()):
        order = order + [o ^ bit for o in order]
    return order


def scatter_rows(values):
    for bit in row_bits():
        half = values.shape[0] // 2
        received = swap(values[half:], "row", bit)
        values = (values[:half].astype(FULL) + received.astype(FULL)).astype(LOW)
    return values.astype(FULL)


def col_of_row(row_count):
    if row_count == 4:
        return [0, 2, 1, 3]
    return list(range(row_count))


def relayout_pairs(step):
    row_count = lax.axis_size("row")
    col_count = lax.axis_size("col")
    per_row = col_count // row_count
    table = col_of_row(row_count)
    pairs = []
    for r in range(row_count):
        for c in range(col_count):
            j, q = divmod((c + step) % col_count, row_count)
            pairs.append((r * col_count + c, q * col_count + table[r] * per_row + j))
    return pairs


def relayout_in(values):
    row_count = lax.axis_size("row")
    col_count = lax.axis_size("col")
    col_index = lax.axis_index("col")
    row_index = lax.axis_index("row")
    per_row = col_count // row_count
    width_local = values.shape[0]
    own = values.shape[1] // col_count
    table = jnp.array(col_of_row(row_count), jnp.int32)
    chunks = values.reshape(width_local, col_count, own)
    result = jnp.zeros((width_local * col_count, own), values.dtype)
    mine = col_index % per_row * row_count + row_index
    for step in range(col_count):
        piece = lax.dynamic_index_in_dim(chunks, (col_index + step) % col_count, 1, False)
        got = lax.ppermute(piece, ("row", "col"), relayout_pairs(step))
        source = (mine - step) % col_count
        result = lax.dynamic_update_slice(result, got, (source * width_local, 0))
    return result


def relayout_out(values):
    row_count = lax.axis_size("row")
    col_count = lax.axis_size("col")
    col_index = lax.axis_index("col")
    row_index = lax.axis_index("row")
    per_row = col_count // row_count
    width_local = values.shape[0] // col_count
    own = values.shape[1]
    result = jnp.zeros((width_local, col_count, own), values.dtype)
    mine = col_index % per_row * row_count + row_index
    for step in range(col_count):
        source = (mine - step) % col_count
        piece = lax.dynamic_slice_in_dim(values, source * width_local, width_local, 0)
        got = lax.ppermute(
            piece, ("row", "col"), [(b, a) for a, b in relayout_pairs(step)]
        )
        result = lax.dynamic_update_slice(
            result, got[:, None, :], (0, (col_index + step) % col_count, 0)
        )
    return result.reshape(width_local, col_count * own)


def rope_tables(positions, head_size):
    half_size = head_size // 2
    inverse_freq = 1.0 / 10000.0 ** (jnp.arange(half_size, dtype=FULL) * 2.0 / head_size)
    angles = positions[:, None] * inverse_freq[None, :]
    cosine_table = jnp.cos(angles)
    sine_table = jnp.sin(angles)
    return (
        jnp.concatenate([cosine_table, cosine_table], 1),
        jnp.concatenate([sine_table, sine_table], 1),
    )


def rotate(vectors, cosine_table, sine_table):
    half_size = vectors.shape[-1] // 2
    turned = jnp.concatenate([-vectors[..., half_size:], vectors[..., :half_size]], -1)
    return vectors * cosine_table[:, None, :] + turned * sine_table[:, None, :]


def rotate_back(grads, cosine_table, sine_table):
    half_size = grads.shape[-1] // 2
    scaled = grads * sine_table[:, None, :]
    turned_back = jnp.concatenate([scaled[..., half_size:], -scaled[..., :half_size]], -1)
    return grads * cosine_table[:, None, :] + turned_back


def gelu_back(hidden_pre, hidden_grad):

    def activation(inner):
        return jax.nn.gelu(inner, approximate=True)

    return jax.vjp(activation, hidden_pre)[1](hidden_grad)[0]


def normalize(stream):
    center = jnp.mean(stream, axis=1, keepdims=True)
    offset = stream - center
    inverse = lax.rsqrt(jnp.mean(offset * offset, axis=1, keepdims=True) + EPSILON)
    return offset * inverse, inverse


def normalize_back(grad_normed, normed, inverse):
    center = jnp.mean(grad_normed, axis=1, keepdims=True)
    along = jnp.mean(grad_normed * normed, axis=1, keepdims=True)
    return inverse * (grad_normed - center - normed * along)


def dot(left, right, left_dim, right_dim):
    return lax.dot_general(
        left, right, (((left_dim,), (right_dim,)), ((), ())), preferred_element_type=FULL
    )


def attention_forward(queries, key_vecs, value_vecs, segs):
    score_scale = HEAD_DIM ** (-0.5)
    scores = jnp.einsum("qhd,khd->hqk", queries, key_vecs, preferred_element_type=FULL) * score_scale
    allowed = (segs[:, None] == segs[None, :]) & (segs[None, :] != 0)
    masked = jnp.where(allowed[None], scores, MASK_FILL)
    largest = jnp.max(masked, axis=-1)
    exponent = jnp.where(allowed[None], jnp.exp(masked - largest[..., None]), 0.0)
    padding = (segs == 0).astype(FULL)
    denominator = jnp.sum(exponent, axis=-1) + padding[None, :]
    probability = exponent / denominator[..., None]
    mixed_out = jnp.einsum(
        "hqk,khd->qhd", probability.astype(LOW), value_vecs, preferred_element_type=FULL
    )
    return mixed_out, largest + jnp.log(denominator)


def attention_backward(queries, key_vecs, value_vecs, segs, logsum, grad_mixed):
    score_scale = HEAD_DIM ** (-0.5)
    scores = jnp.einsum("qhd,khd->hqk", queries, key_vecs, preferred_element_type=FULL) * score_scale
    allowed = (segs[:, None] == segs[None, :]) & (segs[None, :] != 0)
    masked = jnp.where(allowed[None], scores, MASK_FILL)
    probability = jnp.where(allowed[None], jnp.exp(masked - logsum[..., None]), 0.0)
    grad_probs = jnp.einsum("qhd,khd->hqk", grad_mixed, value_vecs, preferred_element_type=FULL)
    value_grad = jnp.einsum(
        "hqk,qhd->khd", probability.astype(LOW), grad_mixed, preferred_element_type=FULL
    )
    inner_sum = jnp.sum(probability * grad_probs, axis=-1)
    score_grad = (probability * (grad_probs - inner_sum[..., None])).astype(LOW)
    query_grad = (
        jnp.einsum("hqk,khd->qhd", score_grad, key_vecs, preferred_element_type=FULL) * score_scale
    )
    key_grad = (
        jnp.einsum("hqk,qhd->khd", score_grad, queries, preferred_element_type=FULL) * score_scale
    )
    return query_grad, key_grad, value_grad


def per_device(
    tokens,
    cotangent,
    segment_ids,
    doc_times,
    time_table,
    attn_gain,
    mlp_gain,
    mod_weight,
    mod_bias,
    qkv_weight,
    proj_weight,
    up_weight,
    up_bias,
    down_weight,
    down_bias,
):
    row_count = lax.axis_size("row")
    col_count = lax.axis_size("col")
    row_index = lax.axis_index("row")
    col_index = lax.axis_index("col")
    per_row = col_count // row_count
    width_local = tokens.shape[0]
    width = width_local * col_count
    own = tokens.shape[1] // col_count
    head_width = qkv_weight.shape[2]
    heads_local = head_width // HEAD_DIM
    slot_count = doc_times.shape[1]
    cond_width = mod_weight.shape[2]
    if segment_ids.shape[0] != col_count * SEQ or own * row_count != SEQ:
        raise ValueError("sequence split")

    table = col_of_row(row_count)
    seq_of_col = [0] * col_count
    for r in range(row_count):
        for j in range(per_row):
            seq_of_col[table[r] * per_row + j] = r * per_row + j
    seq_segs = segment_ids.reshape(col_count, SEQ)[jnp.array(seq_of_col)]
    seq_times = doc_times[jnp.array(seq_of_col)]

    segs_natural = lax.dynamic_index_in_dim(seq_segs, col_index, 0, False)
    places = jnp.arange(SEQ, dtype=jnp.int32)
    slots = jnp.arange(slot_count, dtype=jnp.int32)
    starts = jnp.min(
        jnp.where(segs_natural[None, :] == slots[:, None], places[None, :], SEQ), axis=1
    )
    start_of = jnp.sum(jnp.where(segs_natural[None, :] == slots[:, None], starts[:, None], 0), axis=0)
    positions_natural = (places - start_of).astype(FULL)
    order = jnp.array(xor_order(), jnp.int32) ^ row_index
    segs = segs_natural.reshape(row_count, own)[order].reshape(-1)
    positions = positions_natural.reshape(row_count, own)[order].reshape(-1)
    own_segs = segs[:own]

    doc_embed = jnp.take(time_table, seq_times.reshape(-1), axis=0)
    mod_full = mod_weight.astype(FULL).transpose(2, 0, 1).reshape(cond_width, 6 * width_local)
    doc_mods_part = jnp.dot(doc_embed, mod_full, precision=PRECISE) + mod_bias.astype(FULL).reshape(-1)
    doc_mods_part = doc_mods_part.reshape(col_count, slot_count * 6, width_local)
    vectors = jnp.stack([attn_gain, mlp_gain, down_bias]).astype(FULL)
    mods_send = jnp.concatenate(
        [doc_mods_part, jnp.broadcast_to(vectors[None], (col_count,) + vectors.shape)], 1
    )
    mods_got = lax.all_to_all(mods_send, "col", 0, 2, tiled=True).reshape(-1, width)
    doc_mods = mods_got[: slot_count * 6].reshape(slot_count, 6 * width)
    gain_one, gain_two, down_bias_full = mods_got[-3], mods_got[-2], mods_got[-1]
    selector = (own_segs[:, None] == slots[None, :]).astype(FULL)
    token_mods = jnp.dot(selector, doc_mods, precision=PRECISE).reshape(own, 6, width)
    shift_one, scale_one, gate_one, shift_two, scale_two, gate_two = [
        token_mods[:, i] for i in range(6)
    ]

    def gather_cols(values):
        return lax.all_gather(values, "col", axis=0, tiled=True)

    qkv_full = gather_cols(qkv_weight.reshape(width_local, 3 * head_width))
    proj_full = gather_cols(proj_weight.T)
    up_full = gather_cols(up_weight)
    down_full = gather_cols(down_weight)

    stream = relayout_in(tokens).T.astype(FULL)
    normed_one, inverse_one = normalize(stream)
    scaled_one = normed_one * gain_one
    input_one = (scaled_one * (1.0 + scale_one) + shift_one).astype(LOW)
    rows_one = gather_rows(input_one)
    projected = dot(rows_one, qkv_full, 1, 0)
    cosine_table, sine_table = rope_tables(positions, HEAD_DIM)
    split_heads = projected.reshape(SEQ, 3, heads_local, HEAD_DIM)
    queries = rotate(split_heads[:, 0], cosine_table, sine_table).astype(LOW)
    key_vecs = rotate(split_heads[:, 1], cosine_table, sine_table).astype(LOW)
    value_vecs = split_heads[:, 2].astype(LOW)
    mixed_out, logsum = attention_forward(queries, key_vecs, value_vecs, segs)
    mixed = mixed_out.reshape(SEQ, head_width).astype(LOW)
    attn_out = scatter_rows(dot(mixed, proj_full, 1, 1).astype(LOW))

    grad_result = relayout_in(cotangent).T.astype(FULL)
    grad_branch = (grad_result * gate_two).astype(LOW)
    branch_rows = gather_rows(grad_branch)

    middle = stream + gate_one * attn_out
    normed_two, inverse_two = normalize(middle)
    scaled_two = normed_two * gain_two
    input_two = (scaled_two * (1.0 + scale_two) + shift_two).astype(LOW)
    rows_two = gather_rows(input_two)
    hidden_pre = dot(rows_two, up_full, 1, 0) + up_bias.astype(FULL)
    hidden = jax.nn.gelu(hidden_pre, approximate=True).astype(LOW)
    mlp_out = scatter_rows(dot(hidden, down_full, 1, 1).astype(LOW)) + down_bias_full

    hidden_grad = dot(branch_rows, down_full, 1, 0)
    pre_grad = gelu_back(hidden_pre, hidden_grad).astype(LOW)
    input_grad_two = scatter_rows(dot(pre_grad, up_full, 1, 1).astype(LOW))
    down_grad_part = dot(branch_rows, hidden, 0, 0)
    up_grad_part = dot(rows_two, pre_grad, 0, 0)
    up_bias_part = jnp.sum(pre_grad.astype(FULL), axis=0)

    result = middle + gate_two * mlp_out
    block_output = relayout_out(result.astype(LOW).T)
    valid_rows = (own_segs != 0).astype(FULL)[:, None]
    attn_term = gate_one * attn_out
    mlp_term = gate_two * mlp_out
    stat_terms = jnp.stack(
        [
            jnp.sum(valid_rows * result * result),
            jnp.sum(valid_rows * attn_term * attn_term),
            jnp.sum(valid_rows * mlp_term * mlp_term),
            jnp.sum(valid_rows) * width,
        ]
    )
    grad_gate_two = grad_result * mlp_out
    down_bias_part = jnp.sum(grad_branch.astype(FULL), axis=0)

    grad_scaled_two = input_grad_two * (1.0 + scale_two)
    gain_two_part = jnp.sum(grad_scaled_two * normed_two, axis=0)
    grad_middle = grad_result + normalize_back(grad_scaled_two * gain_two, normed_two, inverse_two)
    grad_gate_one = grad_middle * attn_out
    grad_attn = (grad_middle * gate_one).astype(LOW)
    attn_rows = gather_rows(grad_attn)
    proj_grad_part = dot(attn_rows, mixed, 0, 0)
    grad_mixed = dot(attn_rows, proj_full, 1, 0).astype(LOW)
    query_grad, key_grad, value_grad = attention_backward(
        queries, key_vecs, value_vecs, segs, logsum, grad_mixed.reshape(SEQ, heads_local, HEAD_DIM)
    )
    query_back = rotate_back(query_grad, cosine_table, sine_table)
    key_back = rotate_back(key_grad, cosine_table, sine_table)
    qkv_grad = (
        jnp.stack([query_back, key_back, value_grad], axis=1).reshape(SEQ, 3 * head_width).astype(LOW)
    )
    qkv_grad_part = dot(rows_one, qkv_grad, 0, 0)
    input_grad_one = scatter_rows(dot(qkv_grad, qkv_full, 1, 1).astype(LOW))
    grad_scaled_one = input_grad_one * (1.0 + scale_one)
    gain_one_part = jnp.sum(grad_scaled_one * normed_one, axis=0)
    grad_stream = grad_middle + normalize_back(grad_scaled_one * gain_one, normed_one, inverse_one)
    tokens_grad = relayout_out(grad_stream.astype(LOW).T)

    def sum_weight(part):
        part = lax.psum_scatter(part.astype(LOW), "col", scatter_dimension=0, tiled=True)
        return sum_dp(part)

    def sum_dp(part):
        total = part.astype(FULL)
        bit = 1
        while bit < lax.axis_size("dp"):
            total = total + swap(total.astype(LOW), "dp", bit).astype(FULL)
            bit *= 2
        return total

    qkv_out = sum_weight(qkv_grad_part).reshape(width_local, 3, head_width)
    proj_out = sum_weight(proj_grad_part).T
    up_out = sum_weight(up_grad_part)
    down_out = sum_weight(down_grad_part)
    up_bias_out = lax.psum(up_bias_part.astype(LOW), ("dp", "col")).astype(FULL)

    token_mod_grads = jnp.stack(
        [
            input_grad_one,
            input_grad_one * scaled_one,
            grad_gate_one,
            input_grad_two,
            input_grad_two * scaled_two,
            grad_gate_two,
        ],
        axis=1,
    ).reshape(own, 6 * width)
    doc_grads = lax.dot_general(
        selector, token_mod_grads, (((0,), (0,)), ((), ())), precision=PRECISE
    )
    small = jnp.concatenate(
        [
            doc_grads.reshape(slot_count * 6, width),
            jnp.stack([gain_one_part, gain_two_part, down_bias_part]),
        ],
        0,
    )
    small = lax.psum(small, "row")
    small = lax.all_to_all(
        small.reshape(1, -1, col_count, width_local).transpose(2, 1, 0, 3), "col", 0, 0, tiled=True
    )[:, :, 0]
    small = lax.all_gather(small, "dp", axis=0, tiled=True)
    all_embed = lax.all_gather(doc_embed, "dp", axis=0, tiled=True)
    all_times = lax.all_gather(seq_times, "dp", axis=0, tiled=True)
    vector_out = jnp.sum(small[:, slot_count * 6 :], axis=0)
    slot_grads = small[:, : slot_count * 6].reshape(-1, 6 * width_local)
    mod_bias_out = jnp.sum(slot_grads, axis=0).reshape(6, width_local)
    mod_weight_out = (
        lax.dot_general(slot_grads, all_embed, (((0,), (0,)), ((), ())), precision=PRECISE)
    ).reshape(6, width_local, cond_width)
    embed_grads = lax.dot_general(slot_grads, mod_full, (((1,), (1,)), ((), ())), precision=PRECISE)
    time_select = (
        all_times.reshape(-1)[:, None] == jnp.arange(time_table.shape[0], dtype=jnp.int32)[None, :]
    ).astype(FULL)
    embed_grads = lax.psum(embed_grads, "col")
    table_out = lax.dot_general(
        time_select, embed_grads, (((0,), (0,)), ((), ())), precision=PRECISE
    )
    stats = lax.psum(stat_terms, ("dp", "row", "col"))
    stream_rms = jnp.sqrt(stats[:3] / stats[3])
    return (
        block_output,
        tokens_grad,
        table_out,
        vector_out[0],
        vector_out[1],
        mod_weight_out,
        mod_bias_out,
        qkv_out,
        proj_out,
        up_out,
        up_bias_out,
        down_out,
        vector_out[2],
        stream_rms,
    )


def solution(mesh):
    return jax.shard_map(
        per_device,
        mesh=mesh,
        in_specs=(
            P("col", ("dp", "row")),
            P("col", ("dp", "row")),
            P("dp"),
            P("dp", None),
            P(),
            P("col"),
            P("col"),
            P(None, "col", None),
            P(None, "col"),
            P("col", None, "row"),
            P("row", "col"),
            P("col", "row"),
            P("row"),
            P("col", "row"),
            P("col"),
        ),
        out_specs=(
            P("col", ("dp", "row")),
            P("col", ("dp", "row")),
            P(),
            P("col"),
            P("col"),
            P(None, "col", None),
            P(None, "col"),
            P("col", None, "row"),
            P("row", "col"),
            P("col", "row"),
            P("row"),
            P("col", "row"),
            P("col"),
            P(),
        ),
        check_vma=False,
    )
```

time: 1640 us -> 525 us (0.32)
  waiting for transfers between devices: 1290 us -> 103 us
  starting transfers between devices: 1.58 us -> 66.6 us
  blocking collectives: 105 us -> 130 us
  matrix products: 98.2 us -> 73.3 us
  local copies, waits for them, and re-layouts: 43.9 us -> 66.1 us
    reduce_scatter x8 -> x4, waiting for transfers between devices: 722 us -> 0.02 us  [sum_weight(): lax.psum_scatter(part.astype(LOW), 'col', scatter_dimension=0, tiled=True)]
    all_gather x4 -> x2, waiting for transfers between devices: 340 us -> 0.02 us  [gather_cols(): return lax.all_gather(values, 'col', axis=0, tiled=True)]
    psum x3 -> x1, waiting for transfers between devices: 161 us -> 11.7 us  [per_device(): small = lax.psum(small, 'row')]
    ppermute x0 -> x36, waiting for transfers between devices: none -> 81.6 us  [the longest x20 58.4 us: swap(): return lax.ppermute(values, axis, [(i, i ^ bit) for i in range(count)])]
    all_gather x4 -> x0, waiting for transfers between devices: 65.1 us -> none  [gather_rows(): return lax.all_gather(values, 'row', axis=0, tiled=True)]
    ppermute x0 -> x36, starting transfers between devices: none -> 58.2 us  [the longest x8 23.4 us: relayout_in(): got = lax.ppermute(piece, ('row', 'col'), relayout_pairs(step))]
    all_gather x0 -> x5, blocking collectives: none -> 52.1 us  [the longest x2 37.2 us: gather_cols(): return lax.all_gather(values, 'col', axis=0, tiled=True)]
    psum x7 -> x3, blocking collectives: 105 us -> 77.9 us  [the longest x1 41.6 us: per_device(): stats = lax.psum(stat_terms, ('dp', 'row', 'col'))]
  transfers between devices with their start and end apart: 19 -> 45, of which waited for: 18 -> 14; matrix products, arithmetic and copies ran while one was open for 4% -> 36% of each run, Pallas kernels for 0% -> 0%
where the time goes in v1:
time: 525 us; the launch traced here: 516 us
  blocking collectives  130 us (25%)
  waiting for transfers between devices  103 us (20%)
  matrix products  73.3 us (14%)
  starting transfers between devices  66.6 us (13%)
  local copies, waits for them, and re-layouts  66.1 us (13%)
  other arithmetic  60.4 us (12%)
  between operations  16.7 us (3%)
    ppermute x20, waiting for transfers between devices, swap(): return lax.ppermute(values, axis, [(i, i ^ bit) for i in range(count)])  58.4 us
    psum x1, blocking collectives, per_device(): stats = lax.psum(stat_terms, ('dp', 'row', 'col'))  41.6 us
    all_gather x2, blocking collectives, gather_cols(): return lax.all_gather(values, 'col', axis=0, tiled=True)  37.2 us
    dot_general x12, matrix products, dot(): lax.dot_general(left, right, (((left_dim,), (right_dim,)), ((), ())), pre...  36.9 us
    ppermute x8, starting transfers between devices, relayout_in(): got = lax.ppermute(piece, ('row', 'col'), relayout_pairs(step))  23.4 us
    ppermute x8, waiting for transfers between devices, relayout_in(): got = lax.ppermute(piece, ('row', 'col'), relayout_pairs(step))  23.1 us
    ppermute x8, starting transfers between devices, relayout_out(): lax.ppermute(piece, ('row', 'col'), [(b, a) for a, b in relayout_pairs(st...  21.7 us
    psum x1, blocking collectives, per_device(): embed_grads = lax.psum(embed_grads, 'col')  19.1 us
  transfers between devices with their start and end apart: 45, of which 14 were waited for; matrix products, arithmetic and copies ran while one was open for 36% of the time, Pallas kernels for 0%

profile of v1, /device:TPU:0, one launch (start us, length us, event | category | flops | bytes accessed | tf_op | source)
XLA Modules:
  0.0 516.0 jit_solution(12304051883263717855)
XLA Ops:
  9.3 7.3 %collective-permute-start.1 = (bf16[192,256]{0,1:T(8,128)(2,1)S(1)}, bf16[192,256]{0,1:T(8,128)(2,1)S(1)}, u32[]{:S(2)}, u32[]{:S(2)}) collective-permute-start(bf16[192,256]{0,1:T(8,128)(2,1)S(1)} %get-tuple-element.160), channel_id=1, source_target_pairs={{0,4},{1,8},{2,12},{3,0},{4,6},{5,10},{6,14},{7,2},{8,5},{9,9},{10... | collective-permute-start | bytes 294920 | tf_op jit(solution)/shard_map/ppermute | solution.py:85
  29.8 4.2 all-to-all-start
  51.4 9.1 %collective-permute-done.4 = bf16[256,768]{1,0:T(8,128)(2,1)S(1)} collective-permute-done((bf16[256,768]{1,0:T(8,128)(2,1)S(1)}, bf16[256,768]{1,0:T(8,128)(2,1)S(1)}, u32[]{:S(2)}, u32[]{:S(2)}) %collective-permute-start.4) | collective-permute-done | bytes 393248 | tf_op jit(solution)/shard_map/ppermute | solution.py:18
  61.5 15.9 %all_gather.22 = bf16[768,192]{1,0:T(8,128)(2,1)S(1)} all-gather(bf16[192,192]{1,0:T(8,128)(2,1)S(1)} %bitcast.312), channel_id=1, replica_groups=mesh['dp'=2,'row'=4,'col'=4] {'col'}, dimensions={0}, use_global_device_ids=true | all-gather | bytes 368640 | tf_op jit(solution)/shard_map/all_gather | solution.py:273
  80.3 21.3 %all_gather.21 = bf16[768,576]{1,0:T(8,128)(2,1)S(1)} all-gather(bf16[192,576]{1,0:T(8,128)(2,1)S(1)} %copy.205), channel_id=1, replica_groups=mesh['dp'=2,'row'=4,'col'=4] {'col'}, dimensions={0}, use_global_device_ids=true | all-gather | bytes 1105920 | tf_op jit(solution)/shard_map/all_gather | solution.py:273
  112.5 4.5 fusion.15
  131.0 4.8 collective-permute-start.19
  142.2 19.9 %collective-permute-done.19 = bf16[192,256]{0,1:T(8,128)(2,1)S(1)} collective-permute-done((bf16[192,256]{0,1:T(8,128)(2,1)}, bf16[192,256]{0,1:T(8,128)(2,1)S(1)}, u32[]{:S(2)}, u32[]{:S(2)}) %collective-permute-start.19) | collective-permute-done | bytes 98336 | tf_op jit(solution)/shard_map/ppermute | solution.py:85
  168.3 7.8 %collective-permute-done.8 = bf16[256,768]{1,0:T(8,128)(2,1)S(1)} collective-permute-done((bf16[256,768]{1,0:T(8,128)(2,1)S(1)}, bf16[256,768]{1,0:T(8,128)(2,1)S(1)}, u32[]{:S(2)}, u32[]{:S(2)}) %collective-permute-start.8) | collective-permute-done | bytes 393248 | tf_op jit(solution)/shard_map/ppermute | solution.py:18
  177.1 11.5 %collective-permute-done.20 = bf16[256,768]{1,0:T(8,128)(2,1)S(1)} collective-permute-done((bf16[256,768]{1,0:T(8,128)(2,1)S(1)}, bf16[256,768]{1,0:T(8,128)(2,1)S(1)}, u32[]{:S(2)}, u32[]{:S(2)}) %collective-permute-start.20) | collective-permute-done | bytes 393248 | tf_op jit(solution)/shard_map/ppermute | solution.py:18
  189.8 4.8 fusion.61
  194.6 4.5 convolution_convert_fusion.2
  200.6 4.2 fusion.108
  223.3 7.9 %collective-permute-done.23 = bf16[256,768]{1,0:T(8,128)(2,1)} collective-permute-done((bf16[256,768]{1,0:T(8,128)(2,1)}, bf16[256,768]{1,0:T(8,128)(2,1)}, u32[]{:S(2)}, u32[]{:S(2)}) %collective-permute-start.23) | collective-permute-done | bytes 393248 | tf_op jit(solution)/shard_map/ppermute | solution.py:18
  238.2 10.3 %collective-permute-done.24 = bf16[256,768]{1,0:T(8,128)(2,1)S(1)} collective-permute-done((bf16[256,768]{1,0:T(8,128)(2,1)S(1)}, bf16[256,768]{1,0:T(8,128)(2,1)S(1)}, u32[]{:S(2)}, u32[]{:S(2)}) %collective-permute-start.24) | collective-permute-done | bytes 393248 | tf_op jit(solution)/shard_map/ppermute | solution.py:18
  249.6 4.4 all-gather.3
  254.1 4.3 all-gather.2
  260.4 17.2 %psum.30 = bf16[768]{0:T(1024)(128)(2,1)S(1)} all-reduce(bf16[768]{0:T(1024)(128)(2,1)S(1)} %get-tuple-element.190), channel_id=1, replica_groups=mesh['dp'=2,'row'=4,'col'=4] {'dp','col'}, use_global_device_ids=true, to_apply=%region_24.25 | all-reduce | flops 768 | bytes 3072 | tf_op jit(solution)/shard_map/psum | solution.py:370
  278.3 4.4 convolution_convert_fusion.5
  284.7 41.6 %psum.31 = f32[4]{0:T(128)S(1)} all-reduce(f32[4]{0:T(128)S(1)} %pad_maximum_fusion.23), channel_id=1, replica_groups=mesh['dp'=2,'row'=4,'col'=4] {'dp','row','col'}, use_global_device_ids=true, to_apply=%region_30.31 | all-reduce | flops 4 | bytes 32 | tf_op jit(solution)/shard_map/psum | solution.py:414
  329.2 10.4 %multiply_reduce_fusion = (f32[3,1024]{1,0:T(4,128)S(1)}, f32[3,1024,1024]{1,2,0:T(8,128)}) fusion(f32[3,1024]{1,0:T(4,128)S(1)} %get-tuple-element.130, f32[3,1024,1024]{1,2,0:T(8,128)} %copy-done.1, pred[1024,1024]{0,1:T(8,128)(4,1)S(1)} %compare_and_fusion, bf16[1024,3,64]{0,2,1:T(8,128)(2,1)S(1)} %bitcast.328, f32[1024,3,3,64]{0,3,2,1:T(8,128)} %bitcast.293), kind=kOutput, calls=%fused_computation.6 | convolution fusion | flops 421524480 | bytes 27025408 | tf_op jit(solution)/shard_map/qhd,khd->hqk/dot_general | solution.py:187
  339.6 5.0 fusion.16
  344.6 7.2 %multiply_convert_fusion = bf16[3,1024,1024]{1,2,0:T(8,128)(2,1)S(1)} fusion(f32[3,1024,1024]{1,2,0:T(8,128)} %get-tuple-element.188, f32[3,1024]{1,0:T(4,128)S(1)} %get-tuple-element.187, f32[3,1024]{1,0:T(4,128)S(1)} %get-tuple-element.130, f32[3,1024,1024]{1,2,0:T(8,128)S(1)} %bitcast.288, pred[1024,1024]{0,1:T(8,128)(4,1)S(1)} %compare_and_fusion), kind=kLoop, calls=%fused_computation.5 | loop fusion | flops 22020096 | bytes 32530432 | tf_op jit(solution)/shard_map/convert_element_type | solution.py:192
  361.7 8.8 %collective-permute-start.13 = (bf16[192,256]{0,1:T(8,128)(2,1)S(1)}, bf16[192,256]{0,1:T(8,128)(2,1)S(1)}, u32[]{:S(2)}, u32[]{:S(2)}) collective-permute-start(bf16[192,256]{0,1:T(8,128)(2,1)S(1)} %get-tuple-element.168), channel_id=1, source_target_pairs={{4,0},{8,1},{12,2},{0,3},{6,4},{10,5},{14,6},{2,7},{5,8},{9,9},{13... | collective-permute-start | bytes 294920 | tf_op jit(solution)/shard_map/ppermute | solution.py:104
  380.8 5.0 dynamic_update_slice.55
  404.8 6.1 %copy.222 = f32[256,6,768]{0,2,1:T(8,128)} copy(f32[256,6,768]{2,0,1:T(8,128)} %bitcast_dynamic-update-slice_fusion) | data formatting | bytes 9437184 | tf_op jit(solution)/shard_map/stack | solution.py:372
  410.9 4.6 fusion.77
  438.1 5.1 collective-permute-start.31
  443.2 11.7 %all-reduce.2.cloned.1.call-done = f32[4,45,1,192]{3,0,1,2:T(4,128)} async-done(((f32[4,45,1,192]{3,0,1,2:T(4,128)}), f32[4,45,1,192]{3,0,1,2:T(4,128)}) %all-reduce.2.cloned.1.call-update) | async-done | bytes 138256 | tf_op jit(solution)/shard_map/psum | solution.py:393
  461.8 8.8 %all-to-all-done.1 = f32[4,45,1,192]{3,2,1,0:T(1,128)S(1)} async-done(((f32[4,45,1,192]{3,2,1,0:T(1,128)}), f32[4,45,1,192]{3,2,1,0:T(1,128)S(1)}, u32[]{:S(2)}, u32[]{:S(2)}) %all-to-all-start.1) | async-done | bytes 138272 | tf_op jit(solution)/shard_map/all_to_all | solution.py:394
  470.5 6.2 %all-gather.1 = f32[8,45,1,192]{3,2,1,0:T(1,128)S(1)} all-gather(f32[4,45,1,192]{3,2,1,0:T(1,128)S(1)} %all-to-all-done.1), channel_id=3, replica_groups=mesh['dp'=2,'row'=4,'col'=4] {'dp'}, dimensions={0}, use_global_device_ids=true | all-gather | bytes 414720 | tf_op jit(solution)/shard_map/all_gather | solution.py:397
  478.2 19.1 %psum.29 = f32[56,128]{1,0:T(8,128)S(1)} all-reduce(f32[56,128]{1,0:T(8,128)S(1)} %fusion.109), channel_id=1, replica_groups=mesh['dp'=2,'row'=4,'col'=4] {'col'}, use_global_device_ids=true, to_apply=%region_17.18 | all-reduce | flops 7168 | bytes 57344 | tf_op jit(solution)/shard_map/psum | solution.py:410
  (418 shorter events, 191.7 us)
Async XLA Ops:
  8.6 30.2 %collective-permute-start = (bf16[192,256]{0,1:T(8,128)(2,1)S(1)}, bf16[192,256]{0,1:T(8,128)(2,1)S(1)}, u32[]{:S(2)}, u32[]{:S(2)}) collective-permute-start(bf16[192,256]{0,1:T(8,128)(2,1)S(1)} %get-tuple-element.161), channel_id=1, source_target_pairs={{0,0},{1,4},{2,8},{3,12},{4,2},{5,6},{6,10},{7,14},{8,1},{9,5},{10... | collective-permute-start | bytes 294920 | tf_op jit(solution)/shard_map/ppermute | solution.py:85
  9.3 30.7 %collective-permute-start.1 = (bf16[192,256]{0,1:T(8,128)(2,1)S(1)}, bf16[192,256]{0,1:T(8,128)(2,1)S(1)}, u32[]{:S(2)}, u32[]{:S(2)}) collective-permute-start(bf16[192,256]{0,1:T(8,128)(2,1)S(1)} %get-tuple-element.160), channel_id=1, source_target_pairs={{0,4},{1,8},{2,12},{3,0},{4,6},{5,10},{6,14},{7,2},{8,5},{9,9},{10... | collective-permute-start | bytes 294920 | tf_op jit(solution)/shard_map/ppermute | solution.py:85
  16.6 24.5 %collective-permute-start.2 = (bf16[192,256]{0,1:T(8,128)(2,1)S(1)}, bf16[192,256]{0,1:T(8,128)(2,1)S(1)}, u32[]{:S(2)}, u32[]{:S(2)}) collective-permute-start(bf16[192,256]{0,1:T(8,128)(2,1)S(1)} %get-tuple-element.159), channel_id=1, source_target_pairs={{0,8},{1,12},{2,0},{3,4},{4,10},{5,14},{6,2},{7,6},{8,9},{9,13},{1... | collective-permute-start | bytes 294920 | tf_op jit(solution)/shard_map/ppermute | solution.py:85
  17.7 24.2 %collective-permute-start.3 = (bf16[192,256]{0,1:T(8,128)(2,1)S(1)}, bf16[192,256]{0,1:T(8,128)(2,1)S(1)}, u32[]{:S(2)}, u32[]{:S(2)}) collective-permute-start(bf16[192,256]{0,1:T(8,128)(2,1)S(1)} %get-tuple-element.158), channel_id=1, source_target_pairs={{0,12},{1,0},{2,4},{3,8},{4,14},{5,2},{6,6},{7,10},{8,13},{9,1},{1... | collective-permute-start | bytes 294920 | tf_op jit(solution)/shard_map/ppermute | solution.py:85
  29.8 14.0 %all-to-all-start = ((f32[4,45,192]{2,1,0:T(8,128)}), f32[4,45,192]{2,1,0:T(8,128)S(1)}, u32[]{:S(2)}, u32[]{:S(2)}) async-start(f32[4,45,192]{2,1,0:T(8,128)} %pad_maximum_fusion.21), calls=%async_computation | async-start | bytes 393216 | tf_op jit(solution)/shard_map/all_to_all | solution.py:263
  34.0 155.7 %all-gather.7.cloned.1.call-start = ((), (), s32[]{:S(2)}) async-start(), calls=%async_computation.6 | async-start | bytes 1474560 | tf_op jit(solution)/shard_map/all_gather | solution.py:273
  34.8 159.8 %all-gather.9.cloned.1.call-start = ((), (), s32[]{:S(2)}) async-start(), calls=%async_computation.7 | async-start | bytes 1474560 | tf_op jit(solution)/shard_map/all_gather | solution.py:273
  61.5 40.2 %collective-permute-start.5 = (bf16[512,768]{1,0:T(8,128)(2,1)}, bf16[512,768]{1,0:T(8,128)(2,1)}, u32[]{:S(2)}, u32[]{:S(2)}) collective-permute-start(bf16[512,768]{1,0:T(8,128)(2,1)} %pad_maximum_fusion.5), channel_id=1, source_target_pairs={{0,4},{4,0},{8,12},{12,8},{1,5},{5,1},{9,13},{13,9},{2,6},{6,2},{1... | collective-permute-start | bytes 2359304 | tf_op jit(solution)/shard_map/ppermute | solution.py:18
  121.8 42.6 %collective-permute-start.7 = (bf16[256,768]{1,0:T(8,128)(2,1)}, bf16[256,768]{1,0:T(8,128)(2,1)}, u32[]{:S(2)}, u32[]{:S(2)}) collective-permute-start(bf16[256,768]{1,0:T(8,128)(2,1)} %slice.212), channel_id=1, source_target_pairs={{0,8},{4,12},{8,0},{12,4},{1,9},{5,13},{9,1},{13,5},{2,10},{6,14},... | collective-permute-start | bytes 1179656 | tf_op jit(solution)/shard_map/ppermute | solution.py:18
  129.9 11.6 %collective-permute-start.18 = (bf16[192,256]{0,1:T(8,128)(2,1)}, bf16[192,256]{0,1:T(8,128)(2,1)S(1)}, u32[]{:S(2)}, u32[]{:S(2)}) collective-permute-start(bf16[192,256]{0,1:T(8,128)(2,1)} %get-tuple-element.155), channel_id=1, source_target_pairs={{0,8},{1,12},{2,0},{3,4},{4,10},{5,14},{6,2},{7,6},{8,9},{9,13},{1... | collective-permute-start | bytes 294920 | tf_op jit(solution)/shard_map/ppermute | solution.py:85
  131.0 31.0 %collective-permute-start.19 = (bf16[192,256]{0,1:T(8,128)(2,1)}, bf16[192,256]{0,1:T(8,128)(2,1)S(1)}, u32[]{:S(2)}, u32[]{:S(2)}) collective-permute-start(bf16[192,256]{0,1:T(8,128)(2,1)} %get-tuple-element.154), channel_id=1, source_target_pairs={{0,12},{1,0},{2,4},{3,8},{4,14},{5,2},{6,6},{7,10},{8,13},{9,1},{1... | collective-permute-start | bytes 294920 | tf_op jit(solution)/shard_map/ppermute | solution.py:85
  135.9 254.7 %reduce-scatter.11.cloned.1.call-start = ((), (), s32[]{:S(2)}) async-start(), calls=%async_computation.12 | async-start | bytes 1474560 | tf_op jit(solution)/shard_map/reduce_scatter | solution.py:355
  177.1 12.6 %collective-permute-start.9 = (bf16[512,768]{1,0:T(8,128)(2,1)}, bf16[512,768]{1,0:T(8,128)(2,1)}, u32[]{:S(2)}, u32[]{:S(2)}) collective-permute-start(bf16[512,768]{1,0:T(8,128)(2,1)} %pad_maximum_fusion.6), channel_id=1, source_target_pairs={{0,4},{4,0},{8,12},{12,8},{1,5},{5,1},{9,13},{13,9},{2,6},{6,2},{1... | collective-permute-start | bytes 2359304 | tf_op jit(solution)/shard_map/ppermute | solution.py:18
  177.1 11.5 %collective-permute-start.20 = (bf16[256,768]{1,0:T(8,128)(2,1)S(1)}, bf16[256,768]{1,0:T(8,128)(2,1)S(1)}, u32[]{:S(2)}, u32[]{:S(2)}) collective-permute-start(bf16[256,768]{1,0:T(8,128)(2,1)S(1)} %get-tuple-element.128), channel_id=1, source_target_pairs={{0,8},{4,12},{8,0},{12,4},{1,9},{5,13},{9,1},{13,5},{2,10},{6,14},... | collective-permute-start | bytes 1179656 | tf_op jit(solution)/shard_map/ppermute | solution.py:18
  211.0 12.3 %collective-permute-start.11 = (bf16[256,768]{1,0:T(8,128)(2,1)}, bf16[256,768]{1,0:T(8,128)(2,1)}, u32[]{:S(2)}, u32[]{:S(2)}) collective-permute-start(bf16[256,768]{1,0:T(8,128)(2,1)} %slice.220), channel_id=1, source_target_pairs={{0,8},{4,12},{8,0},{12,4},{1,9},{5,13},{9,1},{13,5},{2,10},{6,14},... | collective-permute-start | bytes 1179656 | tf_op jit(solution)/shard_map/ppermute | solution.py:18
  214.3 16.8 %collective-permute-start.23 = (bf16[256,768]{1,0:T(8,128)(2,1)}, bf16[256,768]{1,0:T(8,128)(2,1)}, u32[]{:S(2)}, u32[]{:S(2)}) collective-permute-start(bf16[256,768]{1,0:T(8,128)(2,1)} %slice.225), channel_id=1, source_target_pairs={{0,8},{4,12},{8,0},{12,4},{1,9},{5,13},{9,1},{13,5},{2,10},{6,14},... | collective-permute-start | bytes 1179656 | tf_op jit(solution)/shard_map/ppermute | solution.py:18
  219.9 173.1 %reduce-scatter.9.cloned.1.call-start = ((), (), s32[]{:S(2)}) async-start(), calls=%async_computation.11 | async-start | bytes 1474560 | tf_op jit(solution)/shard_map/reduce_scatter | solution.py:355
  249.5 77.3 %collective-permute-start.25 = (bf16[512,768]{1,0:T(8,128)(2,1)}, bf16[512,768]{1,0:T(8,128)(2,1)}, u32[]{:S(2)}, u32[]{:S(2)}) collective-permute-start(bf16[512,768]{1,0:T(8,128)(2,1)} %pad_maximum_fusion.8), channel_id=1, source_target_pairs={{0,4},{4,0},{8,12},{12,8},{1,5},{5,1},{9,13},{13,9},{2,6},{6,2},{1... | collective-permute-start | bytes 2359304 | tf_op jit(solution)/shard_map/ppermute | solution.py:18
  284.7 143.0 %reduce-scatter.7.cloned.1.call-start = ((), (), s32[]{:S(2)}) async-start(), calls=%async_computation.10 | async-start | bytes 491520 | tf_op jit(solution)/shard_map/reduce_scatter | solution.py:355
  358.9 16.1 %collective-permute-start.26 = (bf16[512,768]{1,0:T(8,128)(2,1)S(1)}, bf16[512,768]{1,0:T(8,128)(2,1)S(1)}, u32[]{:S(2)}, u32[]{:S(2)}) collective-permute-start(bf16[512,768]{1,0:T(8,128)(2,1)S(1)} %slice.231), channel_id=1, source_target_pairs={{0,4},{4,0},{8,12},{12,8},{1,5},{5,1},{9,13},{13,9},{2,6},{6,2},{1... | collective-permute-start | bytes 2359304 | tf_op jit(solution)/shard_map/ppermute | solution.py:18
  359.9 12.8 %collective-permute-start.12 = (bf16[192,256]{0,1:T(8,128)(2,1)S(1)}, bf16[192,256]{0,1:T(8,128)(2,1)S(1)}, u32[]{:S(2)}, u32[]{:S(2)}) collective-permute-start(bf16[192,256]{0,1:T(8,128)(2,1)S(1)} %get-tuple-element.169), channel_id=1, source_target_pairs={{0,0},{4,1},{8,2},{12,3},{2,4},{6,5},{10,6},{14,7},{1,8},{5,9},{9,... | collective-permute-start | bytes 294920 | tf_op jit(solution)/shard_map/ppermute | solution.py:104
  361.7 12.6 %collective-permute-start.13 = (bf16[192,256]{0,1:T(8,128)(2,1)S(1)}, bf16[192,256]{0,1:T(8,128)(2,1)S(1)}, u32[]{:S(2)}, u32[]{:S(2)}) collective-permute-start(bf16[192,256]{0,1:T(8,128)(2,1)S(1)} %get-tuple-element.168), channel_id=1, source_target_pairs={{4,0},{8,1},{12,2},{0,3},{6,4},{10,5},{14,6},{2,7},{5,8},{9,9},{13... | collective-permute-start | bytes 294920 | tf_op jit(solution)/shard_map/ppermute | solution.py:104
  376.1 17.1 %collective-permute-start.27 = (bf16[256,768]{1,0:T(8,128)(2,1)}, bf16[256,768]{1,0:T(8,128)(2,1)}, u32[]{:S(2)}, u32[]{:S(2)}) collective-permute-start(bf16[256,768]{1,0:T(8,128)(2,1)} %slice.233), channel_id=1, source_target_pairs={{0,8},{4,12},{8,0},{12,4},{1,9},{5,13},{9,1},{13,5},{2,10},{6,14},... | collective-permute-start | bytes 1179656 | tf_op jit(solution)/shard_map/ppermute | solution.py:18
  390.5 64.4 %all-reduce.2.cloned.1.call-start = ((), (), s32[]{:S(2)}) async-start(), calls=%async_computation.8 | async-start | bytes 368640 | tf_op jit(solution)/shard_map/psum | solution.py:393
  390.6 33.4 %collective-permute-start.35 = (bf16[192,768]{1,0:T(8,128)(2,1)}, bf16[192,768]{1,0:T(8,128)(2,1)}, u32[]{:S(2)}, u32[]{:S(2)}) collective-permute-start(bf16[192,768]{1,0:T(8,128)(2,1)} %reduce-scatter.11.cloned.1.call-done), channel_id=1, source_target_pairs={{0,16},{16,0},{1,17},{17,1},{2,18},{18,2},{3,19},{19,3},{4,20},{20... | collective-permute-start | bytes 884744 | tf_op jit(solution)/shard_map/ppermute | solution.py:18
  393.0 32.8 %collective-permute-start.34 = (bf16[192,768]{1,0:T(8,128)(2,1)}, bf16[192,768]{1,0:T(8,128)(2,1)}, u32[]{:S(2)}, u32[]{:S(2)}) collective-permute-start(bf16[192,768]{1,0:T(8,128)(2,1)} %reduce-scatter.9.cloned.1.call-done), channel_id=1, source_target_pairs={{0,16},{16,0},{1,17},{17,1},{2,18},{18,2},{3,19},{19,3},{4,20},{20... | collective-permute-start | bytes 884744 | tf_op jit(solution)/shard_map/ppermute | solution.py:18
  419.7 80.5 %reduce-scatter.5.cloned.1.call-start = ((), (), s32[]{:S(2)}) async-start(), calls=%async_computation.9 | async-start | bytes 1228800 | tf_op jit(solution)/shard_map/reduce_scatter | solution.py:355
  430.1 30.6 %collective-permute-start.28 = (bf16[192,256]{0,1:T(8,128)(2,1)S(1)}, bf16[192,256]{0,1:T(8,128)(2,1)S(1)}, u32[]{:S(2)}, u32[]{:S(2)}) collective-permute-start(bf16[192,256]{0,1:T(8,128)(2,1)S(1)} %get-tuple-element.165), channel_id=1, source_target_pairs={{0,0},{4,1},{8,2},{12,3},{2,4},{6,5},{10,6},{14,7},{1,8},{5,9},{9,... | collective-permute-start | bytes 294920 | tf_op jit(solution)/shard_map/ppermute | solution.py:104
  433.7 27.0 %collective-permute-start.29 = (bf16[192,256]{0,1:T(8,128)(2,1)S(1)}, bf16[192,256]{0,1:T(8,128)(2,1)S(1)}, u32[]{:S(2)}, u32[]{:S(2)}) collective-permute-start(bf16[192,256]{0,1:T(8,128)(2,1)S(1)} %get-tuple-element.164), channel_id=1, source_target_pairs={{4,0},{8,1},{12,2},{0,3},{6,4},{10,5},{14,6},{2,7},{5,8},{9,9},{13... | collective-permute-start | bytes 294920 | tf_op jit(solution)/shard_map/ppermute | solution.py:104
  437.1 23.7 %collective-permute-start.30 = (bf16[192,256]{0,1:T(8,128)(2,1)S(1)}, bf16[192,256]{0,1:T(8,128)(2,1)S(1)}, u32[]{:S(2)}, u32[]{:S(2)}) collective-permute-start(bf16[192,256]{0,1:T(8,128)(2,1)S(1)} %get-tuple-element.163), channel_id=1, source_target_pairs={{8,0},{12,1},{0,2},{4,3},{10,4},{14,5},{2,6},{6,7},{9,8},{13,9},{1... | collective-permute-start | bytes 294920 | tf_op jit(solution)/shard_map/ppermute | solution.py:104
  438.1 22.7 %collective-permute-start.31 = (bf16[192,256]{0,1:T(8,128)(2,1)S(1)}, bf16[192,256]{0,1:T(8,128)(2,1)S(1)}, u32[]{:S(2)}, u32[]{:S(2)}) collective-permute-start(bf16[192,256]{0,1:T(8,128)(2,1)S(1)} %get-tuple-element.162), channel_id=1, source_target_pairs={{12,0},{0,1},{4,2},{8,3},{14,4},{2,5},{6,6},{10,7},{13,8},{1,9},{5... | collective-permute-start | bytes 294920 | tf_op jit(solution)/shard_map/ppermute | solution.py:104
  456.7 13.8 %all-to-all-start.1 = ((f32[4,45,1,192]{3,2,1,0:T(1,128)}), f32[4,45,1,192]{3,2,1,0:T(1,128)S(1)}, u32[]{:S(2)}, u32[]{:S(2)}) async-start(f32[4,45,1,192]{3,2,1,0:T(1,128)} %copy.223), calls=%async_computation.1 | async-start | bytes 368640 | tf_op jit(solution)/shard_map/all_to_all | solution.py:394
  (93 other events, 806.5 us)
Sparse Core Ops, SparseCore 0:
  36.4 30.5 all-gather.6
  136.0 30.6 all-gather.8
  220.0 26.5 reduce-scatter.10
  284.8 28.6 reduce-scatter.8
  390.6 22.9 reduce-scatter.6
  419.8 35.0 all-reduce.1
  457.2 27.2 reduce-scatter.4

commit v2 on v1

v2 whole, which is shorter than its diff:
```python
import functools

import jax
import jax.numpy as jnp
from jax import lax
from jax.experimental import pallas as pl
from jax.experimental.pallas import tpu as pltpu
from jax.sharding import PartitionSpec as P

HEAD_DIM = 64
SEQ = 1024

PRECISE = lax.Precision.HIGHEST
EPSILON = 1e-05
MASK_FILL = -1e30
MASK_FLOOR = -1e29
LOW = jnp.bfloat16
FULL = jnp.float32
SLOTS = 8
LANES = 64
GAIN_ONE, GAIN_TWO, DOWN_BIAS = 48, 49, 50
STATS = 51
VMEM_SMALL = 12 * 1024 * 1024
VMEM_LARGE = 56 * 1024 * 1024
VMEM_LIMIT = {
    name: VMEM_LARGE
    for name in ("attend", "feed_first", "feed_grads", "feed_out", "attend_back", "attend_weights")
}


def swap(values, axis, bit):
    count = lax.axis_size(axis)
    return lax.ppermute(values, axis, [(i, i ^ bit) for i in range(count)])


def gather_rows(values, filler=None, deps=()):
    far = swap(values, "row", 2)
    near = swap(values, "row", 1)
    filled = None
    if filler is not None:
        filled = filler(near)
        deps = list(deps) + list(filled[:1])
    if deps:
        [far] = after(deps, [far])
    last = swap(far, "row", 1)
    pieces = [values, near, far, last]
    return pieces if filler is None else (pieces, after([last], filled))


def scatter_rows(parts, filler=None, hold=False):
    width = parts[0].shape[0]
    near = swap(parts[2], "row", 1)
    total = (parts[1].astype(FULL) + near[width:].astype(FULL)).astype(LOW)
    far = swap(total, "row", 2)
    if filler is None:
        return [parts[0], near, far]
    filled = filler(total)
    [far] = after(filled[:1], [far])
    return [parts[0], near, far], after([far], filled) if hold else filled


def col_of_row(row_count):
    if row_count == 4:
        return [0, 2, 1, 3]
    return list(range(row_count))


def relayout_pairs(step):
    row_count = lax.axis_size("row")
    col_count = lax.axis_size("col")
    per_row = col_count // row_count
    table = col_of_row(row_count)
    pairs = []
    for r in range(row_count):
        for c in range(col_count):
            j, q = divmod((c + step) % col_count, row_count)
            pairs.append((r * col_count + c, q * col_count + table[r] * per_row + j))
    return pairs


def relayout(pieces, back=False):
    got = []
    for step, piece in enumerate(pieces):
        pairs = relayout_pairs(step)
        if back:
            pairs = [(b, a) for a, b in pairs]
        got.append(lax.ppermute(piece, ("row", "col"), pairs))
    return got


def after(deps, values):
    return lax.optimization_barrier((list(values), list(deps)))[0]


class Grid:
    def __init__(self):
        self.rows = lax.axis_size("row")
        self.cols = lax.axis_size("col")
        self.per_row = self.cols // self.rows
        table = col_of_row(self.rows)
        self.seq_of_col = [0] * self.cols
        for r in range(self.rows):
            for j in range(self.per_row):
                self.seq_of_col[table[r] * self.per_row + j] = r * self.per_row + j

    def row(self):
        return lax.axis_index("row")

    def col(self):
        return lax.axis_index("col")

    def sequence(self):
        return sum(jnp.where(self.col() == c, s, 0) for c, s in enumerate(self.seq_of_col))

    def half(self):
        return lax.axis_index("dp") % 2

    def half_start(self, block, which, size):
        return pl.multiple_of((2 * block + which) * size, size)

    def source(self, step):
        mine = self.col() % self.per_row * self.rows + self.row()
        return (mine + self.cols - step) % self.cols

    def place(self, step):
        return (self.col() + step) % self.cols


def whole(memory_space=pltpu.VMEM):
    return pl.BlockSpec(memory_space=memory_space)


class Far:
    def __init__(self, value):
        self.value = value


class FarIn:
    def __init__(self, source, buffer, sem):
        self.copy = pltpu.make_async_copy(source, buffer, sem)
        self.buffer, self.waiting = buffer, True
        self.copy.start()

    @property
    def shape(self):
        return self.buffer.shape

    @property
    def ref(self):
        if self.waiting:
            self.copy.wait()
            self.waiting = False
        return self.buffer

    @property
    def at(self):
        return self.ref.at

    def __getitem__(self, index):
        return self.ref[index]


class FarOut:
    def __init__(self, buffer, target, sem):
        self.copy = pltpu.make_async_copy(buffer, target, sem)
        self.ref, self.shipped = buffer, False

    @property
    def shape(self):
        return self.ref.shape

    @property
    def at(self):
        return self.ref.at

    def __getitem__(self, index):
        return self.ref[index]

    def __setitem__(self, index, value):
        self.ref[index] = value

    def ship(self):
        if not self.shipped:
            self.copy.start()
            self.shipped = True


def ship(*refs):
    for ref in refs:
        if isinstance(ref, FarOut):
            ref.ship()


def run(body, name, outs, args, scratch=(), smem=0, flops=0):
    far_args = [isinstance(a, Far) for a in args]
    far_outs = [isinstance(o, Far) for o in outs]
    args = [a.value if isinstance(a, Far) else a for a in args]
    outs = [o.value if isinstance(o, Far) else o for o in outs]
    buffers = [pltpu.VMEM(a.shape, a.dtype) for a, far in zip(args + outs, far_args + far_outs) if far]
    moved = sum(a.size * a.dtype.itemsize for a in args + outs)

    def kernel(*refs):
        ins, rest = list(refs[: len(args)]), refs[len(args) :]
        results, rest = list(rest[: len(outs)]), rest[len(outs) :]
        own, rest = rest[: len(scratch)], list(rest[len(scratch) :])
        count = 0
        for i, far in enumerate(far_args):
            if far:
                ins[i] = FarIn(ins[i], rest[count], rest[-1].at[count])
                count += 1
        for i, far in enumerate(far_outs):
            if far:
                results[i] = FarOut(rest[count], results[i], rest[-1].at[count])
                count += 1
        body(*ins, *results, *own)
        for ref in results:
            ship(ref)
        for ref in ins:
            if isinstance(ref, FarIn):
                ref.ref
        for ref in results:
            if isinstance(ref, FarOut):
                ref.copy.wait()

    def spec(far):
        return whole(pl.ANY) if far else whole()

    found = pl.pallas_call(
        kernel if buffers else body,
        out_shape=outs,
        in_specs=[whole(pltpu.SMEM)] * smem + [spec(far) for far in far_args[smem:]],
        out_specs=[spec(far) for far in far_outs],
        scratch_shapes=list(scratch) + buffers
        + ([pltpu.SemaphoreType.DMA((len(buffers),))] if buffers else []),
        compiler_params=pltpu.CompilerParams(vmem_limit_bytes=VMEM_LIMIT.get(name, VMEM_SMALL)),
        cost_estimate=pl.CostEstimate(flops=flops, bytes_accessed=moved, transcendentals=0),
        name=name,
    )(*args)
    return list(found)


def far_all(values):
    return [Far(v) for v in values]


def shape(dims, dtype):
    return jax.ShapeDtypeStruct(dims, dtype)


def dot(left, right, dims, precision=None):
    return lax.dot_general(
        left, right, (((dims[0],), (dims[1],)), ((), ())),
        preferred_element_type=FULL, precision=precision,
    )


def split(values, terms):
    found = []
    for _ in range(terms):
        term = values.astype(LOW).astype(FULL)
        found.append(term)
        values = values - term
    return found


def block_start(index, size):
    return pl.multiple_of(index * size, size)


def token_mods_of(mods, segs):
    terms = jnp.concatenate(split(mods, 2), 1).astype(LOW)
    rows = lax.broadcasted_iota(jnp.int32, (2 * LANES, segs.shape[1]), 0) % LANES

    def pick(k):
        chosen = (rows == segs + k * SLOTS).astype(LOW)
        return dot(terms, chosen, (1, 0))

    return pick


def part_of(parts, e):
    if e % 2 == 0:
        return parts[e // 2]
    width = parts[0].shape[0]
    return parts[2].at[(e // 2) * width : (e // 2 + 1) * width]


def ship_part(parts, e):
    if e != 3:
        ship({1: parts[2], 2: parts[1], 0: parts[0]}[e])


def three_terms(part, near, far):
    return (
        part[...].astype(FULL) + near[: part.shape[0], :].astype(FULL) + far[...].astype(FULL)
    )


def normalize(stream):
    count = 1.0 / stream.shape[0]
    center = jnp.sum(stream, axis=0, keepdims=True) * count
    offset = stream - center
    inverse = lax.rsqrt(jnp.sum(offset * offset, axis=0, keepdims=True) * count + EPSILON)
    return offset * inverse, inverse


def normalize_back(grad_normed, normed, inverse):
    count = 1.0 / normed.shape[0]
    center = jnp.sum(grad_normed, axis=0, keepdims=True) * count
    along = jnp.sum(grad_normed * normed, axis=0, keepdims=True) * count
    return inverse * (grad_normed - center - normed * along)


def prepare(grid, slot_count, times, table, weight, bias, gain_one, gain_two, down_bias, tokens, cot, *rest):
    outs, (embed, rows, blocks) = rest[: grid.cols], rest[grid.cols :]
    own = (outs[0].shape[1] - 2 * LANES) // 2
    rows[...] = jnp.zeros_like(rows)
    for k in range(6):
        rows[k * SLOTS : (k + 1) * SLOTS, :] = jnp.broadcast_to(
            bias[k : k + 1, :].astype(FULL), (SLOTS, rows.shape[1])
        )
    rows[GAIN_ONE : GAIN_ONE + 1, :] = gain_one[...].astype(FULL)[None]
    rows[GAIN_TWO : GAIN_TWO + 1, :] = gain_two[...].astype(FULL)[None]
    rows[DOWN_BIAS : DOWN_BIAS + 1, :] = down_bias[...].astype(FULL)[None]
    fixed = rows[...].T
    cond = weight.shape[2]
    flat = jnp.concatenate([weight[k] for k in range(6)], 1)
    row = lax.broadcasted_iota(jnp.int32, (LANES, 6 * cond), 0)
    lane = lax.broadcasted_iota(jnp.int32, (LANES, 6 * cond), 1)
    match = row // SLOTS == lane // cond
    for j in range(grid.per_row):
        embed[...] = jnp.zeros_like(embed)
        for slot in range(slot_count):
            time = times[grid.row() * grid.per_row + j, slot]
            embed[slot : slot + 1, :] = table[pl.ds(time, 1), :]
        tiled = jnp.concatenate([embed[...]] * (LANES // SLOTS), 0)
        tiled = jnp.concatenate([tiled] * 6, 1)
        total = fixed
        for term in split(jnp.where(match, tiled, 0.0), 3):
            total = total + dot(flat, term.astype(LOW), (1, 1))
        blocks[j] = jnp.concatenate(split(total, 2), 1).astype(LOW)
    for step in range(grid.cols):
        place = grid.place(step)
        outs[step][:, :own] = tokens[:, pl.ds(block_start(place, own), own)]
        outs[step][:, own : 2 * own] = cot[:, pl.ds(block_start(place, own), own)]
        outs[step][:, 2 * own :] = blocks[place // grid.rows]


def unbundle(grid, *rest):
    bundles, (grad_out, result_out, small_out) = rest[: grid.cols], rest[grid.cols :]
    size = grad_out.shape[0]
    own = grad_out.shape[1] // grid.cols
    small_out[...] = jnp.zeros_like(small_out)
    for step in range(grid.cols):
        place = grid.place(step)
        span = pl.ds(block_start(place, own), own)
        grad_out[:, span] = bundles[step][:size, :own]
        result_out[:, span] = bundles[step][:size, own : 2 * own]
        terms = bundles[step][:, 2 * own :].astype(FULL)
        small_out[place // grid.rows] += (terms[:, :LANES] + terms[:, LANES:]).T


def pack(qkv, proj, attn_out):
    width = qkv.shape[2]
    for i in range(3):
        attn_out[:, i * width : (i + 1) * width] = qkv[i]
    attn_out[:, 3 * width :] = proj[...].T


def places(grid, slot_count, segs, segs_row, segs_col, segs_own, cosine, sine):
    own = segs_own.shape[1]
    base = grid.sequence() * grid.rows
    lane = lax.broadcasted_iota(jnp.int32, (1, own), 1)

    def segs_of(q):
        return segs[pl.ds(base + q, 1), :]

    starts = []
    for slot in range(slot_count):
        start = jnp.full((1, 1), SEQ, jnp.int32)
        for q in range(grid.rows):
            there = jnp.where(segs_of(q) == slot, lane + q * own, SEQ)
            start = jnp.minimum(start, jnp.min(there, axis=1, keepdims=True))
        starts.append(start)
    half = cosine.shape[0]
    step = lax.broadcasted_iota(jnp.int32, (half, own), 0).astype(FULL)
    inverse_freq = 1.0 / jnp.exp(step * (2.0 / HEAD_DIM) * jnp.log(FULL(10000.0)))
    for e in range(grid.rows):
        q = grid.row() ^ e
        span = slice(e * own, (e + 1) * own)
        row = segs_of(q)
        position = lane + q * own
        for slot in range(slot_count):
            position = position - jnp.where(row == slot, starts[slot], 0)
        angle = position.astype(FULL) * inverse_freq
        cosine[:, span] = jnp.cos(angle)
        sine[:, span] = jnp.sin(angle)
        segs_row[:, span] = row
        segs_col[span, :] = jnp.broadcast_to(row.astype(FULL), (8, own)).T[:, :1].astype(jnp.int32)
    segs_own[...] = segs_row[:, :own]


def first_norm(grid, segs, *rest):
    bundles, (input_out, stream_out, cot_out, mods_out) = rest[: grid.cols], rest[grid.cols :]
    size, own = bundles[0].shape[0], input_out.shape[1]
    for step in range(grid.cols):
        place = pl.ds(block_start(grid.source(step), size), size)
        stream_out[place, :] = bundles[step][:, :own]
        cot_out[place, :] = bundles[step][:, own : 2 * own]
        terms = bundles[step][:, 2 * own :].astype(FULL)
        mods_out[place, :] = terms[:, :LANES] + terms[:, LANES:]
    stream = stream_out[...].astype(FULL)
    mods = mods_out[...]
    pick = token_mods_of(mods, segs[...])
    normed, _ = normalize(stream)
    scaled = normed * mods[:, GAIN_ONE : GAIN_ONE + 1]
    input_out[...] = (scaled * (1.0 + pick(1)) + pick(0)).astype(LOW)


def branch_grad(segs, mods, cot, branch_out):
    pick = token_mods_of(mods[...], segs[...])
    branch_out[...] = (cot[...].astype(FULL) * pick(5)).astype(LOW)


def attend(segs_row, segs_col, cosine, sine, weight_all, *rest):
    pieces, outs = rest[:4], rest[4:]
    parts, (query, key, value, mixed, logsum, inputs_all, key_rows) = outs[:3], outs[3:]
    own = pieces[0].shape[1]
    head_width = query.shape[0]
    weight, proj = weight_all[:, : 3 * head_width], weight_all[:, 3 * head_width :]
    half = HEAD_DIM // 2
    scale = HEAD_DIM ** (-0.5)
    for e in range(4):
        span = slice(e * own, (e + 1) * own)
        cos, sin = cosine[:, span], sine[:, span]
        inputs_all[:, span] = pieces[e][...]
        found = dot(weight, inputs_all[:, span], (0, 0))
        for h in range(head_width // HEAD_DIM):
            for out, base, factor in ((query, 0, scale), (key, head_width, 1.0)):
                at = h * HEAD_DIM
                one = found[base + at : base + at + half]
                two = found[base + at + half : base + at + HEAD_DIM]
                out[at : at + half, span] = ((one * cos - two * sin) * factor).astype(LOW)
                out[at + half : at + HEAD_DIM, span] = ((two * cos + one * sin) * factor).astype(LOW)
        value[:, span] = found[2 * head_width :].astype(LOW)
    ship(query, key, value, inputs_all)
    key_segs = jnp.where(segs_col[...] == 0, -1, segs_col[...])
    for h in range(head_width // HEAD_DIM):
        rows = slice(h * HEAD_DIM, (h + 1) * HEAD_DIM)
        key_rows[h] = key[rows, :].astype(FULL).T.astype(LOW)
    for e in (3, 1, 2, 0):
        span = slice(e * own, (e + 1) * own)
        query_segs = segs_row[:, span]
        allowed = key_segs == query_segs
        padding = (query_segs == 0).astype(FULL)
        for h in range(head_width // HEAD_DIM):
            rows = slice(h * HEAD_DIM, (h + 1) * HEAD_DIM)
            scores = dot(key_rows[h], query[rows, span], (1, 0))
            scores = jnp.where(allowed, scores, MASK_FILL)
            largest = jnp.maximum(jnp.max(scores, axis=0, keepdims=True), MASK_FLOOR)
            exponent = jnp.exp(scores - largest)
            total = jnp.sum(exponent, axis=0, keepdims=True) + padding
            found = dot(value[rows, :], exponent.astype(LOW), (1, 0))
            mixed[rows, span] = (found / total).astype(LOW)
            logsum[h : h + 1, span] = largest + jnp.log(total)
        part_of(parts, e)[...] = dot(proj, mixed[:, span], (1, 0)).astype(LOW)
        ship_part(parts, e)


def second_norm(segs, mods, stream, part, near, far, input_out, middle_out, attn_out):
    pick = token_mods_of(mods[...], segs[...])
    attn = three_terms(part, near, far)
    attn_out[...] = attn.astype(LOW)
    middle = stream[...].astype(FULL) + pick(2) * attn
    middle_out[...] = middle
    normed, _ = normalize(middle)
    scaled = normed * mods[:, GAIN_TWO : GAIN_TWO + 1]
    input_out[...] = (scaled * (1.0 + pick(4)) + pick(3)).astype(LOW)


GELU_SCALE = 0.7978845608028654
GELU_CUBE = 0.044715


def feed_first(weights, up_bias, *rest):
    pieces, branches, outs = rest[:4], rest[4:8], rest[8:]
    parts, (hidden, pre_grad, inputs_all, branch_all) = outs[:3], outs[3:]
    own = pieces[0].shape[1]
    count = hidden.shape[0]
    up, down = weights[:, :count], weights[:, count:]
    bias = jnp.broadcast_to(up_bias[...].astype(FULL)[None], (8, count)).T[:, :1]
    for e in (3, 1, 2, 0):
        span = slice(e * own, (e + 1) * own)
        inputs_all[:, span] = pieces[e][...]
        branch_all[:, span] = branches[e][...]
        pre = dot(up, pieces[e][...], (0, 0)) + bias
        square = pre * pre
        curve = jnp.tanh(GELU_SCALE * (pre + GELU_CUBE * square * pre))
        hidden[:, span] = (0.5 * pre * (1.0 + curve)).astype(LOW)
        slope = 0.5 * (1.0 + curve) + 0.5 * pre * (1.0 - curve * curve) * (
            GELU_SCALE * (1.0 + 3.0 * GELU_CUBE * square)
        )
        grad = dot(down, branches[e][...], (0, 0))
        pre_grad[:, span] = (grad * slope).astype(LOW)
        part_of(parts, e)[...] = dot(up, pre_grad[:, span], (1, 0)).astype(LOW)
        ship_part(parts, e)


def feed_grads_of(hidden, pre_grad, inputs_all, branch_all, grads):
    count = hidden.shape[0]
    blocks = grads.shape[0]
    size = inputs_all.shape[0] // blocks
    ones = jnp.ones((16, hidden.shape[1]), LOW)
    bias = dot(ones, pre_grad[...], (1, 1)).astype(LOW)
    for j in range(blocks):
        grads[j, size:, :count] = bias
        grads[j, size:, count:] = jnp.zeros_like(bias)
    up_total = dot(inputs_all[...], pre_grad[...], (1, 1)).astype(LOW)
    for j in range(blocks):
        grads[j, :size, :count] = up_total[j * size : (j + 1) * size]
    down_total = dot(branch_all[...], hidden[...], (1, 1)).astype(LOW)
    for j in range(blocks):
        grads[j, :size, count:] = down_total[j * size : (j + 1) * size]


def feed_out(weights, hidden, *parts):
    count = hidden.shape[0]
    own = parts[0].shape[1]
    for e in (3, 1, 2, 0):
        part_of(parts, e)[...] = dot(
            weights[:, count:], hidden[:, e * own : (e + 1) * own], (1, 0)
        ).astype(LOW)
        ship_part(parts, e)


def middle_grad(segs, mods, middle, cot, part, near, far, grad_out, attn_grad_out, input_grad_out):
    pick = token_mods_of(mods[...], segs[...])
    input_grad = three_terms(part, near, far)
    input_grad_out[...] = input_grad.astype(LOW)
    normed, inverse = normalize(middle[...])
    grad_scaled = input_grad * (1.0 + pick(4)) * mods[:, GAIN_TWO : GAIN_TWO + 1]
    grad = cot[...].astype(FULL) + normalize_back(grad_scaled, normed, inverse)
    grad_out[...] = grad
    attn_grad_out[...] = (grad * pick(2)).astype(LOW)


def doc_sums(values, chosen):
    terms = jnp.concatenate(split(values, 2), 1).astype(LOW)
    return dot(jnp.concatenate([chosen, chosen], 1), terms, (1, 1))


def slot_rows(segs):
    return (lax.broadcasted_iota(jnp.int32, (16, segs.shape[1]), 0) == segs).astype(LOW)


def finish_forward(segs, mods, middle, cot, attn, grad_middle, input_grad, part, near, far, result_out, small):
    pick = token_mods_of(mods[...], segs[...])
    chosen = slot_rows(segs[...])
    ones = jnp.ones(chosen.shape, LOW)
    valid = (segs[...] != 0).astype(FULL)
    mlp = (
        three_terms(part, near, far)
        + mods[:, DOWN_BIAS : DOWN_BIAS + 1]
    )
    gate = pick(5)
    mlp_term = gate * mlp
    result = middle[...] + mlp_term
    result_out[...] = result.astype(LOW)
    small[...] = jnp.zeros_like(small)
    cot_full = cot[...].astype(FULL)
    attn_all = attn[...].astype(FULL)
    input_all = input_grad[...].astype(FULL)
    normed, _ = normalize(middle[...])
    along = input_all * normed
    terms = (
        (2, grad_middle[...] * attn_all),
        (3, input_all),
        (4, along * mods[:, GAIN_TWO : GAIN_TWO + 1]),
        (5, cot_full * mlp),
    )
    for k, values in terms:
        small[k * SLOTS : (k + 1) * SLOTS, :] = doc_sums(values, chosen)[:SLOTS]
    small[GAIN_TWO : GAIN_TWO + 1, :] = doc_sums(along * (1.0 + pick(4)), ones)[:1]
    branch = (cot_full * gate).astype(LOW)
    small[DOWN_BIAS : DOWN_BIAS + 1, :] = dot(ones, branch, (1, 1))[:1]
    attn_term = pick(2) * attn_all
    squares = [
        jnp.sum(jnp.sum(v * v, axis=0, keepdims=True) * valid, axis=1, keepdims=True)
        for v in (result, attn_term, mlp_term)
    ]
    squares.append(jnp.sum(valid, axis=1, keepdims=True) * middle.shape[0])
    lane = lax.broadcasted_iota(jnp.int32, (1, small.shape[1]), 1)
    total = jnp.zeros(lane.shape, FULL)
    for i, value in enumerate(squares):
        total = jnp.where(lane == i, value, total)
    small[STATS : STATS + 1, :] = total


def attend_back(segs_row, segs_col, cosine, sine, weight_all, query, key, value, mixed, logsum, *rest):
    pieces, outs = rest[:4], rest[4:]
    parts, (grads, pieces_all, key_rows, value_rows, out_grad, key_grad, value_grad) = outs[:3], outs[3:]
    own = pieces[0].shape[1]
    head_width = query.shape[0]
    heads = head_width // HEAD_DIM
    weight, proj = weight_all[:, : 3 * head_width], weight_all[:, 3 * head_width :]
    half = HEAD_DIM // 2
    scale = HEAD_DIM ** (-0.5)
    for h in range(heads):
        rows = slice(h * HEAD_DIM, (h + 1) * HEAD_DIM)
        key_rows[h] = key[rows, :].astype(FULL).T.astype(LOW)
        value_rows[h] = value[rows, :].astype(FULL).T.astype(LOW)
    key_segs = jnp.where(segs_col[...] == 0, -1, segs_col[...])
    key_grad[...] = jnp.zeros_like(key_grad)
    value_grad[...] = jnp.zeros_like(value_grad)

    def turn_back(grad, span, base, at):
        cos, sin = cosine[:, span], sine[:, span]
        one, two = grad[:half], grad[half:]
        grads[base + at : base + at + half, span] = (one * cos + two * sin).astype(LOW)
        grads[base + at + half : base + at + HEAD_DIM, span] = (two * cos - one * sin).astype(LOW)

    for e in range(4):
        span = slice(e * own, (e + 1) * own)
        allowed = key_segs == segs_row[:, span]
        pieces_all[:, span] = pieces[e][...]
        out_grad[...] = dot(proj, pieces[e][...], (0, 0)).astype(LOW)
        for h in range(heads):
            rows = slice(h * HEAD_DIM, (h + 1) * HEAD_DIM)
            back = out_grad[rows, :]
            inner = jnp.sum(
                back.astype(FULL) * mixed[rows, span].astype(FULL), axis=0, keepdims=True
            )
            scores = dot(key_rows[h], query[rows, span], (1, 0))
            scores = jnp.where(allowed, scores, MASK_FILL)
            probability = jnp.exp(scores - logsum[h : h + 1, span])
            grad_probs = dot(value_rows[h], back, (1, 0))
            score_grad = (probability * (grad_probs - inner)).astype(LOW)
            value_grad[rows, :] += dot(back, probability.astype(LOW), (1, 1))
            key_grad[rows, :] += dot(query[rows, span], score_grad, (1, 1))
            turn_back(dot(key[rows, :], score_grad, (1, 0)) * scale, span, 0, h * HEAD_DIM)
    ship(pieces_all)
    for e in (3, 1, 2, 0):
        span = slice(e * own, (e + 1) * own)
        for h in range(heads):
            turn_back(key_grad[h * HEAD_DIM : (h + 1) * HEAD_DIM, span], span, head_width, h * HEAD_DIM)
        grads[2 * head_width :, span] = value_grad[:, span].astype(LOW)
        part_of(parts, e)[...] = dot(weight, grads[:, span], (1, 0)).astype(LOW)
        ship_part(parts, e)


def attend_weights(grid, grads, mixed, inputs_all, pieces_all, *rest):
    blocks, total = rest[: grid.cols], rest[grid.cols]
    count = grads.shape[0]
    total[:, :count] = dot(inputs_all[...], grads[...], (1, 1)).astype(LOW)
    total[:, count:] = dot(pieces_all[...], mixed[...], (1, 1)).astype(LOW)
    size = blocks[0].shape[0]
    for j in range(grid.cols):
        blocks[j][...] = total[pl.ds(block_start(grid.col() ^ j, size), size), :]


def block_sum(*rest):
    total = rest[0][...].astype(FULL)
    for piece in rest[1:-1]:
        total = total + piece[...].astype(FULL)
    rest[-1][...] = total.astype(LOW)


def attn_weight_out(*rest):
    parts, (qkv_out, proj_out) = rest[:-2], rest[-2:]
    total = parts[0][...].astype(FULL)
    for part in parts[1:]:
        total = total + part[...].astype(FULL)
    width = qkv_out.shape[2]
    for i in range(3):
        qkv_out[i] = total[:, i * width : (i + 1) * width]
    proj_out[...] = total[:, 3 * width :].T


def feed_weight_out(*rest):
    parts, (up_out, bias_out, down_out) = rest[:-3], rest[-3:]
    total = parts[0][...].astype(FULL)
    for part in parts[1:]:
        total = total + part[...].astype(FULL)
    size, count = up_out.shape
    up_out[...] = total[:size, :count]
    down_out[...] = total[:size, count:]
    bias_out[...] = total[size, :count]


def finish_backward(grid, segs, mods, stream, grad_middle, result, small_in, part, near, far, *rest):
    outs, (grad_low, blocks) = rest[: grid.cols], rest[grid.cols :]
    pick = token_mods_of(mods[...], segs[...])
    chosen = slot_rows(segs[...])
    ones = jnp.ones(chosen.shape, LOW)
    input_grad = three_terms(part, near, far)
    normed, inverse = normalize(stream[...].astype(FULL))
    gain = mods[:, GAIN_ONE : GAIN_ONE + 1]
    grown = input_grad * (1.0 + pick(1))
    grad = grad_middle[...] + normalize_back(grown * gain, normed, inverse)
    grad_low[...] = grad.astype(LOW)
    size = grad.shape[0] // grid.cols
    own = grad.shape[1]
    for step in range(grid.cols):
        place = pl.ds(block_start(grid.source(step), size), size)
        outs[step][:size, :own] = grad_low[place, :]
        outs[step][:size, own : 2 * own] = result[place, :]
    shift = doc_sums(input_grad, chosen)[:SLOTS]
    scale = doc_sums(input_grad * normed * gain, chosen)[:SLOTS]
    norm_gain = doc_sums(grown * normed, ones)[:1]
    for c in range(grid.cols):
        span = slice(c * size, (c + 1) * size)
        blocks[c, :, :size] = small_in[:, span]
        blocks[c, :SLOTS, :size] = shift[:, span]
        blocks[c, SLOTS : 2 * SLOTS, :size] = scale[:, span]
        blocks[c, GAIN_ONE : GAIN_ONE + 1, :size] = norm_gain[:, span]
        blocks[c, STATS : STATS + 1, :size] = small_in[STATS : STATS + 1, :size]
    for step in range(grid.cols):
        terms = split(blocks[grid.source(step)].T, 2)
        outs[step][:, 2 * own :] = jnp.concatenate(terms, 1).astype(LOW)


def modulation_back(grid, slot_count, dp_count, *rest):
    times, (table, weight), rest = rest[:dp_count], rest[dp_count : dp_count + 2], rest[dp_count + 2 :]
    pieces, outs = rest[: 2 * dp_count], rest[2 * dp_count :]
    weight_out, bias_out, gain_one_out, gain_two_out, down_bias_out, stats_out, embed_out = outs[:7]
    embed, grads = outs[7:]
    per = grid.per_row
    embed[...] = jnp.zeros_like(embed)
    size = grads.shape[2]
    total = jnp.zeros((LANES - 6 * SLOTS, size), FULL)
    for d in range(dp_count):
        for far in range(2):
            piece = pieces[2 * d + far]
            for s in range(2 * per):
                sequence = (grid.row() ^ (2 * far + s // per)) * per + s % per
                first = block_start(d * per * grid.rows + sequence, SLOTS)
                for slot in range(slot_count):
                    time = times[d][sequence, slot]
                    embed[pl.ds(first + slot, 1), :] = table[pl.ds(time, 1), :]
                for k in range(6):
                    grads[k, pl.ds(first, SLOTS), :] = piece[s, k * SLOTS : (k + 1) * SLOTS, :]
                total = total + piece[s, 6 * SLOTS :, :]
    for k in range(6):
        rows = grads[k]
        weight_out[k] = dot(rows, embed[...], (0, 0), PRECISE)
        bias_out[k : k + 1, :] = jnp.sum(rows, axis=0, keepdims=True)
        part = dot(rows, weight[k].astype(FULL), (1, 0), PRECISE)
        embed_out[...] = part if k == 0 else embed_out[...] + part
    gain_one_out[...] = total[GAIN_ONE - 6 * SLOTS]
    gain_two_out[...] = total[GAIN_TWO - 6 * SLOTS]
    down_bias_out[...] = total[DOWN_BIAS - 6 * SLOTS]
    squares = total[STATS - 6 * SLOTS : STATS - 6 * SLOTS + 1, :]
    stats_out[...] = jnp.sqrt(squares / squares[:, 3:4])[0, :3]


def table_sum(grid, slot_count, dp_count, *rest):
    times, parts, (table_out, total) = rest[:dp_count], rest[dp_count:-2], rest[-2:]
    found = parts[0][...]
    for part in parts[1:]:
        found = found + part[...]
    total[...] = found
    table_out[...] = jnp.zeros_like(table_out)
    for d in range(dp_count):
        for sequence in range(grid.cols):
            for slot in range(slot_count):
                time = times[d][sequence, slot]
                at = (d * grid.cols + sequence) * SLOTS + slot
                table_out[pl.ds(time, 1), :] += total[at : at + 1, :]


def per_device(
    tokens,
    cotangent,
    segment_ids,
    doc_times,
    time_table,
    attn_gain,
    mlp_gain,
    mod_weight,
    mod_bias,
    qkv_weight,
    proj_weight,
    up_weight,
    up_bias,
    down_weight,
    down_bias,
):
    grid = Grid()
    dp_count = lax.axis_size("dp")
    width_local = tokens.shape[0]
    width = width_local * grid.cols
    own = tokens.shape[1] // grid.cols
    head_width = qkv_weight.shape[2]
    hidden_local = up_weight.shape[1]
    slot_count = doc_times.shape[1]
    cond_width = mod_weight.shape[2]
    if segment_ids.shape[0] != grid.cols * SEQ or own * grid.rows != SEQ or grid.rows != 4:
        raise ValueError("sequence split")
    low_tile = shape((width, own), LOW)
    full_tile = shape((width, own), FULL)
    low_piece = shape((width_local, own), LOW)
    part_tiles = [low_tile, low_tile, shape((2 * width, own), LOW)]

    part_rows = width_local // dp_count
    part_start = lax.axis_index("dp") * part_rows

    def gather_weight(parts):
        parts = [lax.dynamic_slice_in_dim(p, part_start, part_rows, 0) for p in parts]
        part = jnp.concatenate(parts, 1) if len(parts) > 1 else parts[0]
        return lax.all_gather(part, ("col", "dp"), axis=0, tiled=True)

    attn_block = run(
        pack, "pack", [shape((width_local, 4 * head_width), LOW)],
        [qkv_weight.transpose(1, 0, 2), proj_weight],
    )
    attn_weights = gather_weight(attn_block)

    bundles = run(
        functools.partial(prepare, grid, slot_count), "prepare",
        [shape((width_local, 2 * own + 2 * LANES), LOW)] * grid.cols,
        [doc_times, time_table, mod_weight, mod_bias, attn_gain, mlp_gain,
         down_bias, tokens, cotangent],
        [pltpu.VMEM((SLOTS, cond_width), FULL), pltpu.VMEM((LANES, width_local), FULL),
         pltpu.VMEM((grid.per_row, width_local, 2 * LANES), LOW)],
        smem=1,
    )
    bundles = relayout(bundles)
    segs_row, segs_col, segs_own, cosine, sine = run(
        functools.partial(places, grid, slot_count), "places",
        [shape((1, SEQ), jnp.int32), shape((SEQ, 1), jnp.int32), shape((1, own), jnp.int32)]
        + [shape((HEAD_DIM // 2, SEQ), FULL)] * 2,
        [segment_ids.reshape(-1, own)],
    )
    input_one, stream, cot, mods = run(
        functools.partial(first_norm, grid), "first_norm",
        [low_tile] + far_all([low_tile] * 2) + [shape((width, LANES), FULL)], [segs_own] + bundles,
    )

    def branch_filler(ready):
        [late] = after([ready], [cot])
        return run(branch_grad, "branch_grad", [low_tile], [segs_own, mods, Far(late)])

    rows_one, [branch] = gather_rows(input_one, branch_filler)
    branch_rows = gather_rows(branch)
    times = [doc_times] + [swap(doc_times, "dp", d) for d in range(1, dp_count)]
    rows_one[3:] = after([branch_rows[1]] + times[1:], rows_one[3:])

    feed_weights = gather_weight(after(rows_one[2:3] + [attn_weights], [up_weight, down_weight]))
    *parts, query, key, value, mixed, logsum, inputs_one = run(
        attend, "attend",
        far_all(part_tiles + [shape((head_width, SEQ), LOW)] * 4) + [shape((8, SEQ), FULL)]
        + [Far(shape((width, SEQ), LOW))],
        [segs_row] + far_all([segs_col, cosine, sine, attn_weights] + rows_one),
        [pltpu.VMEM((head_width // HEAD_DIM, SEQ, HEAD_DIM), LOW)],
    )
    attn_terms = scatter_rows(parts)
    input_two, middle, attn = run(
        second_norm, "second_norm", [low_tile] + far_all([full_tile, low_tile]),
        [segs_own, mods, Far(stream), Far(attn_terms[0])] + attn_terms[1:],
    )
    rows_two = gather_rows(input_two)
    hidden_tile = shape((hidden_local, SEQ), LOW)
    *parts, hidden, pre_grad, inputs_two, branch_all = run(
        feed_first, "feed_first",
        far_all(part_tiles + [hidden_tile] * 2 + [shape((width, SEQ), LOW)] * 2),
        [Far(feed_weights), up_bias] + far_all(rows_two + branch_rows),
    )
    def grads_filler(ready):
        [late] = after([ready], [hidden])
        return run(
            feed_grads_of, "feed_grads",
            [Far(shape((grid.cols, width_local + 16, 2 * hidden_local), LOW))],
            far_all([late, pre_grad, inputs_two, branch_all]),
        )

    input_terms, [feed_grads] = scatter_rows(parts, grads_filler, True)
    feed_grads = lax.psum_scatter(
        feed_grads.reshape(-1, 2 * hidden_local), "col", scatter_dimension=0, tiled=True
    )
    grad_middle, grad_attn, input_grad = run(
        middle_grad, "middle_grad", [Far(full_tile), low_tile, Far(low_tile)],
        [segs_own, mods, Far(middle), Far(cot), Far(input_terms[0])] + input_terms[1:],
    )

    def feed_filler(ready):
        [late] = after([ready], [hidden])
        return run(feed_out, "feed_out", far_all(part_tiles), far_all([feed_weights, late]))

    attn_rows, parts = gather_rows(grad_attn, feed_filler)
    mlp_terms = scatter_rows(parts)
    *parts, qkv_grads, attn_all = run(
        attend_back, "attend_back",
        far_all(part_tiles + [shape((3 * head_width, SEQ), LOW), shape((width, SEQ), LOW)]),
        [segs_row] + far_all([segs_col, cosine, sine, attn_weights, query, key, value, mixed])
        + [logsum] + far_all(attn_rows),
        [pltpu.VMEM((head_width // HEAD_DIM, SEQ, HEAD_DIM), LOW)] * 2
        + [pltpu.VMEM((head_width, own), LOW)] + [pltpu.VMEM((head_width, SEQ), FULL)] * 2,
    )

    def back_filler(ready):
        [late] = after([ready], [qkv_grads])
        blocks = run(
            functools.partial(attend_weights, grid), "attend_weights",
            far_all([shape((width_local, 4 * head_width), LOW)] * grid.cols),
            far_all([late, mixed, inputs_one, attn_all]), [pltpu.VMEM((width, 4 * head_width), LOW)],
        )
        [first] = after(blocks[:1], mlp_terms[:1])
        found = run(
            finish_forward, "finish_forward", [low_tile, shape((LANES, width), FULL)],
            [segs_own, mods] + far_all([middle, cot, attn, grad_middle, input_grad, first])
            + mlp_terms[1:],
        )
        return found + blocks

    back_terms, (result, small, *attn_grads) = scatter_rows(parts, back_filler)
    wide = width_local
    bundles = run(
        functools.partial(finish_backward, grid), "finish_backward",
        [shape((wide, 2 * own + 2 * LANES), LOW)] * grid.cols,
        [segs_own, mods, Far(stream), Far(grad_middle), result, small, Far(back_terms[0])]
        + back_terms[1:],
        [pltpu.VMEM((width, own), LOW), pltpu.VMEM((grid.cols, LANES, wide), FULL)],
    )
    out_tile = shape((width_local, grid.cols * own), LOW)
    tokens_grad, block_output, small = run(
        functools.partial(unbundle, grid), "unbundle",
        [out_tile, out_tile, shape((grid.per_row, LANES, wide), FULL)], relayout(bundles, back=True),
    )

    small = jnp.concatenate([small, swap(small, "row", 1)], 0)
    pieces = []
    for d in range(dp_count):
        for far in range(2):
            count = dp_count * grid.rows
            pairs = [(i, i ^ (d * grid.rows + 2 * far)) for i in range(count)]
            pieces.append(lax.ppermute(small, ("dp", "row"), pairs) if d or far else small)
    seq_total = grid.cols * dp_count
    vector = shape((width_local,), FULL)
    embed_tile = shape((seq_total * SLOTS, cond_width), FULL)
    weight_out, bias_out, gain_one_out, gain_two_out, down_bias_out, stats, embed = run(
        functools.partial(modulation_back, grid, slot_count, dp_count), "modulation_back",
        [
            shape((6, width_local, cond_width), FULL), shape((6, width_local), FULL),
            vector, vector, vector, shape((3,), FULL), embed_tile,
        ],
        times + [time_table, mod_weight] + pieces,
        [pltpu.VMEM((seq_total * SLOTS, cond_width), FULL),
         pltpu.VMEM((6, seq_total * SLOTS, width_local), FULL)],
        smem=dp_count,
    )
    [table_out] = run(
        functools.partial(table_sum, grid, slot_count, dp_count), "table_sum",
        [shape(time_table.shape, FULL)],
        times + [embed] + [swap(embed, "col", j) for j in range(1, grid.cols)],
        [pltpu.VMEM((seq_total * SLOTS, cond_width), FULL)], smem=dp_count,
    )

    def all_dp(part):
        return [part] + [swap(part, "dp", d) for d in range(1, dp_count)]

    attn_grads = attn_grads[:1] + [swap(attn_grads[j], "col", j) for j in range(1, grid.cols)]
    [attn_sum] = run(
        block_sum, "block_sum", [shape((width_local, 4 * head_width), LOW)], attn_grads
    )
    up_out, up_bias_out, down_out = run(
        feed_weight_out, "feed_weight_out",
        [shape(up_weight.shape, FULL), shape(up_bias.shape, FULL), shape(down_weight.shape, FULL)],
        all_dp(feed_grads),
    )
    qkv_out, proj_out = run(
        attn_weight_out, "attn_weight_out",
        [shape((3, width_local, head_width), FULL), shape(proj_weight.shape, FULL)],
        all_dp(attn_sum),
    )
    return (
        block_output,
        tokens_grad,
        table_out,
        gain_one_out,
        gain_two_out,
        weight_out,
        bias_out,
        qkv_out.transpose(1, 0, 2),
        proj_out,
        up_out,
        up_bias_out,
        down_out,
        down_bias_out,
        stats,
    )


def solution(mesh):
    return jax.shard_map(
        per_device,
        mesh=mesh,
        in_specs=(
            P("col", ("dp", "row")),
            P("col", ("dp", "row")),
            P("dp"),
            P("dp", None),
            P(),
            P("col"),
            P("col"),
            P(None, "col", None),
            P(None, "col"),
            P("col", None, "row"),
            P("row", "col"),
            P("col", "row"),
            P("row"),
            P("col", "row"),
            P("col"),
        ),
        out_specs=(
            P("col", ("dp", "row")),
            P("col", ("dp", "row")),
            P(),
            P("col"),
            P("col"),
            P(None, "col", None),
            P(None, "col"),
            P("col", None, "row"),
            P("row", "col"),
            P("col", "row"),
            P("row"),
            P("col", "row"),
            P("col"),
            P(),
        ),
        check_vma=False,
    )
```

time: 525 us -> 296 us (0.56); the launches traced: 516 us -> 293 us
  blocking collectives: 130 us -> 0 us
  Pallas kernels: 0 us -> 86.2 us
  matrix products: 73.3 us -> 0 us
  other arithmetic: 60.4 us -> 4.96 us
  local copies, waits for them, and re-layouts: 66.1 us -> 24.2 us
  starting transfers between devices: 66.6 us -> 60.9 us
    pallas_call x0 -> x21, Pallas kernels: none -> 86.2 us  [run(): pl.pallas_call(kernel if buffers else body, out_shape=outs, in_specs=[who...]
    psum x3 -> x0, blocking collectives: 77.9 us -> none  [the longest x1 41.6 us: per_device(): stats = lax.psum(stat_terms, ('dp', 'row', 'col'))]
    dot_general x24 -> x0, matrix products: 73.3 us -> none  [the longest x12 36.9 us: dot(): lax.dot_general(left, right, (((left_dim,), (right_dim,)), ((), ())), pre...]
    all_gather x5 -> x0, blocking collectives: 52.1 us -> none  [the longest x2 37.2 us: gather_cols(): return lax.all_gather(values, 'col', axis=0, tiled=True)]
    dynamic_update_slice x17 -> x0, local copies, waits for them, and re-layouts: 18.2 us -> none  [the longest x8 9.16 us: relayout_in(): result = lax.dynamic_update_slice(result, got, (source * width_local, 0))]
    ppermute x16 -> x11, waiting for transfers between devices: 23.2 us -> 40.1 us  [the longest x8 34.3 us: relayout(): got.append(lax.ppermute(piece, ('row', 'col'), pairs))]
    reduce_sum x12 -> x0, other arithmetic: 14.4 us -> none  [the longest x1 3.83 us: per_device(): jnp.sum(valid_rows * result * result)]
    ppermute x20 -> x30, starting transfers between devices: 13.1 us -> 24.8 us  [swap(): return lax.ppermute(values, axis, [(i, i ^ bit) for i in range(count)])]
  transfers between devices with their start and end apart: 45 -> 44, of which waited for: 14 -> 26; matrix products, arithmetic and copies ran while one was open for 36% -> 1% of each run, Pallas kernels for 0% -> 25%
where the time goes in v2:
time: 296 us; the launch traced here: 293 us
  waiting for transfers between devices  102 us (34%)
  Pallas kernels  86.2 us (29%)
  starting transfers between devices  60.9 us (21%)
  local copies, waits for them, and re-layouts  24.2 us (8%)
  between operations  14.8 us (5%)
  other arithmetic  4.96 us (2%)
    pallas_call x21, Pallas kernels, run(): pl.pallas_call(kernel if buffers else body, out_shape=outs, in_specs=[who...  86.2 us
    ppermute x30, waiting for transfers between devices, swap(): return lax.ppermute(values, axis, [(i, i ^ bit) for i in range(count)])  61.4 us
    ppermute x8, waiting for transfers between devices, relayout(): got.append(lax.ppermute(piece, ('row', 'col'), pairs))  34.3 us
    ppermute x8, starting transfers between devices, relayout(): got.append(lax.ppermute(piece, ('row', 'col'), pairs))  31.8 us
    ppermute x30, starting transfers between devices, swap(): return lax.ppermute(values, axis, [(i, i ^ bit) for i in range(count)])  24.8 us
    unnamed x107, local copies, waits for them, and re-layouts  23.5 us
  transfers between devices with their start and end apart: 44, of which 26 were waited for; matrix products, arithmetic and copies ran while one was open for 1% of the time, Pallas kernels for 25%

profile of v2, /device:TPU:0, one launch (start us, length us, event | category | flops | bytes accessed | tf_op | source)
XLA Modules:
  0.0 292.5 jit_solution(11655878770118854941)
XLA Ops:
  19.0 7.3 %collective-permute-start.1 = (bf16[192,640]{1,0:T(8,128)(2,1)S(1)}, bf16[192,640]{1,0:T(8,128)(2,1)S(1)}, u32[]{:S(2)}, u32[]{:S(2)}) collective-permute-start(bf16[192,640]{1,0:T(8,128)(2,1)S(1)} %get-tuple-element.101), channel_id=1, source_target_pairs={{0,4},{1,8},{2,12},{3,0},{4,6},{5,10},{6,14},{7,2},{8,5},{9,9},{10... | collective-permute-start | bytes 737288 | tf_op jit(solution)/shard_map/ppermute | solution.py:87
  27.5 3.5 %collective-permute-start.3 = (bf16[192,640]{1,0:T(8,128)(2,1)S(1)}, bf16[192,640]{1,0:T(8,128)(2,1)S(1)}, u32[]{:S(2)}, u32[]{:S(2)}) collective-permute-start(bf16[192,640]{1,0:T(8,128)(2,1)S(1)} %get-tuple-element.103), channel_id=1, source_target_pairs={{0,12},{1,0},{2,4},{3,8},{4,14},{5,2},{6,6},{7,10},{8,13},{9,1},{1... | collective-permute-start | bytes 737288 | tf_op jit(solution)/shard_map/ppermute | solution.py:87
  33.9 7.6 %collective-permute-done.1.refs_2_ = bf16[192,640]{1,0:T(8,128)(2,1)S(1)} collective-permute-done((bf16[192,640]{1,0:T(8,128)(2,1)S(1)}, bf16[192,640]{1,0:T(8,128)(2,1)S(1)}, u32[]{:S(2)}, u32[]{:S(2)}) %collective-permute-start.1) | collective-permute-done | bytes 245792 | tf_op jit(solution)/shard_map/ppermute | solution.py:87
  41.5 4.5 %collective-permute-done.2.refs_3_ = bf16[192,640]{1,0:T(8,128)(2,1)S(1)} collective-permute-done((bf16[192,640]{1,0:T(8,128)(2,1)S(1)}, bf16[192,640]{1,0:T(8,128)(2,1)S(1)}, u32[]{:S(2)}, u32[]{:S(2)}) %collective-permute-start.2) | collective-permute-done | bytes 245792 | tf_op jit(solution)/shard_map/ppermute | solution.py:87
  46.0 19.3 %collective-permute-done.3.refs_4_ = bf16[192,640]{1,0:T(8,128)(2,1)S(1)} collective-permute-done((bf16[192,640]{1,0:T(8,128)(2,1)S(1)}, bf16[192,640]{1,0:T(8,128)(2,1)S(1)}, u32[]{:S(2)}, u32[]{:S(2)}) %collective-permute-start.3) | collective-permute-done | bytes 245792 | tf_op jit(solution)/shard_map/ppermute | solution.py:87
  68.8 9.2 %collective-permute-done.5.refs_7_ = bf16[768,256]{1,0:T(8,128)(2,1)S(1)} collective-permute-done((bf16[768,256]{1,0:T(8,128)(2,1)S(1)}, bf16[768,256]{1,0:T(8,128)(2,1)S(1)}, u32[]{:S(2)}, u32[]{:S(2)}) %collective-permute-start.5) | collective-permute-done | bytes 393248 | tf_op jit(solution)/shard_map/ppermute | solution.py:33
  81.4 2.4 collective-permute-start.8
  85.4 14.7 %attend.1 = (bf16[768,256]{1,0:T(8,128)(2,1)}, bf16[768,256]{1,0:T(8,128)(2,1)}, bf16[1536,256]{1,0:T(8,128)(2,1)}, bf16[192,1024]{1,0:T(8,128)(2,1)}, bf16[192,...) custom-call(s32[1,1024]{1,0:T(1,128)} %copy-done.33, ...), custom_call_target="tpu_custom_call" | custom-call | bytes 7774208 | tf_op jit(solution)/shard_map/attend/pallas_call | solution.py:228
  100.2 2.5 collective-permute-done.9.refs_4_
  105.9 9.9 %collective-permute-done.10.refs_5_ = bf16[768,256]{1,0:T(8,128)(2,1)S(1)} collective-permute-done((bf16[768,256]{1,0:T(8,128)(2,1)S(1)}, bf16[768,256]{1,0:T(8,128)(2,1)S(1)}, u32[]{:S(2)}, u32[]{:S(2)}) %collective-permute-start.10) | collective-permute-done | bytes 393248 | tf_op jit(solution)/shard_map/ppermute | solution.py:33
  119.5 4.7 %collective-permute-done.14.refs_8_ = bf16[768,256]{1,0:T(8,128)(2,1)S(1)} collective-permute-done((bf16[768,256]{1,0:T(8,128)(2,1)S(1)}, bf16[768,256]{1,0:T(8,128)(2,1)S(1)}, u32[]{:S(2)}, u32[]{:S(2)}) %collective-permute-start.14) | collective-permute-done | bytes 393248 | tf_op jit(solution)/shard_map/ppermute | solution.py:33
  124.7 7.1 %collective-permute-done.12.refs_4_ = bf16[768,256]{1,0:T(8,128)(2,1)S(1)} collective-permute-done((bf16[768,256]{1,0:T(8,128)(2,1)S(1)}, bf16[768,256]{1,0:T(8,128)(2,1)S(1)}, u32[]{:S(2)}, u32[]{:S(2)}) %collective-permute-start.12) | collective-permute-done | bytes 393248 | tf_op jit(solution)/shard_map/ppermute | solution.py:33
  133.7 12.7 %feed_first.1 = (bf16[768,256]{1,0:T(8,128)(2,1)}, bf16[768,256]{1,0:T(8,128)(2,1)}, bf16[1536,256]{1,0:T(8,128)(2,1)}, bf16[768,1024]{1,0:T(8,128)(2,1)}, bf16[...) custom-call(bf16[768,1536]{1,0:T(8,128)(2,1)} %all-gather.5.cloned.1.call-done.refs_0_, ...), custom_call_target="tpu_custom_call" | custom-call | bytes 13370880 | tf_op jit(solution)/shard_map/feed_first/pallas_call | solution.py:228
  146.7 2.4 collective-permute-done.16.refs_5_
  150.6 7.9 %feed_grads.1 = bf16[4,208,1536]{2,1,0:T(8,128)(2,1)} custom-call(bf16[768,1024]{1,0:T(8,128)(2,1)} %get-tuple-element.136.refs_0_.refs_1_, bf16[768,1024]{1,0:T(8,128)(2,1)} %get-tuple-element.128.refs_1_, bf16[768,1024]{1,0:T(8,128)(2,1)} %get-tuple-element.129.refs_2_, bf16[768,1024]{1,0:T(8,128)(2,1)} %get-tuple-element.130.refs_3_), custom_call_target="tpu_custom_call" | custom-call | bytes 8847360 | tf_op jit(solution)/shard_map/feed_grads/pallas_call | solution.py:228
  158.5 2.9 collective-permute-done.17.refs_6_
  168.5 4.6 %feed_out.1 = (bf16[768,256]{1,0:T(8,128)(2,1)}, bf16[768,256]{1,0:T(8,128)(2,1)}, bf16[1536,256]{1,0:T(8,128)(2,1)}) custom-call(bf16[768,1536]{1,0:T(8,128)(2,1)} %all-gather.5.cloned.1.call-done.refs_0_, bf16[768,1024]{1,0:T(8,128)(2,1)} %get-tuple-element.136.refs_0_.refs_1_), custom_call_target="tpu_custom_call" | custom-call | bytes 5505024 | tf_op jit(solution)/shard_map/feed_out/pallas_call | solution.py:228
  173.2 5.1 %collective-permute-done.19.refs_12_ = bf16[768,256]{1,0:T(8,128)(2,1)S(1)} collective-permute-done((bf16[768,256]{1,0:T(8,128)(2,1)S(1)}, bf16[768,256]{1,0:T(8,128)(2,1)S(1)}, u32[]{:S(2)}, u32[]{:S(2)}) %collective-permute-start.19) | collective-permute-done | bytes 393248 | tf_op jit(solution)/shard_map/ppermute | solution.py:33
  180.8 16.4 %attend_back.1 = (bf16[768,256]{1,0:T(8,128)(2,1)}, bf16[768,256]{1,0:T(8,128)(2,1)}, bf16[1536,256]{1,0:T(8,128)(2,1)}, bf16[576,1024]{1,0:T(8,128)(2,1)}, bf16[768,1024]{1,0:T(8,128)(2,1)}) custom-call(s32[1,1024]{1,0:T(1,128)} %copy-done.33, s32[1024,1]{1,0:T(8,128)} %copy-done, f32[32,1024]{1,0:T(8,128)} %copy-done.7, f32[32,1024]{1,0:T(8,128)} %copy-done.8, ...), custom_call_target="tpu_custom_call" | custom-call | bytes 8953856 | tf_op jit(solution)/shard_map/attend_back/pallas_call | solution.py:228
  202.9 6.4 %attend_weights.1 = (bf16[192,768]{1,0:T(8,128)(2,1)}, bf16[192,768]{1,0:T(8,128)(2,1)}, bf16[192,768]{1,0:T(8,128)(2,1)}, bf16[192,768]{1,0:T(8,128)(2,1)}) custom-call(bf16[576,1024]{1,0:T(8,128)(2,1)} %get-tuple-element.150.refs_0_, bf16[192,1024]{1,0:T(8,128)(2,1)} %get-tuple-element.145.refs_8_.refs_1_, bf16[768,1024]{1,0:T(8,128)(2,1)} %get-tuple-element.151.refs_2_, ...), custom_call_target="tpu_custom_call" | custom-call | bytes 5898240 | tf_op jit(solution)/shard_map/attend_weights/pallas_call | solution.py:228
  210.8 3.0 %collective-permute-start.37 = (bf16[192,768]{1,0:T(8,128)(2,1)}, bf16[192,768]{1,0:T(8,128)(2,1)}, u32[]{:S(2)}, u32[]{:S(2)}) collective-permute-start(bf16[192,768]{1,0:T(8,128)(2,1)} %get-tuple-element.174), channel_id=1, source_target_pairs={{0,2},{1,3},{2,0},{3,1},{4,6},{5,7},{6,4},{7,5},{8,10},{9,11},{10,... | collective-permute-start | bytes 884744 | tf_op jit(solution)/shard_map/ppermute | solution.py:33
  220.6 3.5 %finish_forward.1 = (bf16[768,256]{1,0:T(8,128)(2,1)S(1)}, f32[64,768]{1,0:T(8,128)S(1)}) custom-call(s32[1,256]{1,0:T(1,128)S(1)} %get-tuple-element.99.refs_0_, f32[768,64]{1,0:T(8,128)S(1)} %get-tuple-element.104.refs_1_, f32[768,256]{1,0:T(8,128)S(1)} %get-tuple-element.119.refs_2_, bf16[768,256]{1,0:T(8,128)(2,1)S(1)} %get-tuple-element.112.refs_2_.refs_3_, ...), custom_call_target="tpu_custom_call" | custom-call | bytes 5112832 | tf_op jit(solution)/shard_map/finish_forward/pallas_call | solution.py:228
  224.2 3.9 %finish_backward.1 = (bf16[192,640]{1,0:T(8,128)(2,1)S(1)}, bf16[192,640]{1,0:T(8,128)(2,1)S(1)}, bf16[192,640]{1,0:T(8,128)(2,1)S(1)}, bf16[192,640]{1,0:T(8,128)(2,1)S(1)}) custom-call(s32[1,256]{1,0:T(1,128)S(1)} %get-tuple-element.99.refs_0_, f32[768,64]{1,0:T(8,128)S(1)} %get-tuple-element.104.refs_1_, bf16[768,256]{1,0:T(8,128)(2,1)S(1)} %get-tuple-element.105.refs_2_, ...), custom_call_target="tpu_custom_call" | custom-call | bytes 4523008 | tf_op jit(solution)/shard_map/finish_backward/pallas_call | solution.py:228
  228.9 7.0 %collective-permute-start.26 = (bf16[192,640]{1,0:T(8,128)(2,1)S(1)}, bf16[192,640]{1,0:T(8,128)(2,1)S(1)}, u32[]{:S(2)}, u32[]{:S(2)}) collective-permute-start(bf16[192,640]{1,0:T(8,128)(2,1)S(1)} %get-tuple-element.162), channel_id=1, source_target_pairs={{4,0},{8,1},{12,2},{0,3},{6,4},{10,5},{14,6},{2,7},{5,8},{9,9},{13... | collective-permute-start | bytes 737288 | tf_op jit(solution)/shard_map/ppermute | solution.py:87
  235.9 4.0 %collective-permute-done.37.rest_2_ = bf16[192,768]{1,0:T(8,128)(2,1)} collective-permute-done((bf16[192,768]{1,0:T(8,128)(2,1)}, bf16[192,768]{1,0:T(8,128)(2,1)}, u32[]{:S(2)}, u32[]{:S(2)}) %collective-permute-start.37) | collective-permute-done | bytes 294944 | tf_op jit(solution)/shard_map/ppermute | solution.py:33
  239.9 11.4 %collective-permute-start.28 = (bf16[192,640]{1,0:T(8,128)(2,1)S(1)}, bf16[192,640]{1,0:T(8,128)(2,1)S(1)}, u32[]{:S(2)}, u32[]{:S(2)}) collective-permute-start(bf16[192,640]{1,0:T(8,128)(2,1)S(1)} %get-tuple-element.164), channel_id=1, source_target_pairs={{12,0},{0,1},{4,2},{8,3},{14,4},{2,5},{6,6},{10,7},{13,8},{1,9},{5... | collective-permute-start | bytes 737288 | tf_op jit(solution)/shard_map/ppermute | solution.py:87
  254.7 2.9 %collective-permute-done.28.rest_3_ = bf16[192,640]{1,0:T(8,128)(2,1)S(1)} collective-permute-done((bf16[192,640]{1,0:T(8,128)(2,1)S(1)}, bf16[192,640]{1,0:T(8,128)(2,1)S(1)}, u32[]{:S(2)}, u32[]{:S(2)}) %collective-permute-start.28) | collective-permute-done | bytes 245792 | tf_op jit(solution)/shard_map/ppermute | solution.py:87
  258.8 4.2 %collective-permute-start.29 = (f32[1,64,192]{2,1,0:T(8,128)S(1)}, f32[1,64,192]{2,1,0:T(8,128)S(1)}, u32[]{:S(2)}, u32[]{:S(2)}) collective-permute-start(f32[1,64,192]{2,1,0:T(8,128)S(1)} %get-tuple-element.167), channel_id=1, source_target_pairs={{0,4},{4,0},{8,12},{12,8},{1,5},{5,1},{9,13},{13,9},{2,6},{6,2},{1... | collective-permute-start | bytes 147464 | tf_op jit(solution)/shard_map/ppermute | solution.py:33
  263.9 2.2 collective-permute-start.31
  267.4 3.6 %collective-permute-done.32.rest_7_ = f32[2,64,192]{2,1,0:T(8,128)S(1)} collective-permute-done((f32[2,64,192]{2,1,0:T(8,128)S(1)}, f32[2,64,192]{2,1,0:T(8,128)S(1)}, u32[]{:S(2)}, u32[]{:S(2)}) %collective-permute-start.32) | collective-permute-done | bytes 98336 | tf_op jit(solution)/shard_map/ppermute | solution.py:936
  273.3 2.6 modulation_back.1
  276.0 2.3 collective-permute-start.35
  (196 shorter events, 76.0 us)
Async XLA Ops:
  7.2 70.8 %all-gather.3.cloned.1.call-start = ((), (), s32[]{:S(2)}) async-start(), calls=%async_computation.1 | async-start | bytes 1327104 | tf_op jit(solution)/shard_map/all_gather | solution.py:810
  10.0 123.8 %all-gather.5.cloned.1.call-start = ((), (), s32[]{:S(2)}) async-start(), calls=%async_computation.2 | async-start | bytes 2654208 | tf_op jit(solution)/shard_map/all_gather | solution.py:810
  18.3 15.6 %collective-permute-start = (bf16[192,640]{1,0:T(8,128)(2,1)S(1)}, bf16[192,640]{1,0:T(8,128)(2,1)S(1)}, u32[]{:S(2)}, u32[]{:S(2)}) collective-permute-start(bf16[192,640]{1,0:T(8,128)(2,1)S(1)} %get-tuple-element.100), channel_id=1, source_target_pairs={{0,0},{1,4},{2,8},{3,12},{4,2},{5,6},{6,10},{7,14},{8,1},{9,5},{10... | collective-permute-start | bytes 737288 | tf_op jit(solution)/shard_map/ppermute | solution.py:87
  19.0 22.5 %collective-permute-start.1 = (bf16[192,640]{1,0:T(8,128)(2,1)S(1)}, bf16[192,640]{1,0:T(8,128)(2,1)S(1)}, u32[]{:S(2)}, u32[]{:S(2)}) collective-permute-start(bf16[192,640]{1,0:T(8,128)(2,1)S(1)} %get-tuple-element.101), channel_id=1, source_target_pairs={{0,4},{1,8},{2,12},{3,0},{4,6},{5,10},{6,14},{7,2},{8,5},{9,9},{10... | collective-permute-start | bytes 737288 | tf_op jit(solution)/shard_map/ppermute | solution.py:87
  26.3 19.6 %collective-permute-start.2 = (bf16[192,640]{1,0:T(8,128)(2,1)S(1)}, bf16[192,640]{1,0:T(8,128)(2,1)S(1)}, u32[]{:S(2)}, u32[]{:S(2)}) collective-permute-start(bf16[192,640]{1,0:T(8,128)(2,1)S(1)} %get-tuple-element.102), channel_id=1, source_target_pairs={{0,8},{1,12},{2,0},{3,4},{4,10},{5,14},{6,2},{7,6},{8,9},{9,13},{1... | collective-permute-start | bytes 737288 | tf_op jit(solution)/shard_map/ppermute | solution.py:87
  27.5 37.8 %collective-permute-start.3 = (bf16[192,640]{1,0:T(8,128)(2,1)S(1)}, bf16[192,640]{1,0:T(8,128)(2,1)S(1)}, u32[]{:S(2)}, u32[]{:S(2)}) collective-permute-start(bf16[192,640]{1,0:T(8,128)(2,1)S(1)} %get-tuple-element.103), channel_id=1, source_target_pairs={{0,12},{1,0},{2,4},{3,8},{4,14},{5,2},{6,6},{7,10},{8,13},{9,1},{1... | collective-permute-start | bytes 737288 | tf_op jit(solution)/shard_map/ppermute | solution.py:87
  66.5 11.5 %collective-permute-start.5 = (bf16[768,256]{1,0:T(8,128)(2,1)S(1)}, bf16[768,256]{1,0:T(8,128)(2,1)S(1)}, u32[]{:S(2)}, u32[]{:S(2)}) collective-permute-start(bf16[768,256]{1,0:T(8,128)(2,1)S(1)} %get-tuple-element.110.refs_5_), channel_id=1, source_target_pairs={{0,8},{4,12},{8,0},{12,4},{1,9},{5,13},{9,1},{13,5},{2,10},{6,14},... | collective-permute-start | bytes 1179656 | tf_op jit(solution)/shard_map/ppermute | solution.py:33
  78.9 135.7 %reduce-scatter.2.cloned.1.call-start = ((), (), s32[]{:S(2)}) async-start(), calls=%async_computation.3 | async-start | bytes 3194880 | tf_op jit(solution)/shard_map/reduce_scatter | solution.py:877
  103.8 12.0 %collective-permute-start.10 = (bf16[768,256]{1,0:T(8,128)(2,1)S(1)}, bf16[768,256]{1,0:T(8,128)(2,1)S(1)}, u32[]{:S(2)}, u32[]{:S(2)}) collective-permute-start(bf16[768,256]{1,0:T(8,128)(2,1)S(1)} %add_convert_fusion.3), channel_id=1, source_target_pairs={{0,8},{4,12},{8,0},{12,4},{1,9},{5,13},{9,1},{13,5},{2,10},{6,14},... | collective-permute-start | bytes 1179656 | tf_op jit(solution)/shard_map/ppermute | solution.py:33
  104.1 20.1 %collective-permute-start.14 = (bf16[768,256]{1,0:T(8,128)(2,1)S(1)}, bf16[768,256]{1,0:T(8,128)(2,1)S(1)}, u32[]{:S(2)}, u32[]{:S(2)}) collective-permute-start(bf16[768,256]{1,0:T(8,128)(2,1)S(1)} %branch_grad.1.refs_6_), channel_id=1, source_target_pairs={{0,8},{4,12},{8,0},{12,4},{1,9},{5,13},{9,1},{13,5},{2,10},{6,14},... | collective-permute-start | bytes 1179656 | tf_op jit(solution)/shard_map/ppermute | solution.py:33
  119.3 12.6 %collective-permute-start.12 = (bf16[768,256]{1,0:T(8,128)(2,1)S(1)}, bf16[768,256]{1,0:T(8,128)(2,1)S(1)}, u32[]{:S(2)}, u32[]{:S(2)}) collective-permute-start(bf16[768,256]{1,0:T(8,128)(2,1)S(1)} %get-tuple-element.122.refs_2_), channel_id=1, source_target_pairs={{0,8},{4,12},{8,0},{12,4},{1,9},{5,13},{9,1},{13,5},{2,10},{6,14},... | collective-permute-start | bytes 1179656 | tf_op jit(solution)/shard_map/ppermute | solution.py:33
  124.2 7.6 %collective-permute-start.15 = (bf16[768,256]{1,0:T(8,128)(2,1)S(1)}, bf16[768,256]{1,0:T(8,128)(2,1)S(1)}, u32[]{:S(2)}, u32[]{:S(2)}) collective-permute-start(bf16[768,256]{1,0:T(8,128)(2,1)S(1)} %collective-permute-done.14.refs_8_), channel_id=1, source_target_pairs={{0,4},{4,0},{8,12},{12,8},{1,5},{5,1},{9,13},{13,9},{2,6},{6,2},{1... | collective-permute-start | bytes 1179656 | tf_op jit(solution)/shard_map/ppermute | solution.py:33
  124.2 7.6 %collective-permute-start.11 = (bf16[768,256]{1,0:T(8,128)(2,1)S(1)}, bf16[768,256]{1,0:T(8,128)(2,1)S(1)}, u32[]{:S(2)}, u32[]{:S(2)}) collective-permute-start(bf16[768,256]{1,0:T(8,128)(2,1)S(1)} %get-tuple-element.122.refs_2_), channel_id=1, source_target_pairs={{0,4},{4,0},{8,12},{12,8},{1,5},{5,1},{9,13},{13,9},{2,6},{6,2},{1... | collective-permute-start | bytes 1179656 | tf_op jit(solution)/shard_map/ppermute | solution.py:33
  150.1 11.2 %collective-permute-start.17 = (bf16[768,256]{1,0:T(8,128)(2,1)S(1)}, bf16[768,256]{1,0:T(8,128)(2,1)S(1)}, u32[]{:S(2)}, u32[]{:S(2)}) collective-permute-start(bf16[768,256]{1,0:T(8,128)(2,1)S(1)} %add_convert_fusion.2), channel_id=1, source_target_pairs={{0,8},{4,12},{8,0},{12,4},{1,9},{5,13},{9,1},{13,5},{2,10},{6,14},... | collective-permute-start | bytes 1179656 | tf_op jit(solution)/shard_map/ppermute | solution.py:33
  166.8 11.5 %collective-permute-start.19 = (bf16[768,256]{1,0:T(8,128)(2,1)S(1)}, bf16[768,256]{1,0:T(8,128)(2,1)S(1)}, u32[]{:S(2)}, u32[]{:S(2)}) collective-permute-start(bf16[768,256]{1,0:T(8,128)(2,1)S(1)} %get-tuple-element.135.refs_10_), channel_id=1, source_target_pairs={{0,8},{4,12},{8,0},{12,4},{1,9},{5,13},{9,1},{13,5},{2,10},{6,14},... | collective-permute-start | bytes 1179656 | tf_op jit(solution)/shard_map/ppermute | solution.py:33
  180.1 17.4 %collective-permute-start.22 = (bf16[1536,256]{1,0:T(8,128)(2,1)}, bf16[1536,256]{1,0:T(8,128)(2,1)S(1)}, u32[]{:S(2)}, u32[]{:S(2)}) collective-permute-start(bf16[1536,256]{1,0:T(8,128)(2,1)} %get-tuple-element.155), channel_id=1, source_target_pairs={{0,4},{4,0},{8,12},{12,8},{1,5},{5,1},{9,13},{13,9},{2,6},{6,2},{1... | collective-permute-start | bytes 2359304 | tf_op jit(solution)/shard_map/ppermute | solution.py:33
  197.6 16.2 %collective-permute-start.23 = (bf16[768,256]{1,0:T(8,128)(2,1)S(1)}, bf16[768,256]{1,0:T(8,128)(2,1)S(1)}, u32[]{:S(2)}, u32[]{:S(2)}) collective-permute-start(bf16[768,256]{1,0:T(8,128)(2,1)S(1)} %add_convert_fusion), channel_id=1, source_target_pairs={{0,8},{4,12},{8,0},{12,4},{1,9},{5,13},{9,1},{13,5},{2,10},{6,14},... | collective-permute-start | bytes 1179656 | tf_op jit(solution)/shard_map/ppermute | solution.py:33
  202.6 21.5 %collective-permute-start.24 = (bf16[768,256]{1,0:T(8,128)(2,1)}, bf16[768,256]{1,0:T(8,128)(2,1)}, u32[]{:S(2)}, u32[]{:S(2)}) collective-permute-start(bf16[768,256]{1,0:T(8,128)(2,1)} %add_convert_fusion.1), channel_id=1, source_target_pairs={{0,8},{4,12},{8,0},{12,4},{1,9},{5,13},{9,1},{13,5},{2,10},{6,14},... | collective-permute-start | bytes 1179656 | tf_op jit(solution)/shard_map/ppermute | solution.py:33
  209.3 19.6 %collective-permute-start.36 = (bf16[192,768]{1,0:T(8,128)(2,1)}, bf16[192,768]{1,0:T(8,128)(2,1)}, u32[]{:S(2)}, u32[]{:S(2)}) collective-permute-start(bf16[192,768]{1,0:T(8,128)(2,1)} %get-tuple-element.173), channel_id=1, source_target_pairs={{0,1},{1,0},{2,3},{3,2},{4,5},{5,4},{6,7},{7,6},{8,9},{9,8},{10,11... | collective-permute-start | bytes 884744 | tf_op jit(solution)/shard_map/ppermute | solution.py:33
  210.8 29.1 %collective-permute-start.37 = (bf16[192,768]{1,0:T(8,128)(2,1)}, bf16[192,768]{1,0:T(8,128)(2,1)}, u32[]{:S(2)}, u32[]{:S(2)}) collective-permute-start(bf16[192,768]{1,0:T(8,128)(2,1)} %get-tuple-element.174), channel_id=1, source_target_pairs={{0,2},{1,3},{2,0},{3,1},{4,6},{5,7},{6,4},{7,5},{8,10},{9,11},{10,... | collective-permute-start | bytes 884744 | tf_op jit(solution)/shard_map/ppermute | solution.py:33
  213.8 26.1 %collective-permute-start.38 = (bf16[192,768]{1,0:T(8,128)(2,1)}, bf16[192,768]{1,0:T(8,128)(2,1)}, u32[]{:S(2)}, u32[]{:S(2)}) collective-permute-start(bf16[192,768]{1,0:T(8,128)(2,1)} %get-tuple-element.175), channel_id=1, source_target_pairs={{0,3},{1,2},{2,1},{3,0},{4,7},{5,6},{6,5},{7,4},{8,11},{9,10},{10,... | collective-permute-start | bytes 884744 | tf_op jit(solution)/shard_map/ppermute | solution.py:33
  214.5 70.0 %collective-permute-start.40 = (bf16[208,1536]{1,0:T(8,128)(2,1)}, bf16[208,1536]{1,0:T(8,128)(2,1)S(1)}, u32[]{:S(2)}, u32[]{:S(2)}) collective-permute-start(bf16[208,1536]{1,0:T(8,128)(2,1)} %reduce-scatter.2.cloned.1.call-done.rest_0_), channel_id=1, source_target_pairs={{0,16},{16,0},{1,17},{17,1},{2,18},{18,2},{3,19},{19,3},{4,20},{20... | collective-permute-start | bytes 1916936 | tf_op jit(solution)/shard_map/ppermute | solution.py:33
  228.1 24.6 %collective-permute-start.25 = (bf16[192,640]{1,0:T(8,128)(2,1)S(1)}, bf16[192,640]{1,0:T(8,128)(2,1)S(1)}, u32[]{:S(2)}, u32[]{:S(2)}) collective-permute-start(bf16[192,640]{1,0:T(8,128)(2,1)S(1)} %get-tuple-element.161), channel_id=1, source_target_pairs={{0,0},{4,1},{8,2},{12,3},{2,4},{6,5},{10,6},{14,7},{1,8},{5,9},{9,... | collective-permute-start | bytes 737288 | tf_op jit(solution)/shard_map/ppermute | solution.py:87
  228.9 25.8 %collective-permute-start.26 = (bf16[192,640]{1,0:T(8,128)(2,1)S(1)}, bf16[192,640]{1,0:T(8,128)(2,1)S(1)}, u32[]{:S(2)}, u32[]{:S(2)}) collective-permute-start(bf16[192,640]{1,0:T(8,128)(2,1)S(1)} %get-tuple-element.162), channel_id=1, source_target_pairs={{4,0},{8,1},{12,2},{0,3},{6,4},{10,5},{14,6},{2,7},{5,8},{9,9},{13... | collective-permute-start | bytes 737288 | tf_op jit(solution)/shard_map/ppermute | solution.py:87
  239.9 14.8 %collective-permute-start.27 = (bf16[192,640]{1,0:T(8,128)(2,1)S(1)}, bf16[192,640]{1,0:T(8,128)(2,1)S(1)}, u32[]{:S(2)}, u32[]{:S(2)}) collective-permute-start(bf16[192,640]{1,0:T(8,128)(2,1)S(1)} %get-tuple-element.163), channel_id=1, source_target_pairs={{8,0},{12,1},{0,2},{4,3},{10,4},{14,5},{2,6},{6,7},{9,8},{13,9},{1... | collective-permute-start | bytes 737288 | tf_op jit(solution)/shard_map/ppermute | solution.py:87
  239.9 17.7 %collective-permute-start.28 = (bf16[192,640]{1,0:T(8,128)(2,1)S(1)}, bf16[192,640]{1,0:T(8,128)(2,1)S(1)}, u32[]{:S(2)}, u32[]{:S(2)}) collective-permute-start(bf16[192,640]{1,0:T(8,128)(2,1)S(1)} %get-tuple-element.164), channel_id=1, source_target_pairs={{12,0},{0,1},{4,2},{8,3},{14,4},{2,5},{6,6},{10,7},{13,8},{1,9},{5... | collective-permute-start | bytes 737288 | tf_op jit(solution)/shard_map/ppermute | solution.py:87
  252.7 27.7 %collective-permute-start.39 = (bf16[192,768]{1,0:T(8,128)(2,1)S(1)}, bf16[192,768]{1,0:T(8,128)(2,1)S(1)}, u32[]{:S(2)}, u32[]{:S(2)}) collective-permute-start(bf16[192,768]{1,0:T(8,128)(2,1)S(1)} %block_sum.1.rest_0_), channel_id=1, source_target_pairs={{0,16},{16,0},{1,17},{17,1},{2,18},{18,2},{3,19},{19,3},{4,20},{20... | collective-permute-start | bytes 884744 | tf_op jit(solution)/shard_map/ppermute | solution.py:33
  258.8 5.1 %collective-permute-start.29 = (f32[1,64,192]{2,1,0:T(8,128)S(1)}, f32[1,64,192]{2,1,0:T(8,128)S(1)}, u32[]{:S(2)}, u32[]{:S(2)}) collective-permute-start(f32[1,64,192]{2,1,0:T(8,128)S(1)} %get-tuple-element.167), channel_id=1, source_target_pairs={{0,4},{4,0},{8,12},{12,8},{1,5},{5,1},{9,13},{13,9},{2,6},{6,2},{1... | collective-permute-start | bytes 147464 | tf_op jit(solution)/shard_map/ppermute | solution.py:33
  263.8 7.2 %collective-permute-start.32 = (f32[2,64,192]{2,1,0:T(8,128)S(1)}, f32[2,64,192]{2,1,0:T(8,128)S(1)}, u32[]{:S(2)}, u32[]{:S(2)}) collective-permute-start(f32[2,64,192]{2,1,0:T(8,128)S(1)} %constant_dynamic-update-slice_fusion.rest_4_), channel_id=1, source_target_pairs={{0,24},{4,28},{8,16},{12,20},{16,8},{20,12},{24,0},{28,4},{1,25},{... | collective-permute-start | bytes 294920 | tf_op jit(solution)/shard_map/ppermute | solution.py:936
  263.9 8.9 %collective-permute-start.31 = (f32[2,64,192]{2,1,0:T(8,128)S(1)}, f32[2,64,192]{2,1,0:T(8,128)S(1)}, u32[]{:S(2)}, u32[]{:S(2)}) collective-permute-start(f32[2,64,192]{2,1,0:T(8,128)S(1)} %constant_dynamic-update-slice_fusion.rest_4_), channel_id=1, source_target_pairs={{0,16},{4,20},{8,24},{12,28},{16,0},{20,4},{24,8},{28,12},{1,17},{... | collective-permute-start | bytes 294920 | tf_op jit(solution)/shard_map/ppermute | solution.py:936
  266.1 7.3 %collective-permute-start.30 = (f32[2,64,192]{2,1,0:T(8,128)S(1)}, f32[2,64,192]{2,1,0:T(8,128)S(1)}, u32[]{:S(2)}, u32[]{:S(2)}) collective-permute-start(f32[2,64,192]{2,1,0:T(8,128)S(1)} %constant_dynamic-update-slice_fusion.rest_4_), channel_id=1, source_target_pairs={{0,8},{4,12},{8,0},{12,4},{16,24},{20,28},{24,16},{28,20},{1,9},{5... | collective-permute-start | bytes 294920 | tf_op jit(solution)/shard_map/ppermute | solution.py:936
  276.0 5.9 %collective-permute-start.35 = (f32[64,128]{1,0:T(8,128)S(1)}, f32[64,128]{1,0:T(8,128)S(1)}, u32[]{:S(2)}, u32[]{:S(2)}) collective-permute-start(f32[64,128]{1,0:T(8,128)S(1)} %get-tuple-element.168.rest_2_), channel_id=1, source_target_pairs={{0,3},{1,2},{2,1},{3,0},{4,7},{5,6},{6,5},{7,4},{8,11},{9,10},{10,... | collective-permute-start | bytes 98312 | tf_op jit(solution)/shard_map/ppermute | solution.py:33
  (65 other events, 569.0 us)
Sparse Core Ops, SparseCore 0:
  10.8 62.0 all-gather.2
  79.0 53.5 all-gather.4
  161.5 52.2 reduce-scatter.1

commit v3 on v2

--- a/solution.py
+++ b/solution.py
@@ -20,12 +20,8 @@
 LANES = 64
 GAIN_ONE, GAIN_TWO, DOWN_BIAS = 48, 49, 50
 STATS = 51
-VMEM_SMALL = 12 * 1024 * 1024
-VMEM_LARGE = 56 * 1024 * 1024
-VMEM_LIMIT = {
-    name: VMEM_LARGE
-    for name in ("attend", "feed_first", "feed_grads", "feed_out", "attend_back", "attend_weights")
-}
+VMEM_LIMIT = 56 * 1024 * 1024
+NEAR = {'unbundle': 12, 'modulation_back': 12, 'table_sum': 12, 'attn_weight_out': 12, 'feed_weight_out': 12, 'pair_sum': 12, 'block_sum': 12, 'join': 12, 'finish_forward': 12, 'finish_backward': 12, 'feed_first': 56, 'attend_back_first': 56, 'attend_back_last': 56, 'second_norm': 56, 'middle_grad': 56, 'branch_grad': 56, 'first_norm': 56, 'attend': 40}
 
 
 def swap(values, axis, bit):
@@ -59,6 +55,12 @@
     return [parts[0], near, far], after([far], filled) if hold else filled
 
 
+def scatter_near(parts):
+    near = swap(parts[2], "row", 1)
+    total = (parts[1].astype(FULL) + near[parts[0].shape[0] :].astype(FULL)).astype(LOW)
+    return near, total
+
+
 def col_of_row(row_count):
     if row_count == 4:
         return [0, 2, 1, 3]
@@ -130,16 +132,25 @@
     return pl.BlockSpec(memory_space=memory_space)
 
 
-class Far:
-    def __init__(self, value):
-        self.value = value
+class Joined:
+    def __init__(self, values):
+        self.values = values
 
 
 class FarIn:
-    def __init__(self, source, buffer, sem):
-        self.copy = pltpu.make_async_copy(source, buffer, sem)
+    def __init__(self, sources, buffer, sems):
         self.buffer, self.waiting = buffer, True
-        self.copy.start()
+        if len(sources) == 1:
+            places = [buffer]
+        else:
+            count = sources[0].shape[1]
+            places = [buffer.at[:, i * count : (i + 1) * count] for i in range(len(sources))]
+        self.copies = [
+            pltpu.make_async_copy(source, place, sem)
+            for source, place, sem in zip(sources, places, sems)
+        ]
+        for copy in self.copies:
+            copy.start()
 
     @property
     def shape(self):
@@ -148,7 +159,8 @@
     @property
     def ref(self):
         if self.waiting:
-            self.copy.wait()
+            for copy in self.copies:
+                copy.wait()
             self.waiting = False
         return self.buffer
 
@@ -192,55 +204,62 @@
 
 
 def run(body, name, outs, args, scratch=(), smem=0, flops=0):
-    far_args = [isinstance(a, Far) for a in args]
-    far_outs = [isinstance(o, Far) for o in outs]
-    args = [a.value if isinstance(a, Far) else a for a in args]
-    outs = [o.value if isinstance(o, Far) else o for o in outs]
-    buffers = [pltpu.VMEM(a.shape, a.dtype) for a, far in zip(args + outs, far_args + far_outs) if far]
-    moved = sum(a.size * a.dtype.itemsize for a in args + outs)
+    if name in NEAR:
+        moved = sum(a.size * a.dtype.itemsize for a in list(args) + list(outs))
+        found = pl.pallas_call(
+            body,
+            out_shape=list(outs),
+            in_specs=[whole(pltpu.SMEM)] * smem + [whole() for _ in args[smem:]],
+            out_specs=[whole() for _ in outs],
+            scratch_shapes=list(scratch),
+            compiler_params=pltpu.CompilerParams(vmem_limit_bytes=NEAR[name] * 1024 * 1024),
+            cost_estimate=pl.CostEstimate(flops=flops, bytes_accessed=moved, transcendentals=0),
+            name=name,
+        )(*args)
+        return list(found)
+    groups = [a.values if isinstance(a, Joined) else [a] for a in args[smem:]]
+    flat = [a for group in groups for a in group]
+    outs = list(outs)
+    buffers = [
+        pltpu.VMEM((*group[0].shape[:-1], sum(a.shape[-1] for a in group)), group[0].dtype)
+        for group in groups
+    ] + [pltpu.VMEM(o.shape, o.dtype) for o in outs]
+    moved = sum(a.size * a.dtype.itemsize for a in flat + outs)
 
     def kernel(*refs):
-        ins, rest = list(refs[: len(args)]), refs[len(args) :]
-        results, rest = list(rest[: len(outs)]), rest[len(outs) :]
-        own, rest = rest[: len(scratch)], list(rest[len(scratch) :])
-        count = 0
-        for i, far in enumerate(far_args):
-            if far:
-                ins[i] = FarIn(ins[i], rest[count], rest[-1].at[count])
-                count += 1
-        for i, far in enumerate(far_outs):
-            if far:
-                results[i] = FarOut(rest[count], results[i], rest[-1].at[count])
-                count += 1
-        body(*ins, *results, *own)
+        scalars, rest = list(refs[:smem]), list(refs[smem:])
+        sources, rest = rest[: len(flat)], rest[len(flat) :]
+        targets, rest = rest[: len(outs)], rest[len(outs) :]
+        own, rest = rest[: len(scratch)], rest[len(scratch) :]
+        spaces, sems = rest[:-1], rest[-1]
+        ins, count = [], 0
+        for group, space in zip(groups, spaces):
+            span = range(count, count + len(group))
+            ins.append(FarIn([sources[i] for i in span], space, [sems.at[i] for i in span]))
+            count += len(group)
+        results = [
+            FarOut(space, target, sems.at[count + i])
+            for i, (space, target) in enumerate(zip(spaces[len(groups) :], targets))
+        ]
+        body(*scalars, *ins, *results, *own)
+        ship(*results)
+        for ref in ins:
+            ref.ref
         for ref in results:
-            ship(ref)
-        for ref in ins:
-            if isinstance(ref, FarIn):
-                ref.ref
-        for ref in results:
-            if isinstance(ref, FarOut):
-                ref.copy.wait()
-
-    def spec(far):
-        return whole(pl.ANY) if far else whole()
+            ref.copy.wait()
 
     found = pl.pallas_call(
-        kernel if buffers else body,
+        kernel,
         out_shape=outs,
-        in_specs=[whole(pltpu.SMEM)] * smem + [spec(far) for far in far_args[smem:]],
-        out_specs=[spec(far) for far in far_outs],
+        in_specs=[whole(pltpu.SMEM)] * smem + [whole(pl.ANY) for _ in flat],
+        out_specs=[whole(pl.ANY) for _ in outs],
         scratch_shapes=list(scratch) + buffers
-        + ([pltpu.SemaphoreType.DMA((len(buffers),))] if buffers else []),
-        compiler_params=pltpu.CompilerParams(vmem_limit_bytes=VMEM_LIMIT.get(name, VMEM_SMALL)),
+        + [pltpu.SemaphoreType.DMA((len(flat) + len(outs),))],
+        compiler_params=pltpu.CompilerParams(vmem_limit_bytes=VMEM_LIMIT),
         cost_estimate=pl.CostEstimate(flops=flops, bytes_accessed=moved, transcendentals=0),
         name=name,
-    )(*args)
+    )(*args[:smem], *flat)
     return list(found)
-
-
-def far_all(values):
-    return [Far(v) for v in values]
 
 
 def shape(dims, dtype):
@@ -268,12 +287,11 @@
 
 
 def token_mods_of(mods, segs):
-    terms = jnp.concatenate(split(mods, 2), 1).astype(LOW)
     rows = lax.broadcasted_iota(jnp.int32, (2 * LANES, segs.shape[1]), 0) % LANES
 
     def pick(k):
         chosen = (rows == segs + k * SLOTS).astype(LOW)
-        return dot(terms, chosen, (1, 0))
+        return dot(mods, chosen, (1, 0))
 
     return pick
 
@@ -294,6 +312,10 @@
     return (
         part[...].astype(FULL) + near[: part.shape[0], :].astype(FULL) + far[...].astype(FULL)
     )
+
+
+def column_of(mods, lane):
+    return mods[:, lane : lane + 1].astype(FULL) + mods[:, LANES + lane : LANES + lane + 1].astype(FULL)
 
 
 def normalize(stream):
@@ -314,7 +336,7 @@
 def prepare(grid, slot_count, times, table, weight, bias, gain_one, gain_two, down_bias, tokens, cot, *rest):
     outs, (embed, rows, blocks) = rest[: grid.cols], rest[grid.cols :]
     own = (outs[0].shape[1] - 2 * LANES) // 2
-    rows[...] = jnp.zeros_like(rows)
+    rows[...] = jnp.zeros(rows.shape, FULL)
     for k in range(6):
         rows[k * SLOTS : (k + 1) * SLOTS, :] = jnp.broadcast_to(
             bias[k : k + 1, :].astype(FULL), (SLOTS, rows.shape[1])
@@ -329,7 +351,7 @@
     lane = lax.broadcasted_iota(jnp.int32, (LANES, 6 * cond), 1)
     match = row // SLOTS == lane // cond
     for j in range(grid.per_row):
-        embed[...] = jnp.zeros_like(embed)
+        embed[...] = jnp.zeros(embed.shape, FULL)
         for slot in range(slot_count):
             time = times[grid.row() * grid.per_row + j, slot]
             embed[slot : slot + 1, :] = table[pl.ds(time, 1), :]
@@ -347,17 +369,21 @@
 
 
 def unbundle(grid, *rest):
-    bundles, (grad_out, result_out, small_out) = rest[: grid.cols], rest[grid.cols :]
-    size = grad_out.shape[0]
+    bundles, (grad_out, small_out) = rest[: grid.cols], rest[grid.cols :]
     own = grad_out.shape[1] // grid.cols
-    small_out[...] = jnp.zeros_like(small_out)
+    small_out[...] = jnp.zeros(small_out.shape, FULL)
     for step in range(grid.cols):
         place = grid.place(step)
-        span = pl.ds(block_start(place, own), own)
-        grad_out[:, span] = bundles[step][:size, :own]
-        result_out[:, span] = bundles[step][:size, own : 2 * own]
-        terms = bundles[step][:, 2 * own :].astype(FULL)
+        grad_out[:, pl.ds(block_start(place, own), own)] = bundles[step][:, :own]
+        terms = bundles[step][:, own:].astype(FULL)
         small_out[place // grid.rows] += (terms[:, :LANES] + terms[:, LANES:]).T
+
+
+def join(grid, *rest):
+    pieces, out = rest[: grid.cols], rest[-1]
+    own = pieces[0].shape[1]
+    for step in range(grid.cols):
+        out[:, pl.ds(block_start(grid.place(step), own), own)] = pieces[step][...]
 
 
 def pack(qkv, proj, attn_out):
@@ -407,13 +433,12 @@
         place = pl.ds(block_start(grid.source(step), size), size)
         stream_out[place, :] = bundles[step][:, :own]
         cot_out[place, :] = bundles[step][:, own : 2 * own]
-        terms = bundles[step][:, 2 * own :].astype(FULL)
-        mods_out[place, :] = terms[:, :LANES] + terms[:, LANES:]
+        mods_out[place, :] = bundles[step][:, 2 * own :]
     stream = stream_out[...].astype(FULL)
     mods = mods_out[...]
     pick = token_mods_of(mods, segs[...])
     normed, _ = normalize(stream)
-    scaled = normed * mods[:, GAIN_ONE : GAIN_ONE + 1]
+    scaled = normed * column_of(mods, GAIN_ONE)
     input_out[...] = (scaled * (1.0 + pick(1)) + pick(0)).astype(LOW)
 
 
@@ -422,9 +447,9 @@
     branch_out[...] = (cot[...].astype(FULL) * pick(5)).astype(LOW)
 
 
-def attend(segs_row, segs_col, cosine, sine, weight_all, *rest):
-    pieces, outs = rest[:4], rest[4:]
-    parts, (query, key, value, mixed, logsum, inputs_all, key_rows) = outs[:3], outs[3:]
+def attend(weight_all, cosine, sine, *rest):
+    pieces, (segs_row, segs_col), outs = rest[:4], rest[4:6], rest[6:]
+    parts, (query, key, value, mixed, logsum, key_rows) = outs[:3], outs[3:]
     own = pieces[0].shape[1]
     head_width = query.shape[0]
     weight, proj = weight_all[:, : 3 * head_width], weight_all[:, 3 * head_width :]
@@ -433,8 +458,7 @@
     for e in range(4):
         span = slice(e * own, (e + 1) * own)
         cos, sin = cosine[:, span], sine[:, span]
-        inputs_all[:, span] = pieces[e][...]
-        found = dot(weight, inputs_all[:, span], (0, 0))
+        found = dot(weight, pieces[e][...], (0, 0))
         for h in range(head_width // HEAD_DIM):
             for out, base, factor in ((query, 0, scale), (key, head_width, 1.0)):
                 at = h * HEAD_DIM
@@ -443,7 +467,7 @@
                 out[at : at + half, span] = ((one * cos - two * sin) * factor).astype(LOW)
                 out[at + half : at + HEAD_DIM, span] = ((two * cos + one * sin) * factor).astype(LOW)
         value[:, span] = found[2 * head_width :].astype(LOW)
-    ship(query, key, value, inputs_all)
+    ship(query, key, value)
     key_segs = jnp.where(segs_col[...] == 0, -1, segs_col[...])
     for h in range(head_width // HEAD_DIM):
         rows = slice(h * HEAD_DIM, (h + 1) * HEAD_DIM)
@@ -474,7 +498,7 @@
     middle = stream[...].astype(FULL) + pick(2) * attn
     middle_out[...] = middle
     normed, _ = normalize(middle)
-    scaled = normed * mods[:, GAIN_TWO : GAIN_TWO + 1]
+    scaled = normed * column_of(mods, GAIN_TWO)
     input_out[...] = (scaled * (1.0 + pick(4)) + pick(3)).astype(LOW)
 
 
@@ -482,31 +506,36 @@
 GELU_CUBE = 0.044715
 
 
+FEED_ORDER = (0, 1, 2, 3)
+
+
 def feed_first(weights, up_bias, *rest):
-    pieces, branches, outs = rest[:4], rest[4:8], rest[8:]
-    parts, (hidden, pre_grad, inputs_all, branch_all) = outs[:3], outs[3:]
-    own = pieces[0].shape[1]
-    count = hidden.shape[0]
+    sides, outs = rest[:8], rest[8:]
+    parts, results, hidden, pre_grad = outs[:3], outs[3:6], outs[6:10], outs[10:14]
+    count = hidden[0].shape[0]
     up, down = weights[:, :count], weights[:, count:]
     bias = jnp.broadcast_to(up_bias[...].astype(FULL)[None], (8, count)).T[:, :1]
-    for e in (3, 1, 2, 0):
-        span = slice(e * own, (e + 1) * own)
-        inputs_all[:, span] = pieces[e][...]
-        branch_all[:, span] = branches[e][...]
-        pre = dot(up, pieces[e][...], (0, 0)) + bias
+    for i, e in enumerate(FEED_ORDER):
+        piece, branch = sides[2 * i], sides[2 * i + 1]
+        pre = dot(up, piece[...], (0, 0)) + bias
         square = pre * pre
         curve = jnp.tanh(GELU_SCALE * (pre + GELU_CUBE * square * pre))
-        hidden[:, span] = (0.5 * pre * (1.0 + curve)).astype(LOW)
+        hidden[e][...] = (0.5 * pre * (1.0 + curve)).astype(LOW)
         slope = 0.5 * (1.0 + curve) + 0.5 * pre * (1.0 - curve * curve) * (
             GELU_SCALE * (1.0 + 3.0 * GELU_CUBE * square)
         )
-        grad = dot(down, branches[e][...], (0, 0))
-        pre_grad[:, span] = (grad * slope).astype(LOW)
-        part_of(parts, e)[...] = dot(up, pre_grad[:, span], (1, 0)).astype(LOW)
-        ship_part(parts, e)
-
-
-def feed_grads_of(hidden, pre_grad, inputs_all, branch_all, grads):
+        grad = dot(down, branch[...], (0, 0))
+        pre_grad[e][...] = (grad * slope).astype(LOW)
+        ship(hidden[e], pre_grad[e])
+        part_of(parts, e)[...] = dot(up, pre_grad[e][...], (1, 0)).astype(LOW)
+        part_of(results, e)[...] = dot(down, hidden[e][...], (1, 0)).astype(LOW)
+        if e == 3:
+            ship(parts[2], results[2])
+        elif e != 1:
+            ship(parts[e // 2], results[e // 2])
+
+
+def feed_grads_of(pre_grad, inputs_all, hidden, branch_all, grads):
     count = hidden.shape[0]
     blocks = grads.shape[0]
     size = inputs_all.shape[0] // blocks
@@ -523,22 +552,12 @@
         grads[j, :size, count:] = down_total[j * size : (j + 1) * size]
 
 
-def feed_out(weights, hidden, *parts):
-    count = hidden.shape[0]
-    own = parts[0].shape[1]
-    for e in (3, 1, 2, 0):
-        part_of(parts, e)[...] = dot(
-            weights[:, count:], hidden[:, e * own : (e + 1) * own], (1, 0)
-        ).astype(LOW)
-        ship_part(parts, e)
-
-
 def middle_grad(segs, mods, middle, cot, part, near, far, grad_out, attn_grad_out, input_grad_out):
     pick = token_mods_of(mods[...], segs[...])
     input_grad = three_terms(part, near, far)
     input_grad_out[...] = input_grad.astype(LOW)
     normed, inverse = normalize(middle[...])
-    grad_scaled = input_grad * (1.0 + pick(4)) * mods[:, GAIN_TWO : GAIN_TWO + 1]
+    grad_scaled = input_grad * (1.0 + pick(4)) * column_of(mods, GAIN_TWO)
     grad = cot[...].astype(FULL) + normalize_back(grad_scaled, normed, inverse)
     grad_out[...] = grad
     attn_grad_out[...] = (grad * pick(2)).astype(LOW)
@@ -553,20 +572,24 @@
     return (lax.broadcasted_iota(jnp.int32, (16, segs.shape[1]), 0) == segs).astype(LOW)
 
 
-def finish_forward(segs, mods, middle, cot, attn, grad_middle, input_grad, part, near, far, result_out, small):
+def finish_forward(grid, segs, mods, middle, cot, attn, grad_middle, input_grad, part, near, far, *rest):
+    outs, (small, result_low) = rest[: grid.cols], rest[grid.cols :]
     pick = token_mods_of(mods[...], segs[...])
     chosen = slot_rows(segs[...])
     ones = jnp.ones(chosen.shape, LOW)
     valid = (segs[...] != 0).astype(FULL)
     mlp = (
         three_terms(part, near, far)
-        + mods[:, DOWN_BIAS : DOWN_BIAS + 1]
+        + column_of(mods, DOWN_BIAS)
     )
     gate = pick(5)
     mlp_term = gate * mlp
     result = middle[...] + mlp_term
-    result_out[...] = result.astype(LOW)
-    small[...] = jnp.zeros_like(small)
+    result_low[...] = result.astype(LOW)
+    size = outs[0].shape[0]
+    for step in range(grid.cols):
+        outs[step][...] = result_low[pl.ds(block_start(grid.source(step), size), size), :]
+    small[...] = jnp.zeros(small.shape, FULL)
     cot_full = cot[...].astype(FULL)
     attn_all = attn[...].astype(FULL)
     input_all = input_grad[...].astype(FULL)
@@ -575,7 +598,7 @@
     terms = (
         (2, grad_middle[...] * attn_all),
         (3, input_all),
-        (4, along * mods[:, GAIN_TWO : GAIN_TWO + 1]),
+        (4, along * column_of(mods, GAIN_TWO)),
         (5, cot_full * mlp),
     )
     for k, values in terms:
@@ -596,10 +619,15 @@
     small[STATS : STATS + 1, :] = total
 
 
-def attend_back(segs_row, segs_col, cosine, sine, weight_all, query, key, value, mixed, logsum, *rest):
-    pieces, outs = rest[:4], rest[4:]
-    parts, (grads, pieces_all, key_rows, value_rows, out_grad, key_grad, value_grad) = outs[:3], outs[3:]
-    own = pieces[0].shape[1]
+def attend_back(pieces_of, key, value, weight_all, first, query, mixed, logsum, segs_row, segs_col, cosine, sine, *rest):
+    last = pieces_of[0] != 0
+    if last:
+        second, key_in, value_in, query_in, rest = rest[0], rest[1], rest[2], rest[3], rest[4:]
+        parts, (grads, key_rows, value_rows, out_grad, key_grad, value_grad) = rest[:3], rest[3:]
+    else:
+        second, (grads, key_grad, value_grad, key_rows, value_rows, out_grad) = rest[0], rest[1:]
+    pieces = dict(zip(pieces_of, (first, second)))
+    own = first.shape[1]
     head_width = query.shape[0]
     heads = head_width // HEAD_DIM
     weight, proj = weight_all[:, : 3 * head_width], weight_all[:, 3 * head_width :]
@@ -610,8 +638,13 @@
         key_rows[h] = key[rows, :].astype(FULL).T.astype(LOW)
         value_rows[h] = value[rows, :].astype(FULL).T.astype(LOW)
     key_segs = jnp.where(segs_col[...] == 0, -1, segs_col[...])
-    key_grad[...] = jnp.zeros_like(key_grad)
-    value_grad[...] = jnp.zeros_like(value_grad)
+    if last:
+        grads[:head_width, : 2 * own] = query_in[...]
+        key_grad[...] = key_in[...]
+        value_grad[...] = value_in[...]
+    else:
+        key_grad[...] = jnp.zeros(key_grad.shape, FULL)
+        value_grad[...] = jnp.zeros(value_grad.shape, FULL)
 
     def turn_back(grad, span, base, at):
         cos, sin = cosine[:, span], sine[:, span]
@@ -619,10 +652,9 @@
         grads[base + at : base + at + half, span] = (one * cos + two * sin).astype(LOW)
         grads[base + at + half : base + at + HEAD_DIM, span] = (two * cos - one * sin).astype(LOW)
 
-    for e in range(4):
+    for e in pieces_of:
         span = slice(e * own, (e + 1) * own)
         allowed = key_segs == segs_row[:, span]
-        pieces_all[:, span] = pieces[e][...]
         out_grad[...] = dot(proj, pieces[e][...], (0, 0)).astype(LOW)
         for h in range(heads):
             rows = slice(h * HEAD_DIM, (h + 1) * HEAD_DIM)
@@ -638,7 +670,8 @@
             value_grad[rows, :] += dot(back, probability.astype(LOW), (1, 1))
             key_grad[rows, :] += dot(query[rows, span], score_grad, (1, 1))
             turn_back(dot(key[rows, :], score_grad, (1, 0)) * scale, span, 0, h * HEAD_DIM)
-    ship(pieces_all)
+    if not last:
+        return
     for e in (3, 1, 2, 0):
         span = slice(e * own, (e + 1) * own)
         for h in range(heads):
@@ -648,14 +681,21 @@
         ship_part(parts, e)
 
 
-def attend_weights(grid, grads, mixed, inputs_all, pieces_all, *rest):
-    blocks, total = rest[: grid.cols], rest[grid.cols]
+def attend_weights(grid, grads, mixed, inputs_all, pieces_all, keep, send, total):
     count = grads.shape[0]
     total[:, :count] = dot(inputs_all[...], grads[...], (1, 1)).astype(LOW)
     total[:, count:] = dot(pieces_all[...], mixed[...], (1, 1)).astype(LOW)
-    size = blocks[0].shape[0]
+    size = keep.shape[1]
     for j in range(grid.cols):
-        blocks[j][...] = total[pl.ds(block_start(grid.col() ^ j, size), size), :]
+        send[j] = total[pl.ds(grid.half_start(grid.col() ^ j, 1 - grid.half(), size), size), :]
+    ship(send)
+    for j in range(grid.cols):
+        keep[j] = total[pl.ds(grid.half_start(grid.col() ^ j, grid.half(), size), size), :]
+
+
+def pair_sum(keep, got, *outs):
+    for j, out in enumerate(outs):
+        out[...] = (keep[j].astype(FULL) + got[j].astype(FULL)).astype(LOW)
 
 
 def block_sum(*rest):
@@ -665,15 +705,14 @@
     rest[-1][...] = total.astype(LOW)
 
 
-def attn_weight_out(*rest):
-    parts, (qkv_out, proj_out) = rest[:-2], rest[-2:]
-    total = parts[0][...].astype(FULL)
-    for part in parts[1:]:
-        total = total + part[...].astype(FULL)
+def attn_weight_out(grid, own, other, qkv_out, proj_out, total):
+    size = own.shape[0]
+    total[pl.ds(grid.half_start(0, grid.half(), size), size), :] = own[...]
+    total[pl.ds(grid.half_start(0, 1 - grid.half(), size), size), :] = other[...]
     width = qkv_out.shape[2]
     for i in range(3):
-        qkv_out[i] = total[:, i * width : (i + 1) * width]
-    proj_out[...] = total[:, 3 * width :].T
+        qkv_out[i] = total[:, i * width : (i + 1) * width].astype(FULL)
+    proj_out[...] = total[:, 3 * width :].astype(FULL).T
 
 
 def feed_weight_out(*rest):
@@ -687,14 +726,14 @@
     bias_out[...] = total[size, :count]
 
 
-def finish_backward(grid, segs, mods, stream, grad_middle, result, small_in, part, near, far, *rest):
+def finish_backward(grid, segs, mods, stream, grad_middle, small_in, part, near, far, *rest):
     outs, (grad_low, blocks) = rest[: grid.cols], rest[grid.cols :]
     pick = token_mods_of(mods[...], segs[...])
     chosen = slot_rows(segs[...])
     ones = jnp.ones(chosen.shape, LOW)
     input_grad = three_terms(part, near, far)
     normed, inverse = normalize(stream[...].astype(FULL))
-    gain = mods[:, GAIN_ONE : GAIN_ONE + 1]
+    gain = column_of(mods, GAIN_ONE)
     grown = input_grad * (1.0 + pick(1))
     grad = grad_middle[...] + normalize_back(grown * gain, normed, inverse)
     grad_low[...] = grad.astype(LOW)
@@ -702,8 +741,7 @@
     own = grad.shape[1]
     for step in range(grid.cols):
         place = pl.ds(block_start(grid.source(step), size), size)
-        outs[step][:size, :own] = grad_low[place, :]
-        outs[step][:size, own : 2 * own] = result[place, :]
+        outs[step][:, :own] = grad_low[place, :]
     shift = doc_sums(input_grad, chosen)[:SLOTS]
     scale = doc_sums(input_grad * normed * gain, chosen)[:SLOTS]
     norm_gain = doc_sums(grown * normed, ones)[:1]
@@ -716,7 +754,7 @@
         blocks[c, STATS : STATS + 1, :size] = small_in[STATS : STATS + 1, :size]
     for step in range(grid.cols):
         terms = split(blocks[grid.source(step)].T, 2)
-        outs[step][:, 2 * own :] = jnp.concatenate(terms, 1).astype(LOW)
+        outs[step][:, own:] = jnp.concatenate(terms, 1).astype(LOW)
 
 
 def modulation_back(grid, slot_count, dp_count, *rest):
@@ -725,7 +763,7 @@
     weight_out, bias_out, gain_one_out, gain_two_out, down_bias_out, stats_out, embed_out = outs[:7]
     embed, grads = outs[7:]
     per = grid.per_row
-    embed[...] = jnp.zeros_like(embed)
+    embed[...] = jnp.zeros(embed.shape, FULL)
     size = grads.shape[2]
     total = jnp.zeros((LANES - 6 * SLOTS, size), FULL)
     for d in range(dp_count):
@@ -759,7 +797,7 @@
     for part in parts[1:]:
         found = found + part[...]
     total[...] = found
-    table_out[...] = jnp.zeros_like(table_out)
+    table_out[...] = jnp.zeros(table_out.shape, FULL)
     for d in range(dp_count):
         for sequence in range(grid.cols):
             for slot in range(slot_count):
@@ -833,12 +871,12 @@
     )
     input_one, stream, cot, mods = run(
         functools.partial(first_norm, grid), "first_norm",
-        [low_tile] + far_all([low_tile] * 2) + [shape((width, LANES), FULL)], [segs_own] + bundles,
+        [low_tile] * 3 + [shape((width, 2 * LANES), LOW)], [segs_own] + bundles,
     )
 
     def branch_filler(ready):
         [late] = after([ready], [cot])
-        return run(branch_grad, "branch_grad", [low_tile], [segs_own, mods, Far(late)])
+        return run(branch_grad, "branch_grad", [low_tile], [segs_own, mods, late])
 
     rows_one, [branch] = gather_rows(input_one, branch_filler)
     branch_rows = gather_rows(branch)
@@ -846,31 +884,31 @@
     rows_one[3:] = after([branch_rows[1]] + times[1:], rows_one[3:])
 
     feed_weights = gather_weight(after(rows_one[2:3] + [attn_weights], [up_weight, down_weight]))
-    *parts, query, key, value, mixed, logsum, inputs_one = run(
+    *parts, query, key, value, mixed, logsum = run(
         attend, "attend",
-        far_all(part_tiles + [shape((head_width, SEQ), LOW)] * 4) + [shape((8, SEQ), FULL)]
-        + [Far(shape((width, SEQ), LOW))],
-        [segs_row] + far_all([segs_col, cosine, sine, attn_weights] + rows_one),
+        part_tiles + [shape((head_width, SEQ), LOW)] * 4 + [shape((8, SEQ), FULL)],
+        [attn_weights, cosine, sine] + rows_one + [segs_row, segs_col],
         [pltpu.VMEM((head_width // HEAD_DIM, SEQ, HEAD_DIM), LOW)],
     )
     attn_terms = scatter_rows(parts)
     input_two, middle, attn = run(
-        second_norm, "second_norm", [low_tile] + far_all([full_tile, low_tile]),
-        [segs_own, mods, Far(stream), Far(attn_terms[0])] + attn_terms[1:],
+        second_norm, "second_norm", [low_tile, full_tile, low_tile],
+        [segs_own, mods, stream] + attn_terms,
     )
     rows_two = gather_rows(input_two)
-    hidden_tile = shape((hidden_local, SEQ), LOW)
-    *parts, hidden, pre_grad, inputs_two, branch_all = run(
-        feed_first, "feed_first",
-        far_all(part_tiles + [hidden_tile] * 2 + [shape((width, SEQ), LOW)] * 2),
-        [Far(feed_weights), up_bias] + far_all(rows_two + branch_rows),
-    )
+    hidden_tile = shape((hidden_local, own), LOW)
+    sides = [side for e in FEED_ORDER for side in (rows_two[e], branch_rows[e])]
+    found = run(
+        feed_first, "feed_first", part_tiles * 2 + [hidden_tile] * 8, [feed_weights, up_bias] + sides
+    )
+    parts, results, hidden, pre_grad = found[:3], found[3:6], found[6:10], found[10:]
+
     def grads_filler(ready):
-        [late] = after([ready], [hidden])
+        late = after([ready], pre_grad)
         return run(
             feed_grads_of, "feed_grads",
-            [Far(shape((grid.cols, width_local + 16, 2 * hidden_local), LOW))],
-            far_all([late, pre_grad, inputs_two, branch_all]),
+            [shape((grid.cols, width_local + 16, 2 * hidden_local), LOW)],
+            [Joined(late), Joined(rows_two), Joined(hidden), Joined(branch_rows)],
         )
 
     input_terms, [feed_grads] = scatter_rows(parts, grads_filler, True)
@@ -878,53 +916,69 @@
         feed_grads.reshape(-1, 2 * hidden_local), "col", scatter_dimension=0, tiled=True
     )
     grad_middle, grad_attn, input_grad = run(
-        middle_grad, "middle_grad", [Far(full_tile), low_tile, Far(low_tile)],
-        [segs_own, mods, Far(middle), Far(cot), Far(input_terms[0])] + input_terms[1:],
-    )
-
-    def feed_filler(ready):
-        [late] = after([ready], [hidden])
-        return run(feed_out, "feed_out", far_all(part_tiles), far_all([feed_weights, late]))
-
-    attn_rows, parts = gather_rows(grad_attn, feed_filler)
-    mlp_terms = scatter_rows(parts)
-    *parts, qkv_grads, attn_all = run(
-        attend_back, "attend_back",
-        far_all(part_tiles + [shape((3 * head_width, SEQ), LOW), shape((width, SEQ), LOW)]),
-        [segs_row] + far_all([segs_col, cosine, sine, attn_weights, query, key, value, mixed])
-        + [logsum] + far_all(attn_rows),
-        [pltpu.VMEM((head_width // HEAD_DIM, SEQ, HEAD_DIM), LOW)] * 2
-        + [pltpu.VMEM((head_width, own), LOW)] + [pltpu.VMEM((head_width, SEQ), FULL)] * 2,
+        middle_grad, "middle_grad", [full_tile, low_tile, low_tile],
+        [segs_own, mods, middle, cot] + input_terms,
+    )
+
+    mlp_near, mlp_total = scatter_near(results)
+    head_tile = shape((head_width, SEQ), FULL)
+    back_scratch = [pltpu.VMEM((head_width // HEAD_DIM, SEQ, HEAD_DIM), LOW)] * 2 + [
+        pltpu.VMEM((head_width, own), LOW)
+    ]
+    saved = [query, mixed, logsum, segs_row, segs_col, cosine, sine]
+
+    def first_filler(ready):
+        return run(
+            functools.partial(attend_back, (0, 1)), "attend_back_first",
+            [shape((head_width, 2 * own), LOW), head_tile, head_tile],
+            [key, value, attn_weights, grad_attn] + saved + [ready], back_scratch,
+        )
+
+    attn_rows, (query_grad, key_grad, value_grad) = gather_rows(grad_attn, first_filler)
+    [mlp_total] = after(attn_rows[2:3], [mlp_total])
+    mlp_terms = [results[0], mlp_near, swap(mlp_total, "row", 2)]
+    *parts, qkv_grads = run(
+        functools.partial(attend_back, (2, 3)), "attend_back_last",
+        part_tiles + [shape((3 * head_width, SEQ), LOW)],
+        [key, value, attn_weights, attn_rows[2]] + saved
+        + [attn_rows[3], key_grad, value_grad, query_grad],
+        back_scratch + [pltpu.VMEM((head_width, SEQ), FULL)] * 2,
     )
 
     def back_filler(ready):
         [late] = after([ready], [qkv_grads])
         blocks = run(
             functools.partial(attend_weights, grid), "attend_weights",
-            far_all([shape((width_local, 4 * head_width), LOW)] * grid.cols),
-            far_all([late, mixed, inputs_one, attn_all]), [pltpu.VMEM((width, 4 * head_width), LOW)],
+            [shape((grid.cols, width_local // 2, 4 * head_width), LOW)] * 2,
+            [late, mixed, Joined(rows_one), Joined(attn_rows)], [pltpu.VMEM((width, 4 * head_width), LOW)],
         )
         [first] = after(blocks[:1], mlp_terms[:1])
         found = run(
-            finish_forward, "finish_forward", [low_tile, shape((LANES, width), FULL)],
-            [segs_own, mods] + far_all([middle, cot, attn, grad_middle, input_grad, first])
-            + mlp_terms[1:],
+            functools.partial(finish_forward, grid), "finish_forward",
+            [low_piece] * grid.cols + [shape((LANES, width), FULL)],
+            [segs_own, mods, middle, cot, attn, grad_middle, input_grad, first] + mlp_terms[1:],
+            [pltpu.VMEM((width, own), LOW)],
         )
         return found + blocks
 
-    back_terms, (result, small, *attn_grads) = scatter_rows(parts, back_filler)
-    wide = width_local
+    parts[2:] = after(mlp_terms[2:], parts[2:])
+    back_terms, found = scatter_rows(parts, back_filler)
+    result_chunks, small, attn_grads = found[: grid.cols], found[grid.cols], found[grid.cols + 1 :]
     bundles = run(
         functools.partial(finish_backward, grid), "finish_backward",
-        [shape((wide, 2 * own + 2 * LANES), LOW)] * grid.cols,
-        [segs_own, mods, Far(stream), Far(grad_middle), result, small, Far(back_terms[0])]
-        + back_terms[1:],
-        [pltpu.VMEM((width, own), LOW), pltpu.VMEM((grid.cols, LANES, wide), FULL)],
+        [shape((width_local, own + 2 * LANES), LOW)] * grid.cols,
+        [segs_own, mods, stream, grad_middle, small] + back_terms,
+        [pltpu.VMEM((width, own), LOW), pltpu.VMEM((grid.cols, LANES, width_local), FULL)],
     )
     out_tile = shape((width_local, grid.cols * own), LOW)
-    tokens_grad, block_output, small = run(
+    bundles = relayout(bundles, back=True)
+    tokens_grad, small = run(
         functools.partial(unbundle, grid), "unbundle",
-        [out_tile, out_tile, shape((grid.per_row, LANES, wide), FULL)], relayout(bundles, back=True),
+        [out_tile, shape((grid.per_row, LANES, width_local), FULL)], bundles,
+    )
+    [block_output] = run(
+        functools.partial(join, grid), "join", [out_tile],
+        relayout(after(bundles, result_chunks), back=True),
     )
 
     small = jnp.concatenate([small, swap(small, "row", 1)], 0)
@@ -958,19 +1012,23 @@
     def all_dp(part):
         return [part] + [swap(part, "dp", d) for d in range(1, dp_count)]
 
-    attn_grads = attn_grads[:1] + [swap(attn_grads[j], "col", j) for j in range(1, grid.cols)]
-    [attn_sum] = run(
-        block_sum, "block_sum", [shape((width_local, 4 * head_width), LOW)], attn_grads
-    )
+    half_tile = shape((width_local // 2, 4 * head_width), LOW)
+    pieces = run(pair_sum, "pair_sum", [half_tile] * grid.cols, [attn_grads[0], swap(attn_grads[1], "dp", 1)])
+    pieces = pieces[:1] + [swap(pieces[j], "col", j) for j in range(1, grid.cols)]
+    [attn_half] = run(block_sum, "block_sum", [half_tile], pieces)
+    bit = 2
+    while bit < dp_count:
+        attn_half = (attn_half.astype(FULL) + swap(attn_half, "dp", bit).astype(FULL)).astype(LOW)
+        bit *= 2
     up_out, up_bias_out, down_out = run(
         feed_weight_out, "feed_weight_out",
         [shape(up_weight.shape, FULL), shape(up_bias.shape, FULL), shape(down_weight.shape, FULL)],
         all_dp(feed_grads),
     )
     qkv_out, proj_out = run(
-        attn_weight_out, "attn_weight_out",
+        functools.partial(attn_weight_out, grid), "attn_weight_out",
         [shape((3, width_local, head_width), FULL), shape(proj_weight.shape, FULL)],
-        all_dp(attn_sum),
+        [attn_half, swap(attn_half, "dp", 1)], [pltpu.VMEM((width_local, 4 * head_width), LOW)],
     )
     return (
         block_output,

time: 296 us -> 277 us (0.936)
  local copies, waits for them, and re-layouts: 24.2 us -> 9.45 us
  waiting for transfers between devices: 102 us -> 98.5 us
    unnamed x107, local copies, waits for them, and re-layouts: 23.5 us -> 7.24 us
    ppermute x3, waiting for transfers between devices: 5.86 us -> 0.01 us  [per_device(): lax.ppermute(small, ('dp', 'row'), pairs)]
    ppermute x30 -> x31, starting transfers between devices: 24.8 us -> 29.6 us  [swap(): return lax.ppermute(values, axis, [(i, i ^ bit) for i in range(count)])]
    reduce_scatter x1, waiting for transfers between devices: 0.01 us -> 3.04 us  [per_device(): lax.psum_scatter(feed_grads.reshape(-1, 2 * hidden_local), 'col', scatter...]
    pallas_call x21 -> x23, Pallas kernels: 86.2 us -> 83.4 us  [the longest x18 61.9 us: run(): pl.pallas_call(body, out_shape=list(outs), in_specs=[whole(pltpu.SMEM)] *...]
    ppermute x30 -> x31, waiting for transfers between devices: 61.4 us -> 59.9 us  [swap(): return lax.ppermute(values, axis, [(i, i ^ bit) for i in range(count)])]
    ppermute x8 -> x12, waiting for transfers between devices: 34.3 us -> 33.6 us  [relayout(): got.append(lax.ppermute(piece, ('row', 'col'), pairs))]
    ppermute x8 -> x12, starting transfers between devices: 31.8 us -> 32.2 us  [relayout(): got.append(lax.ppermute(piece, ('row', 'col'), pairs))]
  transfers between devices with their start and end apart: 44 -> 49, of which waited for: 26 -> 31; matrix products, arithmetic and copies ran while one was open for 1% -> 1% of each run, Pallas kernels for 25% -> 26%
where the time goes in v3:
time: 277 us; the launch traced here: 273 us
  waiting for transfers between devices  98.5 us (36%)
  Pallas kernels  83.4 us (30%)
  starting transfers between devices  63 us (23%)
  between operations  14.6 us (5%)
  local copies, waits for them, and re-layouts  9.45 us (3%)
  other arithmetic  4.2 us (2%)
    pallas_call x18, Pallas kernels, run(): pl.pallas_call(body, out_shape=list(outs), in_specs=[whole(pltpu.SMEM)] *...  61.9 us
    ppermute x31, waiting for transfers between devices, swap(): return lax.ppermute(values, axis, [(i, i ^ bit) for i in range(count)])  59.9 us
    ppermute x12, waiting for transfers between devices, relayout(): got.append(lax.ppermute(piece, ('row', 'col'), pairs))  33.6 us
    ppermute x12, starting transfers between devices, relayout(): got.append(lax.ppermute(piece, ('row', 'col'), pairs))  32.2 us
    ppermute x31, starting transfers between devices, swap(): return lax.ppermute(values, axis, [(i, i ^ bit) for i in range(count)])  29.6 us
    pallas_call x5, Pallas kernels, run(): pl.pallas_call(kernel, out_shape=outs, in_specs=[whole(pltpu.SMEM)] * sme...  21.6 us
    unnamed x107, local copies, waits for them, and re-layouts  7.24 us
  transfers between devices with their start and end apart: 49, of which 31 were waited for; matrix products, arithmetic and copies ran while one was open for 1% of the time, Pallas kernels for 26%

profile of v3, /device:TPU:0, one launch (start us, length us, event | category | flops | bytes accessed | tf_op | source)
XLA Modules:
  0.0 273.2 jit_solution(14064219864939972106)
XLA Ops:
  10.9 3.3 %prepare.1 = (bf16[192,640]{1,0:T(8,128)(2,1)}, bf16[192,640]{1,0:T(8,128)(2,1)}, bf16[192,640]{1,0:T(8,128)(2,1)}, bf16[192,640]{1,0:T(8,128)(2,1)}) custom-call(s32[4,7]{1,0:T(4,128)} %rest_0_.3, f32[256,128]{1,0:T(8,128)} %rest_2_.1, bf16[6,192,128]{2,1,0:T(8,128)(2,1)} %rest_3_.1, bf16[6,192]{1,0:T(8,128)(2,1)} %refs_3_.1, bf16[192]{0:T(256)(128)(2,1)} %refs_4_.1, ...), custom_call_target="tpu_custom_call" | custom-call | bytes 2198912 | tf_op jit(solution)/shard_map/prepare/pallas_call | solution.py:251
  15.9 6.4 %collective-permute-start.1 = (bf16[192,640]{1,0:T(8,128)(2,1)}, bf16[192,640]{1,0:T(8,128)(2,1)S(1)}, u32[]{:S(2)}, u32[]{:S(2)}) collective-permute-start(bf16[192,640]{1,0:T(8,128)(2,1)} %get-tuple-element.118), channel_id=1, source_target_pairs={{0,4},{1,8},{2,12},{3,0},{4,6},{5,10},{6,14},{7,2},{8,5},{9,9},{10... | collective-permute-start | bytes 737288 | tf_op jit(solution)/shard_map/ppermute | solution.py:89
  23.4 3.5 %collective-permute-start.3 = (bf16[192,640]{1,0:T(8,128)(2,1)}, bf16[192,640]{1,0:T(8,128)(2,1)S(1)}, u32[]{:S(2)}, u32[]{:S(2)}) collective-permute-start(bf16[192,640]{1,0:T(8,128)(2,1)} %get-tuple-element.120), channel_id=1, source_target_pairs={{0,12},{1,0},{2,4},{3,8},{4,14},{5,2},{6,6},{7,10},{8,13},{9,1},{1... | collective-permute-start | bytes 737288 | tf_op jit(solution)/shard_map/ppermute | solution.py:89
  27.5 2.5 places.1
  30.0 6.9 %collective-permute-done.1.rest_1_ = bf16[192,640]{1,0:T(8,128)(2,1)S(1)} collective-permute-done((bf16[192,640]{1,0:T(8,128)(2,1)}, bf16[192,640]{1,0:T(8,128)(2,1)S(1)}, u32[]{:S(2)}, u32[]{:S(2)}) %collective-permute-start.1) | collective-permute-done | bytes 245792 | tf_op jit(solution)/shard_map/ppermute | solution.py:89
  37.0 6.6 %collective-permute-done.2.rest_2_ = bf16[192,640]{1,0:T(8,128)(2,1)S(1)} collective-permute-done((bf16[192,640]{1,0:T(8,128)(2,1)}, bf16[192,640]{1,0:T(8,128)(2,1)S(1)}, u32[]{:S(2)}, u32[]{:S(2)}) %collective-permute-start.2) | collective-permute-done | bytes 245792 | tf_op jit(solution)/shard_map/ppermute | solution.py:89
  43.6 13.7 %collective-permute-done.3.rest_3_ = bf16[192,640]{1,0:T(8,128)(2,1)S(1)} collective-permute-done((bf16[192,640]{1,0:T(8,128)(2,1)}, bf16[192,640]{1,0:T(8,128)(2,1)S(1)}, u32[]{:S(2)}, u32[]{:S(2)}) %collective-permute-start.3) | collective-permute-done | bytes 245792 | tf_op jit(solution)/shard_map/ppermute | solution.py:89
  58.0 2.7 first_norm.1
  64.8 7.6 %collective-permute-done.5.rest_2_.refs_4_ = bf16[768,256]{1,0:T(8,128)(2,1)S(1)} collective-permute-done((bf16[768,256]{1,0:T(8,128)(2,1)}, bf16[768,256]{1,0:T(8,128)(2,1)S(1)}, u32[]{:S(2)}, u32[]{:S(2)}) %collective-permute-start.5) | collective-permute-done | bytes 393248 | tf_op jit(solution)/shard_map/ppermute | solution.py:29
  80.6 9.3 %attend.1 = (bf16[768,256]{1,0:T(8,128)(2,1)S(1)}, bf16[768,256]{1,0:T(8,128)(2,1)S(1)}, bf16[1536,256]{1,0:T(8,128)(2,1)S(1)}, bf16[192,1024]{1,0:T(8,128)(2,1)...) custom-call(bf16[768,768]{1,0:T(8,128)(2,1)S(1)} %copy-done, ...), custom_call_target="tpu_custom_call" | custom-call | bytes 6201344 | tf_op jit(solution)/shard_map/attend/pallas_call | solution.py:209
  96.5 9.9 %collective-permute-done.10.far = bf16[768,256]{1,0:T(8,128)(2,1)S(1)} collective-permute-done((bf16[768,256]{1,0:T(8,128)(2,1)S(1)}, bf16[768,256]{1,0:T(8,128)(2,1)S(1)}, u32[]{:S(2)}, u32[]{:S(2)}) %collective-permute-start.10) | collective-permute-done | bytes 393248 | tf_op jit(solution)/shard_map/ppermute | solution.py:29
  107.2 3.2 %second_norm.1 = (bf16[768,256]{1,0:T(8,128)(2,1)}, f32[768,256]{1,0:T(8,128)}, bf16[768,256]{1,0:T(8,128)(2,1)}) custom-call(s32[1,256]{1,0:T(1,128)} %get-tuple-element.116.segs, bf16[768,128]{1,0:T(8,128)(2,1)} %get-tuple-element.121.mods, bf16[768,256]{1,0:T(8,128)(2,1)} %get-tuple-element.122.stream, bf16[768,256]{1,0:T(8,128)(2,1)} %copy-done.25, ...), custom_call_target="tpu_custom_call" | custom-call | bytes 3736576 | tf_op jit(solution)/shard_map/second_norm/pallas_call | solution.py:209
  111.8 3.0 %collective-permute-done.13.rest_5_.refs_14_ = bf16[768,256]{1,0:T(8,128)(2,1)S(1)} collective-permute-done((bf16[768,256]{1,0:T(8,128)(2,1)S(1)}, bf16[768,256]{1,0:T(8,128)(2,1)S(1)}, u32[]{:S(2)}, u32[]{:S(2)}) %collective-permute-start.13) | collective-permute-done | bytes 393248 | tf_op jit(solution)/shard_map/ppermute | solution.py:29
  115.4 7.1 %collective-permute-done.12.rest_4_.refs_6_ = bf16[768,256]{1,0:T(8,128)(2,1)S(1)} collective-permute-done((bf16[768,256]{1,0:T(8,128)(2,1)}, bf16[768,256]{1,0:T(8,128)(2,1)S(1)}, u32[]{:S(2)}, u32[]{:S(2)}) %collective-permute-start.12) | collective-permute-done | bytes 393248 | tf_op jit(solution)/shard_map/ppermute | solution.py:29
  125.9 10.2 %feed_first.1 = (bf16[768,256]{1,0:T(8,128)(2,1)}, bf16[768,256]{1,0:T(8,128)(2,1)}, bf16[1536,256]{1,0:T(8,128)(2,1)}, bf16[768,256]{1,0:T(8,128)(2,1)}, bf16[7...) custom-call(bf16[768,1536]{1,0:T(8,128)(2,1)} %all-gather.5.cloned.1, ...), custom_call_target="tpu_custom_call" | custom-call | bytes 11798016 | tf_op jit(solution)/shard_map/feed_first/pallas_call | solution.py:209
  136.1 2.5 collective-permute-done.16.near
  141.5 7.6 %feed_grads.1 = bf16[4,208,1536]{2,1,0:T(8,128)(2,1)} custom-call(bf16[768,256]{1,0:T(8,128)(2,1)} %get-tuple-element.148.refs_0_, bf16[768,256]{1,0:T(8,128)(2,1)} %get-tuple-element.149.refs_1_, bf16[768,256]{1,0:T(8,128)(2,1)} %get-tuple-element.150.refs_2_, bf16[768,256]{1,0:T(8,128)(2,1)} %get-tuple-element.151.refs_3_, ...), custom_call_target="tpu_custom_call" | custom-call | bytes 8847360 | tf_op jit(solution)/shard_map/feed_grads/pallas_call | solution.py:251
  152.0 4.0 %middle_grad.1 = (f32[768,256]{1,0:T(8,128)}, bf16[768,256]{1,0:T(8,128)(2,1)}, bf16[768,256]{1,0:T(8,128)(2,1)}) custom-call(s32[1,256]{1,0:T(1,128)} %get-tuple-element.116.segs, bf16[768,128]{1,0:T(8,128)(2,1)} %get-tuple-element.121.mods, f32[768,256]{1,0:T(8,128)} %get-tuple-element.136.middle, bf16[768,256]{1,0:T(8,128)(2,1)} %get-tuple-element.127.cot, ...), custom_call_target="tpu_custom_call" | custom-call | bytes 4523008 | tf_op jit(solution)/shard_map/middle_grad/pallas_call | solution.py:209
  158.7 8.0 %attend_back_first.1 = (bf16[192,512]{1,0:T(8,128)(2,1)}, f32[192,1024]{1,0:T(8,128)}, f32[192,1024]{1,0:T(8,128)}) custom-call(bf16[192,1024]{1,0:T(8,128)(2,1)} %copy-done.13, bf16[192,1024]{1,0:T(8,128)(2,1)} %copy-done.14, bf16[768,768]{1,0:T(8,128)(2,1)} %all-gather.3.cloned.1.call-done.weight_all, bf16[768,256]{1,0:T(8,128)(2,1)} %get-tuple-element.162.first.refs_6_, ...), custom_call_target="tpu_custom_call" | custom-call | bytes 5611520 | tf_op jit(solution)/shard_map/attend_back_first/pallas_call | solution.py:209
  170.2 10.1 %attend_back_last.1 = (bf16[768,256]{1,0:T(8,128)(2,1)}, bf16[768,256]{1,0:T(8,128)(2,1)}, bf16[1536,256]{1,0:T(8,128)(2,1)}, bf16[576,1024]{1,0:T(8,128)(2,1)}) custom-call(bf16[192,1024]{1,0:T(8,128)(2,1)} %copy-done.13, bf16[192,1024]{1,0:T(8,128)(2,1)} %copy-done.14, bf16[768,768]{1,0:T(8,128)(2,1)} %all-gather.3.cloned.1.call-done.weight_all, ...), custom_call_target="tpu_custom_call" | custom-call | bytes 8364032 | tf_op jit(solution)/shard_map/attend_back_last/pallas_call | solution.py:209
  186.3 6.2 %attend_weights.1 = (bf16[4,96,768]{2,1,0:T(8,128)(2,1)}, bf16[4,96,768]{2,1,0:T(8,128)(2,1)}) custom-call(bf16[576,1024]{1,0:T(8,128)(2,1)} %get-tuple-element.180.refs_0_, bf16[192,1024]{1,0:T(8,128)(2,1)} %copy-done.4, bf16[768,256]{1,0:T(8,128)(2,1)} %get-tuple-element.125.rest_0_.refs_2_, bf16[768,256]{1,0:T(8,128)(2,1)} %copy-done.8, ...), custom_call_target="tpu_custom_call" | custom-call | bytes 5898240 | tf_op jit(solution)/shard_map/attend_weights/pallas_call | solution.py:251
  198.9 3.0 %reduce-scatter.2.cloned.1.call-done.rest_0_ = bf16[208,1536]{1,0:T(8,128)(2,1)} async-done(((bf16[832,1536]{1,0:T(8,128)(2,1)}), bf16[208,1536]{1,0:T(8,128)(2,1)}) %reduce-scatter.2.cloned.1.call-update) | async-done | bytes 638992 | tf_op jit(solution)/shard_map/reduce_scatter | solution.py:915
  203.4 3.9 %collective-permute-start.26 = (bf16[192,384]{1,0:T(8,128)(2,1)S(1)}, bf16[192,384]{1,0:T(8,128)(2,1)S(1)}, u32[]{:S(2)}, u32[]{:S(2)}) collective-permute-start(bf16[192,384]{1,0:T(8,128)(2,1)S(1)} %get-tuple-element.191), channel_id=1, source_target_pairs={{4,0},{8,1},{12,2},{0,3},{6,4},{10,5},{14,6},{2,7},{5,8},{9,9},{13... | collective-permute-start | bytes 442376 | tf_op jit(solution)/shard_map/ppermute | solution.py:89
  207.4 3.5 %collective-permute-start.28 = (bf16[192,384]{1,0:T(8,128)(2,1)S(1)}, bf16[192,384]{1,0:T(8,128)(2,1)S(1)}, u32[]{:S(2)}, u32[]{:S(2)}) collective-permute-start(bf16[192,384]{1,0:T(8,128)(2,1)S(1)} %get-tuple-element.193), channel_id=1, source_target_pairs={{12,0},{0,1},{4,2},{8,3},{14,4},{2,5},{6,6},{10,7},{13,8},{1,9},{5... | collective-permute-start | bytes 442376 | tf_op jit(solution)/shard_map/ppermute | solution.py:89
  211.3 2.5 collective-permute-done.27.rest_2_
  213.8 2.5 collective-permute-done.28.rest_3_
  217.2 5.9 %collective-permute-start.33 = (f32[1,64,192]{2,1,0:T(8,128)S(1)}, f32[1,64,192]{2,1,0:T(8,128)S(1)}, u32[]{:S(2)}, u32[]{:S(2)}) collective-permute-start(f32[1,64,192]{2,1,0:T(8,128)S(1)} %get-tuple-element.199), channel_id=1, source_target_pairs={{0,4},{4,0},{8,12},{12,8},{1,5},{5,1},{9,13},{13,9},{2,6},{6,2},{1... | collective-permute-start | bytes 147464 | tf_op jit(solution)/shard_map/ppermute | solution.py:29
  224.6 3.2 %collective-permute-start.43 = (bf16[96,768]{1,0:T(8,128)(2,1)S(1)}, bf16[96,768]{1,0:T(8,128)(2,1)S(1)}, u32[]{:S(2)}, u32[]{:S(2)}) collective-permute-start(bf16[96,768]{1,0:T(8,128)(2,1)S(1)} %get-tuple-element.209), channel_id=1, source_target_pairs={{0,3},{1,2},{2,1},{3,0},{4,7},{5,6},{6,5},{7,4},{8,11},{9,10},{10,... | collective-permute-start | bytes 442376 | tf_op jit(solution)/shard_map/ppermute | solution.py:29
  230.5 9.9 %collective-permute-done.42.rest_2_ = bf16[96,768]{1,0:T(8,128)(2,1)S(1)} collective-permute-done((bf16[96,768]{1,0:T(8,128)(2,1)S(1)}, bf16[96,768]{1,0:T(8,128)(2,1)S(1)}, u32[]{:S(2)}, u32[]{:S(2)}) %collective-permute-start.42) | collective-permute-done | bytes 147488 | tf_op jit(solution)/shard_map/ppermute | solution.py:29
  242.5 5.2 %collective-permute-start.30 = (bf16[192,256]{1,0:T(8,128)(2,1)S(1)}, bf16[192,256]{1,0:T(8,128)(2,1)S(1)}, u32[]{:S(2)}, u32[]{:S(2)}) collective-permute-start(bf16[192,256]{1,0:T(8,128)(2,1)S(1)} %get-tuple-element.195), channel_id=1, source_target_pairs={{4,0},{8,1},{12,2},{0,3},{6,4},{10,5},{14,6},{2,7},{5,8},{9,9},{13... | collective-permute-start | bytes 294920 | tf_op jit(solution)/shard_map/ppermute | solution.py:89
  248.6 4.6 %collective-permute-start.32 = (bf16[192,256]{1,0:T(8,128)(2,1)S(1)}, bf16[192,256]{1,0:T(8,128)(2,1)S(1)}, u32[]{:S(2)}, u32[]{:S(2)}) collective-permute-start(bf16[192,256]{1,0:T(8,128)(2,1)S(1)} %get-tuple-element.197), channel_id=1, source_target_pairs={{12,0},{0,1},{4,2},{8,3},{14,4},{2,5},{6,6},{10,7},{13,8},{1,9},{5... | collective-permute-start | bytes 294920 | tf_op jit(solution)/shard_map/ppermute | solution.py:89
  253.2 2.6 modulation_back.1
  (208 shorter events, 77.5 us)
Async XLA Ops:
  7.2 65.4 %all-gather.3.cloned.1.call-start = ((), (), s32[]{:S(2)}) async-start(), calls=%async_computation.1 | async-start | bytes 1327104 | tf_op jit(solution)/shard_map/all_gather | solution.py:848
  10.9 114.9 %all-gather.5.cloned.1.call-start = ((), (), s32[]{:S(2)}) async-start(), calls=%async_computation.2 | async-start | bytes 2654208 | tf_op jit(solution)/shard_map/all_gather | solution.py:848
  14.3 15.8 %collective-permute-start = (bf16[192,640]{1,0:T(8,128)(2,1)}, bf16[192,640]{1,0:T(8,128)(2,1)S(1)}, u32[]{:S(2)}, u32[]{:S(2)}) collective-permute-start(bf16[192,640]{1,0:T(8,128)(2,1)} %get-tuple-element.117), channel_id=1, source_target_pairs={{0,0},{1,4},{2,8},{3,12},{4,2},{5,6},{6,10},{7,14},{8,1},{9,5},{10... | collective-permute-start | bytes 737288 | tf_op jit(solution)/shard_map/ppermute | solution.py:89
  15.9 21.1 %collective-permute-start.1 = (bf16[192,640]{1,0:T(8,128)(2,1)}, bf16[192,640]{1,0:T(8,128)(2,1)S(1)}, u32[]{:S(2)}, u32[]{:S(2)}) collective-permute-start(bf16[192,640]{1,0:T(8,128)(2,1)} %get-tuple-element.118), channel_id=1, source_target_pairs={{0,4},{1,8},{2,12},{3,0},{4,6},{5,10},{6,14},{7,2},{8,5},{9,9},{10... | collective-permute-start | bytes 737288 | tf_op jit(solution)/shard_map/ppermute | solution.py:89
  22.2 21.4 %collective-permute-start.2 = (bf16[192,640]{1,0:T(8,128)(2,1)}, bf16[192,640]{1,0:T(8,128)(2,1)S(1)}, u32[]{:S(2)}, u32[]{:S(2)}) collective-permute-start(bf16[192,640]{1,0:T(8,128)(2,1)} %get-tuple-element.119), channel_id=1, source_target_pairs={{0,8},{1,12},{2,0},{3,4},{4,10},{5,14},{6,2},{7,6},{8,9},{9,13},{1... | collective-permute-start | bytes 737288 | tf_op jit(solution)/shard_map/ppermute | solution.py:89
  23.4 33.9 %collective-permute-start.3 = (bf16[192,640]{1,0:T(8,128)(2,1)}, bf16[192,640]{1,0:T(8,128)(2,1)S(1)}, u32[]{:S(2)}, u32[]{:S(2)}) collective-permute-start(bf16[192,640]{1,0:T(8,128)(2,1)} %get-tuple-element.120), channel_id=1, source_target_pairs={{0,12},{1,0},{2,4},{3,8},{4,14},{5,2},{6,6},{7,10},{8,13},{9,1},{1... | collective-permute-start | bytes 737288 | tf_op jit(solution)/shard_map/ppermute | solution.py:89
  60.6 11.7 %collective-permute-start.5 = (bf16[768,256]{1,0:T(8,128)(2,1)}, bf16[768,256]{1,0:T(8,128)(2,1)S(1)}, u32[]{:S(2)}, u32[]{:S(2)}) collective-permute-start(bf16[768,256]{1,0:T(8,128)(2,1)} %get-tuple-element.125.rest_0_.refs_2_), channel_id=1, source_target_pairs={{0,8},{4,12},{8,0},{12,4},{1,9},{5,13},{9,1},{13,5},{2,10},{6,14},... | collective-permute-start | bytes 1179656 | tf_op jit(solution)/shard_map/ppermute | solution.py:29
  73.4 128.5 %reduce-scatter.2.cloned.1.call-start = ((), (), s32[]{:S(2)}) async-start(), calls=%async_computation.3 | async-start | bytes 3194880 | tf_op jit(solution)/shard_map/reduce_scatter | solution.py:915
  94.4 12.0 %collective-permute-start.10 = (bf16[768,256]{1,0:T(8,128)(2,1)S(1)}, bf16[768,256]{1,0:T(8,128)(2,1)S(1)}, u32[]{:S(2)}, u32[]{:S(2)}) collective-permute-start(bf16[768,256]{1,0:T(8,128)(2,1)S(1)} %add_convert_fusion.3), channel_id=1, source_target_pairs={{0,8},{4,12},{8,0},{12,4},{1,9},{5,13},{9,1},{13,5},{2,10},{6,14},... | collective-permute-start | bytes 1179656 | tf_op jit(solution)/shard_map/ppermute | solution.py:29
  96.0 18.9 %collective-permute-start.13 = (bf16[768,256]{1,0:T(8,128)(2,1)S(1)}, bf16[768,256]{1,0:T(8,128)(2,1)S(1)}, u32[]{:S(2)}, u32[]{:S(2)}) collective-permute-start(bf16[768,256]{1,0:T(8,128)(2,1)S(1)} %copy-done.30), channel_id=1, source_target_pairs={{0,8},{4,12},{8,0},{12,4},{1,9},{5,13},{9,1},{13,5},{2,10},{6,14},... | collective-permute-start | bytes 1179656 | tf_op jit(solution)/shard_map/ppermute | solution.py:29
  110.4 12.1 %collective-permute-start.12 = (bf16[768,256]{1,0:T(8,128)(2,1)}, bf16[768,256]{1,0:T(8,128)(2,1)S(1)}, u32[]{:S(2)}, u32[]{:S(2)}) collective-permute-start(bf16[768,256]{1,0:T(8,128)(2,1)} %get-tuple-element.140.rest_0_.refs_4_), channel_id=1, source_target_pairs={{0,8},{4,12},{8,0},{12,4},{1,9},{5,13},{9,1},{13,5},{2,10},{6,14},... | collective-permute-start | bytes 1179656 | tf_op jit(solution)/shard_map/ppermute | solution.py:29
  114.9 7.6 %collective-permute-start.11 = (bf16[768,256]{1,0:T(8,128)(2,1)}, bf16[768,256]{1,0:T(8,128)(2,1)S(1)}, u32[]{:S(2)}, u32[]{:S(2)}) collective-permute-start(bf16[768,256]{1,0:T(8,128)(2,1)} %get-tuple-element.140.rest_0_.refs_4_), channel_id=1, source_target_pairs={{0,4},{4,0},{8,12},{12,8},{1,5},{5,1},{9,13},{13,9},{2,6},{6,2},{1... | collective-permute-start | bytes 1179656 | tf_op jit(solution)/shard_map/ppermute | solution.py:29
  140.0 11.2 %collective-permute-start.17 = (bf16[768,256]{1,0:T(8,128)(2,1)S(1)}, bf16[768,256]{1,0:T(8,128)(2,1)S(1)}, u32[]{:S(2)}, u32[]{:S(2)}) collective-permute-start(bf16[768,256]{1,0:T(8,128)(2,1)S(1)} %add_convert_fusion.2), channel_id=1, source_target_pairs={{0,8},{4,12},{8,0},{12,4},{1,9},{5,13},{9,1},{13,5},{2,10},{6,14},... | collective-permute-start | bytes 1179656 | tf_op jit(solution)/shard_map/ppermute | solution.py:29
  151.2 16.5 %collective-permute-start.21 = (bf16[1536,256]{1,0:T(8,128)(2,1)S(1)}, bf16[1536,256]{1,0:T(8,128)(2,1)S(1)}, u32[]{:S(2)}, u32[]{:S(2)}) collective-permute-start(bf16[1536,256]{1,0:T(8,128)(2,1)S(1)} %copy-done.52), channel_id=1, source_target_pairs={{0,4},{4,0},{8,12},{12,8},{1,5},{5,1},{9,13},{13,9},{2,6},{6,2},{1... | collective-permute-start | bytes 2359304 | tf_op jit(solution)/shard_map/ppermute | solution.py:29
  156.0 11.7 %collective-permute-start.18 = (bf16[768,256]{1,0:T(8,128)(2,1)}, bf16[768,256]{1,0:T(8,128)(2,1)S(1)}, u32[]{:S(2)}, u32[]{:S(2)}) collective-permute-start(bf16[768,256]{1,0:T(8,128)(2,1)} %get-tuple-element.162.first.refs_6_), channel_id=1, source_target_pairs={{0,8},{4,12},{8,0},{12,4},{1,9},{5,13},{9,1},{13,5},{2,10},{6,14},... | collective-permute-start | bytes 1179656 | tf_op jit(solution)/shard_map/ppermute | solution.py:29
  167.8 12.5 %collective-permute-start.22 = (bf16[768,256]{1,0:T(8,128)(2,1)S(1)}, bf16[768,256]{1,0:T(8,128)(2,1)S(1)}, u32[]{:S(2)}, u32[]{:S(2)}) collective-permute-start(bf16[768,256]{1,0:T(8,128)(2,1)S(1)} %add_convert_fusion.1), channel_id=1, source_target_pairs={{0,8},{4,12},{8,0},{12,4},{1,9},{5,13},{9,1},{13,5},{2,10},{6,14},... | collective-permute-start | bytes 1179656 | tf_op jit(solution)/shard_map/ppermute | solution.py:29
  184.8 11.4 %collective-permute-start.24 = (bf16[768,256]{1,0:T(8,128)(2,1)}, bf16[768,256]{1,0:T(8,128)(2,1)S(1)}, u32[]{:S(2)}, u32[]{:S(2)}) collective-permute-start(bf16[768,256]{1,0:T(8,128)(2,1)} %add_convert_fusion), channel_id=1, source_target_pairs={{0,8},{4,12},{8,0},{12,4},{1,9},{5,13},{9,1},{13,5},{2,10},{6,14},... | collective-permute-start | bytes 1179656 | tf_op jit(solution)/shard_map/ppermute | solution.py:29
  192.6 30.6 %collective-permute-start.40 = (bf16[4,96,768]{2,1,0:T(8,128)(2,1)}, bf16[4,96,768]{2,1,0:T(8,128)(2,1)S(1)}, u32[]{:S(2)}, u32[]{:S(2)}) collective-permute-start(bf16[4,96,768]{2,1,0:T(8,128)(2,1)} %get-tuple-element.205), channel_id=1, source_target_pairs={{0,16},{16,0},{1,17},{17,1},{2,18},{18,2},{3,19},{19,3},{4,20},{20... | collective-permute-start | bytes 1769480 | tf_op jit(solution)/shard_map/ppermute | solution.py:29
  198.2 9.2 %collective-permute-start.25 = (bf16[192,384]{1,0:T(8,128)(2,1)S(1)}, bf16[192,384]{1,0:T(8,128)(2,1)S(1)}, u32[]{:S(2)}, u32[]{:S(2)}) collective-permute-start(bf16[192,384]{1,0:T(8,128)(2,1)S(1)} %get-tuple-element.190), channel_id=1, source_target_pairs={{0,0},{4,1},{8,2},{12,3},{2,4},{6,5},{10,6},{14,7},{1,8},{5,9},{9,... | collective-permute-start | bytes 442376 | tf_op jit(solution)/shard_map/ppermute | solution.py:89
  201.9 63.5 %collective-permute-start.45 = (bf16[208,1536]{1,0:T(8,128)(2,1)}, bf16[208,1536]{1,0:T(8,128)(2,1)S(1)}, u32[]{:S(2)}, u32[]{:S(2)}) collective-permute-start(bf16[208,1536]{1,0:T(8,128)(2,1)} %reduce-scatter.2.cloned.1.call-done.rest_0_), channel_id=1, source_target_pairs={{0,16},{16,0},{1,17},{17,1},{2,18},{18,2},{3,19},{19,3},{4,20},{20... | collective-permute-start | bytes 1916936 | tf_op jit(solution)/shard_map/ppermute | solution.py:29
  203.4 7.9 %collective-permute-start.26 = (bf16[192,384]{1,0:T(8,128)(2,1)S(1)}, bf16[192,384]{1,0:T(8,128)(2,1)S(1)}, u32[]{:S(2)}, u32[]{:S(2)}) collective-permute-start(bf16[192,384]{1,0:T(8,128)(2,1)S(1)} %get-tuple-element.191), channel_id=1, source_target_pairs={{4,0},{8,1},{12,2},{0,3},{6,4},{10,5},{14,6},{2,7},{5,8},{9,9},{13... | collective-permute-start | bytes 442376 | tf_op jit(solution)/shard_map/ppermute | solution.py:89
  207.4 8.9 %collective-permute-start.28 = (bf16[192,384]{1,0:T(8,128)(2,1)S(1)}, bf16[192,384]{1,0:T(8,128)(2,1)S(1)}, u32[]{:S(2)}, u32[]{:S(2)}) collective-permute-start(bf16[192,384]{1,0:T(8,128)(2,1)S(1)} %get-tuple-element.193), channel_id=1, source_target_pairs={{12,0},{0,1},{4,2},{8,3},{14,4},{2,5},{6,6},{10,7},{13,8},{1,9},{5... | collective-permute-start | bytes 442376 | tf_op jit(solution)/shard_map/ppermute | solution.py:89
  217.2 10.6 %collective-permute-start.33 = (f32[1,64,192]{2,1,0:T(8,128)S(1)}, f32[1,64,192]{2,1,0:T(8,128)S(1)}, u32[]{:S(2)}, u32[]{:S(2)}) collective-permute-start(f32[1,64,192]{2,1,0:T(8,128)S(1)} %get-tuple-element.199), channel_id=1, source_target_pairs={{0,4},{4,0},{8,12},{12,8},{1,5},{5,1},{9,13},{13,9},{2,6},{6,2},{1... | collective-permute-start | bytes 147464 | tf_op jit(solution)/shard_map/ppermute | solution.py:29
  223.7 16.6 %collective-permute-start.42 = (bf16[96,768]{1,0:T(8,128)(2,1)S(1)}, bf16[96,768]{1,0:T(8,128)(2,1)S(1)}, u32[]{:S(2)}, u32[]{:S(2)}) collective-permute-start(bf16[96,768]{1,0:T(8,128)(2,1)S(1)} %get-tuple-element.208), channel_id=1, source_target_pairs={{0,2},{1,3},{2,0},{3,1},{4,6},{5,7},{6,4},{7,5},{8,10},{9,11},{10,... | collective-permute-start | bytes 442376 | tf_op jit(solution)/shard_map/ppermute | solution.py:29
  224.6 16.3 %collective-permute-start.43 = (bf16[96,768]{1,0:T(8,128)(2,1)S(1)}, bf16[96,768]{1,0:T(8,128)(2,1)S(1)}, u32[]{:S(2)}, u32[]{:S(2)}) collective-permute-start(bf16[96,768]{1,0:T(8,128)(2,1)S(1)} %get-tuple-element.209), channel_id=1, source_target_pairs={{0,3},{1,2},{2,1},{3,0},{4,7},{5,6},{6,5},{7,4},{8,11},{9,10},{10,... | collective-permute-start | bytes 442376 | tf_op jit(solution)/shard_map/ppermute | solution.py:29
  227.8 13.2 %collective-permute-start.29 = (bf16[192,256]{1,0:T(8,128)(2,1)S(1)}, bf16[192,256]{1,0:T(8,128)(2,1)S(1)}, u32[]{:S(2)}, u32[]{:S(2)}) collective-permute-start(bf16[192,256]{1,0:T(8,128)(2,1)S(1)} %get-tuple-element.194), channel_id=1, source_target_pairs={{0,0},{4,1},{8,2},{12,3},{2,4},{6,5},{10,6},{14,7},{1,8},{5,9},{9,... | collective-permute-start | bytes 294920 | tf_op jit(solution)/shard_map/ppermute | solution.py:89
  230.1 12.4 %collective-permute-start.36 = (f32[2,64,192]{2,1,0:T(8,128)S(1)}, f32[2,64,192]{2,1,0:T(8,128)S(1)}, u32[]{:S(2)}, u32[]{:S(2)}) collective-permute-start(f32[2,64,192]{2,1,0:T(8,128)S(1)} %constant_dynamic-update-slice_fusion.rest_4_), channel_id=1, source_target_pairs={{0,24},{4,28},{8,16},{12,20},{16,8},{20,12},{24,0},{28,4},{1,25},{... | collective-permute-start | bytes 294920 | tf_op jit(solution)/shard_map/ppermute | solution.py:990
  240.9 7.7 %collective-permute-start.34 = (f32[2,64,192]{2,1,0:T(8,128)S(1)}, f32[2,64,192]{2,1,0:T(8,128)S(1)}, u32[]{:S(2)}, u32[]{:S(2)}) collective-permute-start(f32[2,64,192]{2,1,0:T(8,128)S(1)} %constant_dynamic-update-slice_fusion.rest_4_), channel_id=1, source_target_pairs={{0,8},{4,12},{8,0},{12,4},{16,24},{20,28},{24,16},{28,20},{1,9},{5... | collective-permute-start | bytes 294920 | tf_op jit(solution)/shard_map/ppermute | solution.py:990
  240.9 23.4 %collective-permute-start.44 = (bf16[96,768]{1,0:T(8,128)(2,1)S(1)}, bf16[96,768]{1,0:T(8,128)(2,1)S(1)}, u32[]{:S(2)}, u32[]{:S(2)}) collective-permute-start(bf16[96,768]{1,0:T(8,128)(2,1)S(1)} %block_sum.1.own), channel_id=1, source_target_pairs={{0,16},{16,0},{1,17},{17,1},{2,18},{18,2},{3,19},{19,3},{4,20},{20... | collective-permute-start | bytes 442376 | tf_op jit(solution)/shard_map/ppermute | solution.py:29
  242.5 13.4 %collective-permute-start.30 = (bf16[192,256]{1,0:T(8,128)(2,1)S(1)}, bf16[192,256]{1,0:T(8,128)(2,1)S(1)}, u32[]{:S(2)}, u32[]{:S(2)}) collective-permute-start(bf16[192,256]{1,0:T(8,128)(2,1)S(1)} %get-tuple-element.195), channel_id=1, source_target_pairs={{4,0},{8,1},{12,2},{0,3},{6,4},{10,5},{14,6},{2,7},{5,8},{9,9},{13... | collective-permute-start | bytes 294920 | tf_op jit(solution)/shard_map/ppermute | solution.py:89
  247.7 9.5 %collective-permute-start.31 = (bf16[192,256]{1,0:T(8,128)(2,1)S(1)}, bf16[192,256]{1,0:T(8,128)(2,1)S(1)}, u32[]{:S(2)}, u32[]{:S(2)}) collective-permute-start(bf16[192,256]{1,0:T(8,128)(2,1)S(1)} %get-tuple-element.196), channel_id=1, source_target_pairs={{8,0},{12,1},{0,2},{4,3},{10,4},{14,5},{2,6},{6,7},{9,8},{13,9},{1... | collective-permute-start | bytes 294920 | tf_op jit(solution)/shard_map/ppermute | solution.py:89
  248.6 10.1 %collective-permute-start.32 = (bf16[192,256]{1,0:T(8,128)(2,1)S(1)}, bf16[192,256]{1,0:T(8,128)(2,1)S(1)}, u32[]{:S(2)}, u32[]{:S(2)}) collective-permute-start(bf16[192,256]{1,0:T(8,128)(2,1)S(1)} %get-tuple-element.197), channel_id=1, source_target_pairs={{12,0},{0,1},{4,2},{8,3},{14,4},{2,5},{6,6},{10,7},{13,8},{1,9},{5... | collective-permute-start | bytes 294920 | tf_op jit(solution)/shard_map/ppermute | solution.py:89
  (70 other events, 997.5 us)
Sparse Core Ops, SparseCore 0:
  11.0 61.5 all-gather.2
  74.8 51.0 all-gather.4
  151.4 50.5 reduce-scatter.1

commit v4 on v3

--- a/solution.py
+++ b/solution.py
@@ -21,7 +21,7 @@
 GAIN_ONE, GAIN_TWO, DOWN_BIAS = 48, 49, 50
 STATS = 51
 VMEM_LIMIT = 56 * 1024 * 1024
-NEAR = {'unbundle': 12, 'modulation_back': 12, 'table_sum': 12, 'attn_weight_out': 12, 'feed_weight_out': 12, 'pair_sum': 12, 'block_sum': 12, 'join': 12, 'finish_forward': 12, 'finish_backward': 12, 'feed_first': 56, 'attend_back_first': 56, 'attend_back_last': 56, 'second_norm': 56, 'middle_grad': 56, 'branch_grad': 56, 'first_norm': 56, 'attend': 40}
+NEAR = {'unbundle': 12, 'modulation_back': 12, 'table_sum': 12, 'attn_weight_out': 12, 'feed_weight_out': 12, 'pair_sum': 12, 'block_sum': 12, 'join': 12, 'finish_forward': 12, 'finish_backward': 12, 'feed_first': 56, 'attend_back_first': 56, 'attend_back_last': 56, 'second_norm': 12, 'middle_grad': 12, 'branch_grad': 12, 'first_norm': 12, 'attend': 40}
 
 
 def swap(values, axis, bit):
@@ -847,12 +847,6 @@
         part = jnp.concatenate(parts, 1) if len(parts) > 1 else parts[0]
         return lax.all_gather(part, ("col", "dp"), axis=0, tiled=True)
 
-    attn_block = run(
-        pack, "pack", [shape((width_local, 4 * head_width), LOW)],
-        [qkv_weight.transpose(1, 0, 2), proj_weight],
-    )
-    attn_weights = gather_weight(attn_block)
-
     bundles = run(
         functools.partial(prepare, grid, slot_count), "prepare",
         [shape((width_local, 2 * own + 2 * LANES), LOW)] * grid.cols,
@@ -862,6 +856,12 @@
          pltpu.VMEM((grid.per_row, width_local, 2 * LANES), LOW)],
         smem=1,
     )
+    attn_block = run(
+        pack, "pack", [shape((width_local, 4 * head_width), LOW)],
+        after(bundles[:1], [qkv_weight.transpose(1, 0, 2), proj_weight]),
+    )
+    attn_weights = gather_weight(attn_block)
+
     bundles = relayout(bundles)
     segs_row, segs_col, segs_own, cosine, sine = run(
         functools.partial(places, grid, slot_count), "places",
@@ -962,7 +962,7 @@
         return found + blocks
 
     parts[2:] = after(mlp_terms[2:], parts[2:])
-    back_terms, found = scatter_rows(parts, back_filler)
+    back_terms, found = scatter_rows(parts, back_filler, True)
     result_chunks, small, attn_grads = found[: grid.cols], found[grid.cols], found[grid.cols + 1 :]
     bundles = run(
         functools.partial(finish_backward, grid), "finish_backward",
@@ -1023,7 +1023,7 @@
     up_out, up_bias_out, down_out = run(
         feed_weight_out, "feed_weight_out",
         [shape(up_weight.shape, FULL), shape(up_bias.shape, FULL), shape(down_weight.shape, FULL)],
-        all_dp(feed_grads),
+        all_dp(after(bundles, [feed_grads])[0]),
     )
     qkv_out, proj_out = run(
         functools.partial(attn_weight_out, grid), "attn_weight_out",

time: 277 us -> 273 us (0.986)
  Pallas kernels: 83.4 us -> 73.9 us
  starting transfers between devices: 63 us -> 68 us
    pallas_call x18, Pallas kernels: 61.9 us -> 52.5 us  [run(): pl.pallas_call(body, out_shape=list(outs), in_specs=[whole(pltpu.SMEM)] *...]
    ppermute x31, waiting for transfers between devices: 59.9 us -> 64 us  [swap(): return lax.ppermute(values, axis, [(i, i ^ bit) for i in range(count)])]
    ppermute x31, starting transfers between devices: 29.6 us -> 33.2 us  [swap(): return lax.ppermute(values, axis, [(i, i ^ bit) for i in range(count)])]
    reduce_scatter x1, waiting for transfers between devices: 3.04 us -> 0.01 us  [per_device(): lax.psum_scatter(feed_grads.reshape(-1, 2 * hidden_local), 'col', scatter...]
    unnamed x107 -> x87, local copies, waits for them, and re-layouts: 7.24 us -> 7.51 us
  transfers between devices with their start and end apart: 49 -> 49, of which waited for: 31 -> 27; matrix products, arithmetic and copies ran while one was open for 1% -> 1% of each run, Pallas kernels for 26% -> 21%
where the time goes in v4:
time: 273 us; the launch traced here: 269 us
  waiting for transfers between devices  98.8 us (36%)
  Pallas kernels  73.9 us (27%)
  starting transfers between devices  68 us (25%)
  between operations  14.6 us (5%)
  local copies, waits for them, and re-layouts  10.7 us (4%)
  other arithmetic  3.2 us (1%)
    ppermute x31, waiting for transfers between devices, swap(): return lax.ppermute(values, axis, [(i, i ^ bit) for i in range(count)])  64 us
    pallas_call x18, Pallas kernels, run(): pl.pallas_call(body, out_shape=list(outs), in_specs=[whole(pltpu.SMEM)] *...  52.5 us
    ppermute x12, starting transfers between devices, relayout(): got.append(lax.ppermute(piece, ('row', 'col'), pairs))  34 us
    ppermute x31, starting transfers between devices, swap(): return lax.ppermute(values, axis, [(i, i ^ bit) for i in range(count)])  33.2 us
    ppermute x12, waiting for transfers between devices, relayout(): got.append(lax.ppermute(piece, ('row', 'col'), pairs))  30.9 us
    pallas_call x5, Pallas kernels, run(): pl.pallas_call(kernel, out_shape=outs, in_specs=[whole(pltpu.SMEM)] * sme...  21.4 us
    unnamed x87, local copies, waits for them, and re-layouts  7.51 us
  transfers between devices with their start and end apart: 49, of which 27 were waited for; matrix products, arithmetic and copies ran while one was open for 1% of the time, Pallas kernels for 21%

profile of v4, /device:TPU:0, one launch (start us, length us, event | category | flops | bytes accessed | tf_op | source)
XLA Modules:
  0.0 269.2 jit_solution(8595927659961510595)
XLA Ops:
  7.2 3.3 %prepare.1 = (bf16[192,640]{1,0:T(8,128)(2,1)}, bf16[192,640]{1,0:T(8,128)(2,1)}, bf16[192,640]{1,0:T(8,128)(2,1)}, bf16[192,640]{1,0:T(8,128)(2,1)}) custom-call(s32[4,7]{1,0:T(4,128)} %rest_0_.3, f32[256,128]{1,0:T(8,128)} %rest_2_.1, bf16[6,192,128]{2,1,0:T(8,128)(2,1)} %rest_3_.1, bf16[6,192]{1,0:T(8,128)(2,1)} %refs_3_.1, bf16[192]{0:T(256)(128)(2,1)} %refs_4_.1, ...), custom_call_target="tpu_custom_call" | custom-call | bytes 2198912 | tf_op jit(solution)/shard_map/prepare/pallas_call | solution.py:251
  14.2 2.4 collective-permute-start.1
  16.5 3.5 %collective-permute-start.2 = (bf16[192,640]{1,0:T(8,128)(2,1)}, bf16[192,640]{1,0:T(8,128)(2,1)S(1)}, u32[]{:S(2)}, u32[]{:S(2)}) collective-permute-start(bf16[192,640]{1,0:T(8,128)(2,1)} %get-tuple-element.129), channel_id=1, source_target_pairs={{0,8},{1,12},{2,0},{3,4},{4,10},{5,14},{6,2},{7,6},{8,9},{9,13},{1... | collective-permute-start | bytes 737288 | tf_op jit(solution)/shard_map/ppermute | solution.py:89
  20.1 4.5 %collective-permute-start.3 = (bf16[192,640]{1,0:T(8,128)(2,1)}, bf16[192,640]{1,0:T(8,128)(2,1)S(1)}, u32[]{:S(2)}, u32[]{:S(2)}) collective-permute-start(bf16[192,640]{1,0:T(8,128)(2,1)} %get-tuple-element.130), channel_id=1, source_target_pairs={{0,12},{1,0},{2,4},{3,8},{4,14},{5,2},{6,6},{7,10},{8,13},{9,1},{1... | collective-permute-start | bytes 737288 | tf_op jit(solution)/shard_map/ppermute | solution.py:89
  26.8 2.5 places.1
  29.4 6.9 %collective-permute-done.2.rest_2_ = bf16[192,640]{1,0:T(8,128)(2,1)S(1)} collective-permute-done((bf16[192,640]{1,0:T(8,128)(2,1)}, bf16[192,640]{1,0:T(8,128)(2,1)S(1)}, u32[]{:S(2)}, u32[]{:S(2)}) %collective-permute-start.2) | collective-permute-done | bytes 245792 | tf_op jit(solution)/shard_map/ppermute | solution.py:89
  36.3 19.7 %collective-permute-done.3.rest_3_ = bf16[192,640]{1,0:T(8,128)(2,1)S(1)} collective-permute-done((bf16[192,640]{1,0:T(8,128)(2,1)}, bf16[192,640]{1,0:T(8,128)(2,1)S(1)}, u32[]{:S(2)}, u32[]{:S(2)}) %collective-permute-start.3) | collective-permute-done | bytes 245792 | tf_op jit(solution)/shard_map/ppermute | solution.py:89
  57.3 2.5 collective-permute-start.4
  62.1 8.8 %collective-permute-done.5.rest_2_.refs_4_ = bf16[768,256]{1,0:T(8,128)(2,1)S(1)} collective-permute-done((bf16[768,256]{1,0:T(8,128)(2,1)S(1)}, bf16[768,256]{1,0:T(8,128)(2,1)S(1)}, u32[]{:S(2)}, u32[]{:S(2)}) %collective-permute-start.5) | collective-permute-done | bytes 393248 | tf_op jit(solution)/shard_map/ppermute | solution.py:29
  77.7 3.0 %collective-permute-done.8.rest_1_ = s32[4,7]{1,0:T(4,128)S(1)} collective-permute-done((s32[4,7]{1,0:T(4,128)S(1)}, s32[4,7]{1,0:T(4,128)S(1)}, u32[]{:S(2)}, u32[]{:S(2)}) %collective-permute-start.8) | collective-permute-done | bytes 144 | tf_op jit(solution)/shard_map/ppermute | solution.py:29
  82.8 9.3 %attend.1 = (bf16[768,256]{1,0:T(8,128)(2,1)S(1)}, bf16[768,256]{1,0:T(8,128)(2,1)S(1)}, bf16[1536,256]{1,0:T(8,128)(2,1)S(1)}, bf16[192,1024]{1,0:T(8,128)(2,1)...) custom-call(bf16[768,768]{1,0:T(8,128)(2,1)S(1)} %copy-done, ...), custom_call_target="tpu_custom_call" | custom-call | bytes 6201344 | tf_op jit(solution)/shard_map/attend/pallas_call | solution.py:209
  92.2 2.3 collective-permute-done.9.near
  96.7 9.9 %collective-permute-done.10.far = bf16[768,256]{1,0:T(8,128)(2,1)S(1)} collective-permute-done((bf16[768,256]{1,0:T(8,128)(2,1)S(1)}, bf16[768,256]{1,0:T(8,128)(2,1)S(1)}, u32[]{:S(2)}, u32[]{:S(2)}) %collective-permute-start.10) | collective-permute-done | bytes 393248 | tf_op jit(solution)/shard_map/ppermute | solution.py:29
  109.0 6.1 %collective-permute-done.13.rest_5_.refs_14_ = bf16[768,256]{1,0:T(8,128)(2,1)S(1)} collective-permute-done((bf16[768,256]{1,0:T(8,128)(2,1)S(1)}, bf16[768,256]{1,0:T(8,128)(2,1)S(1)}, u32[]{:S(2)}, u32[]{:S(2)}) %collective-permute-start.13) | collective-permute-done | bytes 393248 | tf_op jit(solution)/shard_map/ppermute | solution.py:29
  115.6 7.1 %collective-permute-done.12.rest_4_.refs_6_ = bf16[768,256]{1,0:T(8,128)(2,1)S(1)} collective-permute-done((bf16[768,256]{1,0:T(8,128)(2,1)S(1)}, bf16[768,256]{1,0:T(8,128)(2,1)S(1)}, u32[]{:S(2)}, u32[]{:S(2)}) %collective-permute-start.12) | collective-permute-done | bytes 393248 | tf_op jit(solution)/shard_map/ppermute | solution.py:29
  126.1 10.2 %feed_first.1 = (bf16[768,256]{1,0:T(8,128)(2,1)}, bf16[768,256]{1,0:T(8,128)(2,1)}, bf16[1536,256]{1,0:T(8,128)(2,1)}, bf16[768,256]{1,0:T(8,128)(2,1)}, bf16[7...) custom-call(bf16[768,1536]{1,0:T(8,128)(2,1)} %all-gather.5.cloned.1, ...), custom_call_target="tpu_custom_call" | custom-call | bytes 11798016 | tf_op jit(solution)/shard_map/feed_first/pallas_call | solution.py:209
  136.3 2.5 collective-permute-done.16.near
  141.5 7.5 %feed_grads.1 = bf16[4,208,1536]{2,1,0:T(8,128)(2,1)} custom-call(bf16[768,256]{1,0:T(8,128)(2,1)} %get-tuple-element.160.refs_0_, bf16[768,256]{1,0:T(8,128)(2,1)} %get-tuple-element.161.refs_1_, bf16[768,256]{1,0:T(8,128)(2,1)} %get-tuple-element.162.refs_2_, bf16[768,256]{1,0:T(8,128)(2,1)} %get-tuple-element.163.refs_3_, bf16[768,256]{1,0:T(8,128)(2,1)} %copy-done.4, ...), custom_call_target="tpu_custom_call" | custom-call | bytes 8847360 | tf_op jit(solution)/shard_map/feed_grads/pallas_call | solution.py:251
  156.6 8.0 %attend_back_first.1 = (bf16[192,512]{1,0:T(8,128)(2,1)}, f32[192,1024]{1,0:T(8,128)}, f32[192,1024]{1,0:T(8,128)}) custom-call(bf16[192,1024]{1,0:T(8,128)(2,1)} %copy-done.13, bf16[192,1024]{1,0:T(8,128)(2,1)} %copy-done.14, bf16[768,768]{1,0:T(8,128)(2,1)} %all-gather.3.cloned.1.call-done.weight_all, bf16[768,256]{1,0:T(8,128)(2,1)} %copy-done.5, ...), custom_call_target="tpu_custom_call" | custom-call | bytes 5611520 | tf_op jit(solution)/shard_map/attend_back_first/pallas_call | solution.py:209
  168.1 10.2 %attend_back_last.1 = (bf16[768,256]{1,0:T(8,128)(2,1)}, bf16[768,256]{1,0:T(8,128)(2,1)}, bf16[1536,256]{1,0:T(8,128)(2,1)}, bf16[576,1024]{1,0:T(8,128)(2,1)}) custom-call(bf16[192,1024]{1,0:T(8,128)(2,1)} %copy-done.13, bf16[192,1024]{1,0:T(8,128)(2,1)} %copy-done.14, bf16[768,768]{1,0:T(8,128)(2,1)} %all-gather.3.cloned.1.call-done.weight_all, ...), custom_call_target="tpu_custom_call" | custom-call | bytes 8364032 | tf_op jit(solution)/shard_map/attend_back_last/pallas_call | solution.py:209
  178.5 2.3 collective-permute-done.23.near
  183.5 6.2 %attend_weights.1 = (bf16[4,96,768]{2,1,0:T(8,128)(2,1)}, bf16[4,96,768]{2,1,0:T(8,128)(2,1)}) custom-call(bf16[576,1024]{1,0:T(8,128)(2,1)} %get-tuple-element.192.refs_0_, bf16[192,1024]{1,0:T(8,128)(2,1)} %copy-done.3, bf16[768,256]{1,0:T(8,128)(2,1)} %copy-done.6, bf16[768,256]{1,0:T(8,128)(2,1)} %copy-done.7, bf16[768,256]{1,0:T(8,128)(2,1)} %copy-done.8, ...), custom_call_target="tpu_custom_call" | custom-call | bytes 5898240 | tf_op jit(solution)/shard_map/attend_weights/pallas_call | solution.py:251
  196.5 6.6 %collective-permute-start.26 = (bf16[192,384]{1,0:T(8,128)(2,1)S(1)}, bf16[192,384]{1,0:T(8,128)(2,1)S(1)}, u32[]{:S(2)}, u32[]{:S(2)}) collective-permute-start(bf16[192,384]{1,0:T(8,128)(2,1)S(1)} %get-tuple-element.209), channel_id=1, source_target_pairs={{4,0},{8,1},{12,2},{0,3},{6,4},{10,5},{14,6},{2,7},{5,8},{9,9},{13... | collective-permute-start | bytes 442376 | tf_op jit(solution)/shard_map/ppermute | solution.py:89
  203.5 3.9 %collective-permute-start.28 = (bf16[192,384]{1,0:T(8,128)(2,1)S(1)}, bf16[192,384]{1,0:T(8,128)(2,1)S(1)}, u32[]{:S(2)}, u32[]{:S(2)}) collective-permute-start(bf16[192,384]{1,0:T(8,128)(2,1)S(1)} %get-tuple-element.211), channel_id=1, source_target_pairs={{12,0},{0,1},{4,2},{8,3},{14,4},{2,5},{6,6},{10,7},{13,8},{1,9},{5... | collective-permute-start | bytes 442376 | tf_op jit(solution)/shard_map/ppermute | solution.py:89
  207.4 2.7 %collective-permute-done.27.rest_2_ = bf16[192,384]{1,0:T(8,128)(2,1)S(1)} collective-permute-done((bf16[192,384]{1,0:T(8,128)(2,1)S(1)}, bf16[192,384]{1,0:T(8,128)(2,1)S(1)}, u32[]{:S(2)}, u32[]{:S(2)}) %collective-permute-start.27) | collective-permute-done | bytes 147488 | tf_op jit(solution)/shard_map/ppermute | solution.py:89
  214.1 6.6 %collective-permute-start.33 = (f32[1,64,192]{2,1,0:T(8,128)S(1)}, f32[1,64,192]{2,1,0:T(8,128)S(1)}, u32[]{:S(2)}, u32[]{:S(2)}) collective-permute-start(f32[1,64,192]{2,1,0:T(8,128)S(1)} %get-tuple-element.217), channel_id=1, source_target_pairs={{0,4},{4,0},{8,12},{12,8},{1,5},{5,1},{9,13},{13,9},{2,6},{6,2},{1... | collective-permute-start | bytes 147464 | tf_op jit(solution)/shard_map/ppermute | solution.py:29
  221.0 4.3 %collective-permute-start.43 = (bf16[96,768]{1,0:T(8,128)(2,1)S(1)}, bf16[96,768]{1,0:T(8,128)(2,1)S(1)}, u32[]{:S(2)}, u32[]{:S(2)}) collective-permute-start(bf16[96,768]{1,0:T(8,128)(2,1)S(1)} %get-tuple-element.228), channel_id=1, source_target_pairs={{0,3},{1,2},{2,1},{3,0},{4,7},{5,6},{6,5},{7,4},{8,11},{9,10},{10,... | collective-permute-start | bytes 442376 | tf_op jit(solution)/shard_map/ppermute | solution.py:29
  228.0 9.2 %collective-permute-done.42.rest_2_ = bf16[96,768]{1,0:T(8,128)(2,1)S(1)} collective-permute-done((bf16[96,768]{1,0:T(8,128)(2,1)S(1)}, bf16[96,768]{1,0:T(8,128)(2,1)S(1)}, u32[]{:S(2)}, u32[]{:S(2)}) %collective-permute-start.42) | collective-permute-done | bytes 147488 | tf_op jit(solution)/shard_map/ppermute | solution.py:29
  239.4 4.3 %collective-permute-start.30 = (bf16[192,256]{1,0:T(8,128)(2,1)S(1)}, bf16[192,256]{1,0:T(8,128)(2,1)S(1)}, u32[]{:S(2)}, u32[]{:S(2)}) collective-permute-start(bf16[192,256]{1,0:T(8,128)(2,1)S(1)} %get-tuple-element.213), channel_id=1, source_target_pairs={{4,0},{8,1},{12,2},{0,3},{6,4},{10,5},{14,6},{2,7},{5,8},{9,9},{13... | collective-permute-start | bytes 294920 | tf_op jit(solution)/shard_map/ppermute | solution.py:89
  244.5 4.6 %collective-permute-start.32 = (bf16[192,256]{1,0:T(8,128)(2,1)S(1)}, bf16[192,256]{1,0:T(8,128)(2,1)S(1)}, u32[]{:S(2)}, u32[]{:S(2)}) collective-permute-start(bf16[192,256]{1,0:T(8,128)(2,1)S(1)} %get-tuple-element.215), channel_id=1, source_target_pairs={{12,0},{0,1},{4,2},{8,3},{14,4},{2,5},{6,6},{10,7},{13,8},{1,9},{5... | collective-permute-start | bytes 294920 | tf_op jit(solution)/shard_map/ppermute | solution.py:89
  249.2 2.6 modulation_back.1
  253.7 2.7 collective-permute-start.37
  (188 shorter events, 68.4 us)
Async XLA Ops:
  7.2 66.0 %all-gather.3.cloned.1.call-start = ((), (), s32[]{:S(2)}) async-start(), calls=%async_computation.1 | async-start | bytes 1327104 | tf_op jit(solution)/shard_map/all_gather | solution.py:848
  14.1 112.0 %all-gather.5.cloned.1.call-start = ((), (), s32[]{:S(2)}) async-start(), calls=%async_computation.2 | async-start | bytes 2654208 | tf_op jit(solution)/shard_map/all_gather | solution.py:848
  14.2 15.2 %collective-permute-start.1 = (bf16[192,640]{1,0:T(8,128)(2,1)}, bf16[192,640]{1,0:T(8,128)(2,1)S(1)}, u32[]{:S(2)}, u32[]{:S(2)}) collective-permute-start(bf16[192,640]{1,0:T(8,128)(2,1)} %get-tuple-element.128), channel_id=1, source_target_pairs={{0,4},{1,8},{2,12},{3,0},{4,6},{5,10},{6,14},{7,2},{8,5},{9,9},{10... | collective-permute-start | bytes 737288 | tf_op jit(solution)/shard_map/ppermute | solution.py:89
  16.5 19.7 %collective-permute-start.2 = (bf16[192,640]{1,0:T(8,128)(2,1)}, bf16[192,640]{1,0:T(8,128)(2,1)S(1)}, u32[]{:S(2)}, u32[]{:S(2)}) collective-permute-start(bf16[192,640]{1,0:T(8,128)(2,1)} %get-tuple-element.129), channel_id=1, source_target_pairs={{0,8},{1,12},{2,0},{3,4},{4,10},{5,14},{6,2},{7,6},{8,9},{9,13},{1... | collective-permute-start | bytes 737288 | tf_op jit(solution)/shard_map/ppermute | solution.py:89
  20.1 35.9 %collective-permute-start.3 = (bf16[192,640]{1,0:T(8,128)(2,1)}, bf16[192,640]{1,0:T(8,128)(2,1)S(1)}, u32[]{:S(2)}, u32[]{:S(2)}) collective-permute-start(bf16[192,640]{1,0:T(8,128)(2,1)} %get-tuple-element.130), channel_id=1, source_target_pairs={{0,12},{1,0},{2,4},{3,8},{4,14},{5,2},{6,6},{7,10},{8,13},{9,1},{1... | collective-permute-start | bytes 737288 | tf_op jit(solution)/shard_map/ppermute | solution.py:89
  24.6 31.3 %collective-permute-start = (bf16[192,640]{1,0:T(8,128)(2,1)}, bf16[192,640]{1,0:T(8,128)(2,1)S(1)}, u32[]{:S(2)}, u32[]{:S(2)}) collective-permute-start(bf16[192,640]{1,0:T(8,128)(2,1)} %get-tuple-element.127), channel_id=1, source_target_pairs={{0,0},{1,4},{2,8},{3,12},{4,2},{5,6},{6,10},{7,14},{8,1},{9,5},{10... | collective-permute-start | bytes 737288 | tf_op jit(solution)/shard_map/ppermute | solution.py:89
  59.8 11.1 %collective-permute-start.5 = (bf16[768,256]{1,0:T(8,128)(2,1)S(1)}, bf16[768,256]{1,0:T(8,128)(2,1)S(1)}, u32[]{:S(2)}, u32[]{:S(2)}) collective-permute-start(bf16[768,256]{1,0:T(8,128)(2,1)S(1)} %get-tuple-element.137.rest_0_.refs_2_), channel_id=1, source_target_pairs={{0,8},{4,12},{8,0},{12,4},{1,9},{5,13},{9,1},{13,5},{2,10},{6,14},... | collective-permute-start | bytes 1179656 | tf_op jit(solution)/shard_map/ppermute | solution.py:29
  74.9 136.8 %reduce-scatter.2.cloned.1.call-start = ((), (), s32[]{:S(2)}) async-start(), calls=%async_computation.3 | async-start | bytes 3194880 | tf_op jit(solution)/shard_map/reduce_scatter | solution.py:915
  94.6 12.0 %collective-permute-start.10 = (bf16[768,256]{1,0:T(8,128)(2,1)S(1)}, bf16[768,256]{1,0:T(8,128)(2,1)S(1)}, u32[]{:S(2)}, u32[]{:S(2)}) collective-permute-start(bf16[768,256]{1,0:T(8,128)(2,1)S(1)} %add_convert_fusion.3), channel_id=1, source_target_pairs={{0,8},{4,12},{8,0},{12,4},{1,9},{5,13},{9,1},{13,5},{2,10},{6,14},... | collective-permute-start | bytes 1179656 | tf_op jit(solution)/shard_map/ppermute | solution.py:29
  96.2 18.9 %collective-permute-start.13 = (bf16[768,256]{1,0:T(8,128)(2,1)S(1)}, bf16[768,256]{1,0:T(8,128)(2,1)S(1)}, u32[]{:S(2)}, u32[]{:S(2)}) collective-permute-start(bf16[768,256]{1,0:T(8,128)(2,1)S(1)} %branch_grad.1.rest_1_.refs_12_), channel_id=1, source_target_pairs={{0,8},{4,12},{8,0},{12,4},{1,9},{5,13},{9,1},{13,5},{2,10},{6,14},... | collective-permute-start | bytes 1179656 | tf_op jit(solution)/shard_map/ppermute | solution.py:29
  107.4 15.3 %collective-permute-start.12 = (bf16[768,256]{1,0:T(8,128)(2,1)S(1)}, bf16[768,256]{1,0:T(8,128)(2,1)S(1)}, u32[]{:S(2)}, u32[]{:S(2)}) collective-permute-start(bf16[768,256]{1,0:T(8,128)(2,1)S(1)} %get-tuple-element.152.rest_0_.refs_4_), channel_id=1, source_target_pairs={{0,8},{4,12},{8,0},{12,4},{1,9},{5,13},{9,1},{13,5},{2,10},{6,14},... | collective-permute-start | bytes 1179656 | tf_op jit(solution)/shard_map/ppermute | solution.py:29
  115.1 7.6 %collective-permute-start.15 = (bf16[768,256]{1,0:T(8,128)(2,1)S(1)}, bf16[768,256]{1,0:T(8,128)(2,1)S(1)}, u32[]{:S(2)}, u32[]{:S(2)}) collective-permute-start(bf16[768,256]{1,0:T(8,128)(2,1)S(1)} %collective-permute-done.13.rest_5_.refs_14_), channel_id=1, source_target_pairs={{0,4},{4,0},{8,12},{12,8},{1,5},{5,1},{9,13},{13,9},{2,6},{6,2},{1... | collective-permute-start | bytes 1179656 | tf_op jit(solution)/shard_map/ppermute | solution.py:29
  115.1 7.6 %collective-permute-start.11 = (bf16[768,256]{1,0:T(8,128)(2,1)S(1)}, bf16[768,256]{1,0:T(8,128)(2,1)S(1)}, u32[]{:S(2)}, u32[]{:S(2)}) collective-permute-start(bf16[768,256]{1,0:T(8,128)(2,1)S(1)} %get-tuple-element.152.rest_0_.refs_4_), channel_id=1, source_target_pairs={{0,4},{4,0},{8,12},{12,8},{1,5},{5,1},{9,13},{13,9},{2,6},{6,2},{1... | collective-permute-start | bytes 1179656 | tf_op jit(solution)/shard_map/ppermute | solution.py:29
  140.0 11.2 %collective-permute-start.17 = (bf16[768,256]{1,0:T(8,128)(2,1)S(1)}, bf16[768,256]{1,0:T(8,128)(2,1)S(1)}, u32[]{:S(2)}, u32[]{:S(2)}) collective-permute-start(bf16[768,256]{1,0:T(8,128)(2,1)S(1)} %add_convert_fusion.2), channel_id=1, source_target_pairs={{0,8},{4,12},{8,0},{12,4},{1,9},{5,13},{9,1},{13,5},{2,10},{6,14},... | collective-permute-start | bytes 1179656 | tf_op jit(solution)/shard_map/ppermute | solution.py:29
  151.2 14.5 %collective-permute-start.21 = (bf16[1536,256]{1,0:T(8,128)(2,1)}, bf16[1536,256]{1,0:T(8,128)(2,1)S(1)}, u32[]{:S(2)}, u32[]{:S(2)}) collective-permute-start(bf16[1536,256]{1,0:T(8,128)(2,1)} %get-tuple-element.189), channel_id=1, source_target_pairs={{0,4},{4,0},{8,12},{12,8},{1,5},{5,1},{9,13},{13,9},{2,6},{6,2},{1... | collective-permute-start | bytes 2359304 | tf_op jit(solution)/shard_map/ppermute | solution.py:29
  154.1 11.5 %collective-permute-start.18 = (bf16[768,256]{1,0:T(8,128)(2,1)S(1)}, bf16[768,256]{1,0:T(8,128)(2,1)S(1)}, u32[]{:S(2)}, u32[]{:S(2)}) collective-permute-start(bf16[768,256]{1,0:T(8,128)(2,1)S(1)} %get-tuple-element.174.first.refs_6_), channel_id=1, source_target_pairs={{0,8},{4,12},{8,0},{12,4},{1,9},{5,13},{9,1},{13,5},{2,10},{6,14},... | collective-permute-start | bytes 1179656 | tf_op jit(solution)/shard_map/ppermute | solution.py:29
  165.8 12.5 %collective-permute-start.22 = (bf16[768,256]{1,0:T(8,128)(2,1)S(1)}, bf16[768,256]{1,0:T(8,128)(2,1)S(1)}, u32[]{:S(2)}, u32[]{:S(2)}) collective-permute-start(bf16[768,256]{1,0:T(8,128)(2,1)S(1)} %add_convert_fusion.1), channel_id=1, source_target_pairs={{0,8},{4,12},{8,0},{12,4},{1,9},{5,13},{9,1},{13,5},{2,10},{6,14},... | collective-permute-start | bytes 1179656 | tf_op jit(solution)/shard_map/ppermute | solution.py:29
  182.0 11.3 %collective-permute-start.24 = (bf16[768,256]{1,0:T(8,128)(2,1)S(1)}, bf16[768,256]{1,0:T(8,128)(2,1)S(1)}, u32[]{:S(2)}, u32[]{:S(2)}) collective-permute-start(bf16[768,256]{1,0:T(8,128)(2,1)S(1)} %add_convert_fusion), channel_id=1, source_target_pairs={{0,8},{4,12},{8,0},{12,4},{1,9},{5,13},{9,1},{13,5},{2,10},{6,14},... | collective-permute-start | bytes 1179656 | tf_op jit(solution)/shard_map/ppermute | solution.py:29
  193.2 27.4 %collective-permute-start.40 = (bf16[4,96,768]{2,1,0:T(8,128)(2,1)S(1)}, bf16[4,96,768]{2,1,0:T(8,128)(2,1)S(1)}, u32[]{:S(2)}, u32[]{:S(2)}) collective-permute-start(bf16[4,96,768]{2,1,0:T(8,128)(2,1)S(1)} %copy-done.42), channel_id=1, source_target_pairs={{0,16},{16,0},{1,17},{17,1},{2,18},{18,2},{3,19},{19,3},{4,20},{20... | collective-permute-start | bytes 1769480 | tf_op jit(solution)/shard_map/ppermute | solution.py:29
  195.8 11.6 %collective-permute-start.25 = (bf16[192,384]{1,0:T(8,128)(2,1)S(1)}, bf16[192,384]{1,0:T(8,128)(2,1)S(1)}, u32[]{:S(2)}, u32[]{:S(2)}) collective-permute-start(bf16[192,384]{1,0:T(8,128)(2,1)S(1)} %get-tuple-element.208), channel_id=1, source_target_pairs={{0,0},{4,1},{8,2},{12,3},{2,4},{6,5},{10,6},{14,7},{1,8},{5,9},{9,... | collective-permute-start | bytes 442376 | tf_op jit(solution)/shard_map/ppermute | solution.py:89
  196.5 10.9 %collective-permute-start.26 = (bf16[192,384]{1,0:T(8,128)(2,1)S(1)}, bf16[192,384]{1,0:T(8,128)(2,1)S(1)}, u32[]{:S(2)}, u32[]{:S(2)}) collective-permute-start(bf16[192,384]{1,0:T(8,128)(2,1)S(1)} %get-tuple-element.209), channel_id=1, source_target_pairs={{4,0},{8,1},{12,2},{0,3},{6,4},{10,5},{14,6},{2,7},{5,8},{9,9},{13... | collective-permute-start | bytes 442376 | tf_op jit(solution)/shard_map/ppermute | solution.py:89
  203.5 8.2 %collective-permute-start.28 = (bf16[192,384]{1,0:T(8,128)(2,1)S(1)}, bf16[192,384]{1,0:T(8,128)(2,1)S(1)}, u32[]{:S(2)}, u32[]{:S(2)}) collective-permute-start(bf16[192,384]{1,0:T(8,128)(2,1)S(1)} %get-tuple-element.211), channel_id=1, source_target_pairs={{12,0},{0,1},{4,2},{8,3},{14,4},{2,5},{6,6},{10,7},{13,8},{1,9},{5... | collective-permute-start | bytes 442376 | tf_op jit(solution)/shard_map/ppermute | solution.py:89
  211.7 49.7 %collective-permute-start.45 = (bf16[208,1536]{1,0:T(8,128)(2,1)}, bf16[208,1536]{1,0:T(8,128)(2,1)S(1)}, u32[]{:S(2)}, u32[]{:S(2)}) collective-permute-start(bf16[208,1536]{1,0:T(8,128)(2,1)} %reduce-scatter.2.cloned.1.call-done.rest_0_), channel_id=1, source_target_pairs={{0,16},{16,0},{1,17},{17,1},{2,18},{18,2},{3,19},{19,3},{4,20},{20... | collective-permute-start | bytes 1916936 | tf_op jit(solution)/shard_map/ppermute | solution.py:29
  214.1 11.2 %collective-permute-start.33 = (f32[1,64,192]{2,1,0:T(8,128)S(1)}, f32[1,64,192]{2,1,0:T(8,128)S(1)}, u32[]{:S(2)}, u32[]{:S(2)}) collective-permute-start(f32[1,64,192]{2,1,0:T(8,128)S(1)} %get-tuple-element.217), channel_id=1, source_target_pairs={{0,4},{4,0},{8,12},{12,8},{1,5},{5,1},{9,13},{13,9},{2,6},{6,2},{1... | collective-permute-start | bytes 147464 | tf_op jit(solution)/shard_map/ppermute | solution.py:29
  220.9 16.3 %collective-permute-start.42 = (bf16[96,768]{1,0:T(8,128)(2,1)S(1)}, bf16[96,768]{1,0:T(8,128)(2,1)S(1)}, u32[]{:S(2)}, u32[]{:S(2)}) collective-permute-start(bf16[96,768]{1,0:T(8,128)(2,1)S(1)} %get-tuple-element.227), channel_id=1, source_target_pairs={{0,2},{1,3},{2,0},{3,1},{4,6},{5,7},{6,4},{7,5},{8,10},{9,11},{10,... | collective-permute-start | bytes 442376 | tf_op jit(solution)/shard_map/ppermute | solution.py:29
  221.0 16.8 %collective-permute-start.43 = (bf16[96,768]{1,0:T(8,128)(2,1)S(1)}, bf16[96,768]{1,0:T(8,128)(2,1)S(1)}, u32[]{:S(2)}, u32[]{:S(2)}) collective-permute-start(bf16[96,768]{1,0:T(8,128)(2,1)S(1)} %get-tuple-element.228), channel_id=1, source_target_pairs={{0,3},{1,2},{2,1},{3,0},{4,7},{5,6},{6,5},{7,4},{8,11},{9,10},{10,... | collective-permute-start | bytes 442376 | tf_op jit(solution)/shard_map/ppermute | solution.py:29
  225.3 12.5 %collective-permute-start.29 = (bf16[192,256]{1,0:T(8,128)(2,1)S(1)}, bf16[192,256]{1,0:T(8,128)(2,1)S(1)}, u32[]{:S(2)}, u32[]{:S(2)}) collective-permute-start(bf16[192,256]{1,0:T(8,128)(2,1)S(1)} %get-tuple-element.212), channel_id=1, source_target_pairs={{0,0},{4,1},{8,2},{12,3},{2,4},{6,5},{10,6},{14,7},{1,8},{5,9},{9,... | collective-permute-start | bytes 294920 | tf_op jit(solution)/shard_map/ppermute | solution.py:89
  228.0 11.4 %collective-permute-start.36 = (f32[2,64,192]{2,1,0:T(8,128)S(1)}, f32[2,64,192]{2,1,0:T(8,128)S(1)}, u32[]{:S(2)}, u32[]{:S(2)}) collective-permute-start(f32[2,64,192]{2,1,0:T(8,128)S(1)} %constant_dynamic-update-slice_fusion.rest_4_), channel_id=1, source_target_pairs={{0,24},{4,28},{8,16},{12,20},{16,8},{20,12},{24,0},{28,4},{1,25},{... | collective-permute-start | bytes 294920 | tf_op jit(solution)/shard_map/ppermute | solution.py:990
  237.8 22.5 %collective-permute-start.44 = (bf16[96,768]{1,0:T(8,128)(2,1)S(1)}, bf16[96,768]{1,0:T(8,128)(2,1)S(1)}, u32[]{:S(2)}, u32[]{:S(2)}) collective-permute-start(bf16[96,768]{1,0:T(8,128)(2,1)S(1)} %block_sum.1.own), channel_id=1, source_target_pairs={{0,16},{16,0},{1,17},{17,1},{2,18},{18,2},{3,19},{19,3},{4,20},{20... | collective-permute-start | bytes 442376 | tf_op jit(solution)/shard_map/ppermute | solution.py:29
  239.4 12.4 %collective-permute-start.30 = (bf16[192,256]{1,0:T(8,128)(2,1)S(1)}, bf16[192,256]{1,0:T(8,128)(2,1)S(1)}, u32[]{:S(2)}, u32[]{:S(2)}) collective-permute-start(bf16[192,256]{1,0:T(8,128)(2,1)S(1)} %get-tuple-element.213), channel_id=1, source_target_pairs={{4,0},{8,1},{12,2},{0,3},{6,4},{10,5},{14,6},{2,7},{5,8},{9,9},{13... | collective-permute-start | bytes 294920 | tf_op jit(solution)/shard_map/ppermute | solution.py:89
  243.7 9.4 %collective-permute-start.31 = (bf16[192,256]{1,0:T(8,128)(2,1)S(1)}, bf16[192,256]{1,0:T(8,128)(2,1)S(1)}, u32[]{:S(2)}, u32[]{:S(2)}) collective-permute-start(bf16[192,256]{1,0:T(8,128)(2,1)S(1)} %get-tuple-element.214), channel_id=1, source_target_pairs={{8,0},{12,1},{0,2},{4,3},{10,4},{14,5},{2,6},{6,7},{9,8},{13,9},{1... | collective-permute-start | bytes 294920 | tf_op jit(solution)/shard_map/ppermute | solution.py:89
  244.5 9.1 %collective-permute-start.32 = (bf16[192,256]{1,0:T(8,128)(2,1)S(1)}, bf16[192,256]{1,0:T(8,128)(2,1)S(1)}, u32[]{:S(2)}, u32[]{:S(2)}) collective-permute-start(bf16[192,256]{1,0:T(8,128)(2,1)S(1)} %get-tuple-element.215), channel_id=1, source_target_pairs={{12,0},{0,1},{4,2},{8,3},{14,4},{2,5},{6,6},{10,7},{13,8},{1,9},{5... | collective-permute-start | bytes 294920 | tf_op jit(solution)/shard_map/ppermute | solution.py:89
  (60 other events, 960.8 us)
Sparse Core Ops, SparseCore 0:
  14.3 58.8 all-gather.2
  75.3 50.6 all-gather.4
  151.3 49.6 reduce-scatter.1

commit v5 on v4

--- a/solution.py
+++ b/solution.py
@@ -21,7 +21,7 @@
 GAIN_ONE, GAIN_TWO, DOWN_BIAS = 48, 49, 50
 STATS = 51
 VMEM_LIMIT = 56 * 1024 * 1024
-NEAR = {'unbundle': 12, 'modulation_back': 12, 'table_sum': 12, 'attn_weight_out': 12, 'feed_weight_out': 12, 'pair_sum': 12, 'block_sum': 12, 'join': 12, 'finish_forward': 12, 'finish_backward': 12, 'feed_first': 56, 'attend_back_first': 56, 'attend_back_last': 56, 'second_norm': 12, 'middle_grad': 12, 'branch_grad': 12, 'first_norm': 12, 'attend': 40}
+NEAR = {'unbundle': 12, 'modulation_back': 12, 'table_sum': 12, 'attn_weight_out': 12, 'feed_weight_out': 12, 'pair_sum': 12, 'block_sum': 12, 'join': 12, 'finish_forward': 12, 'finish_backward': 12, 'feed_first': 56, 'attend_back_first': 56, 'attend_back_last': 56, 'second_norm': 20, 'middle_grad': 20, 'branch_grad': 12, 'first_norm': 12, 'attend': 44}
 
 
 def swap(values, axis, bit):

time: 273 us -> 273 us (level)
  no operation moved by 1% of the time
where the time goes in v5:
time: 273 us; the launch traced here: 269 us
  waiting for transfers between devices  98.8 us (36%)
  Pallas kernels  73.9 us (27%)
  starting transfers between devices  68 us (25%)
  between operations  14.6 us (5%)
  local copies, waits for them, and re-layouts  10.7 us (4%)
  other arithmetic  3.2 us (1%)
    ppermute x31, waiting for transfers between devices, swap(): return lax.ppermute(values, axis, [(i, i ^ bit) for i in range(count)])  64 us
    pallas_call x18, Pallas kernels, run(): pl.pallas_call(body, out_shape=list(outs), in_specs=[whole(pltpu.SMEM)] *...  52.5 us
    ppermute x12, starting transfers between devices, relayout(): got.append(lax.ppermute(piece, ('row', 'col'), pairs))  34 us
    ppermute x31, starting transfers between devices, swap(): return lax.ppermute(values, axis, [(i, i ^ bit) for i in range(count)])  33.2 us
    ppermute x12, waiting for transfers between devices, relayout(): got.append(lax.ppermute(piece, ('row', 'col'), pairs))  30.9 us
    pallas_call x5, Pallas kernels, run(): pl.pallas_call(kernel, out_shape=outs, in_specs=[whole(pltpu.SMEM)] * sme...  21.4 us
    unnamed x87, local copies, waits for them, and re-layouts  7.51 us
  transfers between devices with their start and end apart: 49, of which 27 were waited for; matrix products, arithmetic and copies ran while one was open for 1% of the time, Pallas kernels for 21%

profile of v5, /device:TPU:0, one launch (start us, length us, event | category | flops | bytes accessed | tf_op | source)
XLA Modules:
  0.0 269.2 jit_solution(7891851032563648537)
XLA Ops:
  7.2 3.3 %prepare.1 = (bf16[192,640]{1,0:T(8,128)(2,1)}, bf16[192,640]{1,0:T(8,128)(2,1)}, bf16[192,640]{1,0:T(8,128)(2,1)}, bf16[192,640]{1,0:T(8,128)(2,1)}) custom-call(s32[4,7]{1,0:T(4,128)} %rest_0_.3, f32[256,128]{1,0:T(8,128)} %rest_2_.1, bf16[6,192,128]{2,1,0:T(8,128)(2,1)} %rest_3_.1, bf16[6,192]{1,0:T(8,128)(2,1)} %refs_3_.1, bf16[192]{0:T(256)(128)(2,1)} %refs_4_.1, ...), custom_call_target="tpu_custom_call" | custom-call | bytes 2198912 | tf_op jit(solution)/shard_map/prepare/pallas_call | solution.py:251
  14.2 2.4 collective-permute-start.1
  16.5 3.5 %collective-permute-start.2 = (bf16[192,640]{1,0:T(8,128)(2,1)}, bf16[192,640]{1,0:T(8,128)(2,1)S(1)}, u32[]{:S(2)}, u32[]{:S(2)}) collective-permute-start(bf16[192,640]{1,0:T(8,128)(2,1)} %get-tuple-element.129), channel_id=1, source_target_pairs={{0,8},{1,12},{2,0},{3,4},{4,10},{5,14},{6,2},{7,6},{8,9},{9,13},{1... | collective-permute-start | bytes 737288 | tf_op jit(solution)/shard_map/ppermute | solution.py:89
  20.1 4.5 %collective-permute-start.3 = (bf16[192,640]{1,0:T(8,128)(2,1)}, bf16[192,640]{1,0:T(8,128)(2,1)S(1)}, u32[]{:S(2)}, u32[]{:S(2)}) collective-permute-start(bf16[192,640]{1,0:T(8,128)(2,1)} %get-tuple-element.130), channel_id=1, source_target_pairs={{0,12},{1,0},{2,4},{3,8},{4,14},{5,2},{6,6},{7,10},{8,13},{9,1},{1... | collective-permute-start | bytes 737288 | tf_op jit(solution)/shard_map/ppermute | solution.py:89
  26.8 2.5 places.1
  29.4 6.9 %collective-permute-done.2.rest_2_ = bf16[192,640]{1,0:T(8,128)(2,1)S(1)} collective-permute-done((bf16[192,640]{1,0:T(8,128)(2,1)}, bf16[192,640]{1,0:T(8,128)(2,1)S(1)}, u32[]{:S(2)}, u32[]{:S(2)}) %collective-permute-start.2) | collective-permute-done | bytes 245792 | tf_op jit(solution)/shard_map/ppermute | solution.py:89
  36.3 19.7 %collective-permute-done.3.rest_3_ = bf16[192,640]{1,0:T(8,128)(2,1)S(1)} collective-permute-done((bf16[192,640]{1,0:T(8,128)(2,1)}, bf16[192,640]{1,0:T(8,128)(2,1)S(1)}, u32[]{:S(2)}, u32[]{:S(2)}) %collective-permute-start.3) | collective-permute-done | bytes 245792 | tf_op jit(solution)/shard_map/ppermute | solution.py:89
  57.3 2.5 collective-permute-start.4
  62.1 8.8 %collective-permute-done.5.rest_2_.refs_4_ = bf16[768,256]{1,0:T(8,128)(2,1)S(1)} collective-permute-done((bf16[768,256]{1,0:T(8,128)(2,1)S(1)}, bf16[768,256]{1,0:T(8,128)(2,1)S(1)}, u32[]{:S(2)}, u32[]{:S(2)}) %collective-permute-start.5) | collective-permute-done | bytes 393248 | tf_op jit(solution)/shard_map/ppermute | solution.py:29
  77.7 3.0 %collective-permute-done.8.rest_1_ = s32[4,7]{1,0:T(4,128)S(1)} collective-permute-done((s32[4,7]{1,0:T(4,128)S(1)}, s32[4,7]{1,0:T(4,128)S(1)}, u32[]{:S(2)}, u32[]{:S(2)}) %collective-permute-start.8) | collective-permute-done | bytes 144 | tf_op jit(solution)/shard_map/ppermute | solution.py:29
  82.8 9.3 %attend.1 = (bf16[768,256]{1,0:T(8,128)(2,1)S(1)}, bf16[768,256]{1,0:T(8,128)(2,1)S(1)}, bf16[1536,256]{1,0:T(8,128)(2,1)S(1)}, bf16[192,1024]{1,0:T(8,128)(2,1)...) custom-call(bf16[768,768]{1,0:T(8,128)(2,1)S(1)} %copy-done, ...), custom_call_target="tpu_custom_call" | custom-call | bytes 6201344 | tf_op jit(solution)/shard_map/attend/pallas_call | solution.py:209
  92.2 2.3 collective-permute-done.9.near
  96.7 9.9 %collective-permute-done.10.far = bf16[768,256]{1,0:T(8,128)(2,1)S(1)} collective-permute-done((bf16[768,256]{1,0:T(8,128)(2,1)S(1)}, bf16[768,256]{1,0:T(8,128)(2,1)S(1)}, u32[]{:S(2)}, u32[]{:S(2)}) %collective-permute-start.10) | collective-permute-done | bytes 393248 | tf_op jit(solution)/shard_map/ppermute | solution.py:29
  109.0 6.1 %collective-permute-done.13.rest_5_.refs_14_ = bf16[768,256]{1,0:T(8,128)(2,1)S(1)} collective-permute-done((bf16[768,256]{1,0:T(8,128)(2,1)S(1)}, bf16[768,256]{1,0:T(8,128)(2,1)S(1)}, u32[]{:S(2)}, u32[]{:S(2)}) %collective-permute-start.13) | collective-permute-done | bytes 393248 | tf_op jit(solution)/shard_map/ppermute | solution.py:29
  115.6 7.1 %collective-permute-done.12.rest_4_.refs_6_ = bf16[768,256]{1,0:T(8,128)(2,1)S(1)} collective-permute-done((bf16[768,256]{1,0:T(8,128)(2,1)S(1)}, bf16[768,256]{1,0:T(8,128)(2,1)S(1)}, u32[]{:S(2)}, u32[]{:S(2)}) %collective-permute-start.12) | collective-permute-done | bytes 393248 | tf_op jit(solution)/shard_map/ppermute | solution.py:29
  126.1 10.2 %feed_first.1 = (bf16[768,256]{1,0:T(8,128)(2,1)}, bf16[768,256]{1,0:T(8,128)(2,1)}, bf16[1536,256]{1,0:T(8,128)(2,1)}, bf16[768,256]{1,0:T(8,128)(2,1)}, bf16[7...) custom-call(bf16[768,1536]{1,0:T(8,128)(2,1)} %all-gather.5.cloned.1, ...), custom_call_target="tpu_custom_call" | custom-call | bytes 11798016 | tf_op jit(solution)/shard_map/feed_first/pallas_call | solution.py:209
  136.3 2.5 collective-permute-done.16.near
  141.5 7.5 %feed_grads.1 = bf16[4,208,1536]{2,1,0:T(8,128)(2,1)} custom-call(bf16[768,256]{1,0:T(8,128)(2,1)} %get-tuple-element.160.refs_0_, bf16[768,256]{1,0:T(8,128)(2,1)} %get-tuple-element.161.refs_1_, bf16[768,256]{1,0:T(8,128)(2,1)} %get-tuple-element.162.refs_2_, bf16[768,256]{1,0:T(8,128)(2,1)} %get-tuple-element.163.refs_3_, bf16[768,256]{1,0:T(8,128)(2,1)} %copy-done.4, ...), custom_call_target="tpu_custom_call" | custom-call | bytes 8847360 | tf_op jit(solution)/shard_map/feed_grads/pallas_call | solution.py:251
  156.6 8.0 %attend_back_first.1 = (bf16[192,512]{1,0:T(8,128)(2,1)}, f32[192,1024]{1,0:T(8,128)}, f32[192,1024]{1,0:T(8,128)}) custom-call(bf16[192,1024]{1,0:T(8,128)(2,1)} %copy-done.13, bf16[192,1024]{1,0:T(8,128)(2,1)} %copy-done.14, bf16[768,768]{1,0:T(8,128)(2,1)} %all-gather.3.cloned.1.call-done.weight_all, bf16[768,256]{1,0:T(8,128)(2,1)} %copy-done.5, ...), custom_call_target="tpu_custom_call" | custom-call | bytes 5611520 | tf_op jit(solution)/shard_map/attend_back_first/pallas_call | solution.py:209
  168.1 10.2 %attend_back_last.1 = (bf16[768,256]{1,0:T(8,128)(2,1)}, bf16[768,256]{1,0:T(8,128)(2,1)}, bf16[1536,256]{1,0:T(8,128)(2,1)}, bf16[576,1024]{1,0:T(8,128)(2,1)}) custom-call(bf16[192,1024]{1,0:T(8,128)(2,1)} %copy-done.13, bf16[192,1024]{1,0:T(8,128)(2,1)} %copy-done.14, bf16[768,768]{1,0:T(8,128)(2,1)} %all-gather.3.cloned.1.call-done.weight_all, ...), custom_call_target="tpu_custom_call" | custom-call | bytes 8364032 | tf_op jit(solution)/shard_map/attend_back_last/pallas_call | solution.py:209
  178.5 2.3 collective-permute-done.23.near
  183.5 6.2 %attend_weights.1 = (bf16[4,96,768]{2,1,0:T(8,128)(2,1)}, bf16[4,96,768]{2,1,0:T(8,128)(2,1)}) custom-call(bf16[576,1024]{1,0:T(8,128)(2,1)} %get-tuple-element.192.refs_0_, bf16[192,1024]{1,0:T(8,128)(2,1)} %copy-done.3, bf16[768,256]{1,0:T(8,128)(2,1)} %copy-done.6, bf16[768,256]{1,0:T(8,128)(2,1)} %copy-done.7, bf16[768,256]{1,0:T(8,128)(2,1)} %copy-done.8, ...), custom_call_target="tpu_custom_call" | custom-call | bytes 5898240 | tf_op jit(solution)/shard_map/attend_weights/pallas_call | solution.py:251
  196.5 6.6 %collective-permute-start.26 = (bf16[192,384]{1,0:T(8,128)(2,1)S(1)}, bf16[192,384]{1,0:T(8,128)(2,1)S(1)}, u32[]{:S(2)}, u32[]{:S(2)}) collective-permute-start(bf16[192,384]{1,0:T(8,128)(2,1)S(1)} %get-tuple-element.209), channel_id=1, source_target_pairs={{4,0},{8,1},{12,2},{0,3},{6,4},{10,5},{14,6},{2,7},{5,8},{9,9},{13... | collective-permute-start | bytes 442376 | tf_op jit(solution)/shard_map/ppermute | solution.py:89
  203.5 3.9 %collective-permute-start.28 = (bf16[192,384]{1,0:T(8,128)(2,1)S(1)}, bf16[192,384]{1,0:T(8,128)(2,1)S(1)}, u32[]{:S(2)}, u32[]{:S(2)}) collective-permute-start(bf16[192,384]{1,0:T(8,128)(2,1)S(1)} %get-tuple-element.211), channel_id=1, source_target_pairs={{12,0},{0,1},{4,2},{8,3},{14,4},{2,5},{6,6},{10,7},{13,8},{1,9},{5... | collective-permute-start | bytes 442376 | tf_op jit(solution)/shard_map/ppermute | solution.py:89
  207.4 2.7 %collective-permute-done.27.rest_2_ = bf16[192,384]{1,0:T(8,128)(2,1)S(1)} collective-permute-done((bf16[192,384]{1,0:T(8,128)(2,1)S(1)}, bf16[192,384]{1,0:T(8,128)(2,1)S(1)}, u32[]{:S(2)}, u32[]{:S(2)}) %collective-permute-start.27) | collective-permute-done | bytes 147488 | tf_op jit(solution)/shard_map/ppermute | solution.py:89
  214.1 6.6 %collective-permute-start.33 = (f32[1,64,192]{2,1,0:T(8,128)S(1)}, f32[1,64,192]{2,1,0:T(8,128)S(1)}, u32[]{:S(2)}, u32[]{:S(2)}) collective-permute-start(f32[1,64,192]{2,1,0:T(8,128)S(1)} %get-tuple-element.217), channel_id=1, source_target_pairs={{0,4},{4,0},{8,12},{12,8},{1,5},{5,1},{9,13},{13,9},{2,6},{6,2},{1... | collective-permute-start | bytes 147464 | tf_op jit(solution)/shard_map/ppermute | solution.py:29
  221.0 4.3 %collective-permute-start.43 = (bf16[96,768]{1,0:T(8,128)(2,1)S(1)}, bf16[96,768]{1,0:T(8,128)(2,1)S(1)}, u32[]{:S(2)}, u32[]{:S(2)}) collective-permute-start(bf16[96,768]{1,0:T(8,128)(2,1)S(1)} %get-tuple-element.228), channel_id=1, source_target_pairs={{0,3},{1,2},{2,1},{3,0},{4,7},{5,6},{6,5},{7,4},{8,11},{9,10},{10,... | collective-permute-start | bytes 442376 | tf_op jit(solution)/shard_map/ppermute | solution.py:29
  228.0 9.2 %collective-permute-done.42.rest_2_ = bf16[96,768]{1,0:T(8,128)(2,1)S(1)} collective-permute-done((bf16[96,768]{1,0:T(8,128)(2,1)S(1)}, bf16[96,768]{1,0:T(8,128)(2,1)S(1)}, u32[]{:S(2)}, u32[]{:S(2)}) %collective-permute-start.42) | collective-permute-done | bytes 147488 | tf_op jit(solution)/shard_map/ppermute | solution.py:29
  239.4 4.3 %collective-permute-start.30 = (bf16[192,256]{1,0:T(8,128)(2,1)S(1)}, bf16[192,256]{1,0:T(8,128)(2,1)S(1)}, u32[]{:S(2)}, u32[]{:S(2)}) collective-permute-start(bf16[192,256]{1,0:T(8,128)(2,1)S(1)} %get-tuple-element.213), channel_id=1, source_target_pairs={{4,0},{8,1},{12,2},{0,3},{6,4},{10,5},{14,6},{2,7},{5,8},{9,9},{13... | collective-permute-start | bytes 294920 | tf_op jit(solution)/shard_map/ppermute | solution.py:89
  244.5 4.6 %collective-permute-start.32 = (bf16[192,256]{1,0:T(8,128)(2,1)S(1)}, bf16[192,256]{1,0:T(8,128)(2,1)S(1)}, u32[]{:S(2)}, u32[]{:S(2)}) collective-permute-start(bf16[192,256]{1,0:T(8,128)(2,1)S(1)} %get-tuple-element.215), channel_id=1, source_target_pairs={{12,0},{0,1},{4,2},{8,3},{14,4},{2,5},{6,6},{10,7},{13,8},{1,9},{5... | collective-permute-start | bytes 294920 | tf_op jit(solution)/shard_map/ppermute | solution.py:89
  249.2 2.6 modulation_back.1
  253.7 2.7 collective-permute-start.37
  (188 shorter events, 68.4 us)
Async XLA Ops:
  7.2 66.0 %all-gather.3.cloned.1.call-start = ((), (), s32[]{:S(2)}) async-start(), calls=%async_computation.1 | async-start | bytes 1327104 | tf_op jit(solution)/shard_map/all_gather | solution.py:848
  14.1 112.0 %all-gather.5.cloned.1.call-start = ((), (), s32[]{:S(2)}) async-start(), calls=%async_computation.2 | async-start | bytes 2654208 | tf_op jit(solution)/shard_map/all_gather | solution.py:848
  14.2 15.2 %collective-permute-start.1 = (bf16[192,640]{1,0:T(8,128)(2,1)}, bf16[192,640]{1,0:T(8,128)(2,1)S(1)}, u32[]{:S(2)}, u32[]{:S(2)}) collective-permute-start(bf16[192,640]{1,0:T(8,128)(2,1)} %get-tuple-element.128), channel_id=1, source_target_pairs={{0,4},{1,8},{2,12},{3,0},{4,6},{5,10},{6,14},{7,2},{8,5},{9,9},{10... | collective-permute-start | bytes 737288 | tf_op jit(solution)/shard_map/ppermute | solution.py:89
  16.5 19.7 %collective-permute-start.2 = (bf16[192,640]{1,0:T(8,128)(2,1)}, bf16[192,640]{1,0:T(8,128)(2,1)S(1)}, u32[]{:S(2)}, u32[]{:S(2)}) collective-permute-start(bf16[192,640]{1,0:T(8,128)(2,1)} %get-tuple-element.129), channel_id=1, source_target_pairs={{0,8},{1,12},{2,0},{3,4},{4,10},{5,14},{6,2},{7,6},{8,9},{9,13},{1... | collective-permute-start | bytes 737288 | tf_op jit(solution)/shard_map/ppermute | solution.py:89
  20.1 35.9 %collective-permute-start.3 = (bf16[192,640]{1,0:T(8,128)(2,1)}, bf16[192,640]{1,0:T(8,128)(2,1)S(1)}, u32[]{:S(2)}, u32[]{:S(2)}) collective-permute-start(bf16[192,640]{1,0:T(8,128)(2,1)} %get-tuple-element.130), channel_id=1, source_target_pairs={{0,12},{1,0},{2,4},{3,8},{4,14},{5,2},{6,6},{7,10},{8,13},{9,1},{1... | collective-permute-start | bytes 737288 | tf_op jit(solution)/shard_map/ppermute | solution.py:89
  24.6 31.3 %collective-permute-start = (bf16[192,640]{1,0:T(8,128)(2,1)}, bf16[192,640]{1,0:T(8,128)(2,1)S(1)}, u32[]{:S(2)}, u32[]{:S(2)}) collective-permute-start(bf16[192,640]{1,0:T(8,128)(2,1)} %get-tuple-element.127), channel_id=1, source_target_pairs={{0,0},{1,4},{2,8},{3,12},{4,2},{5,6},{6,10},{7,14},{8,1},{9,5},{10... | collective-permute-start | bytes 737288 | tf_op jit(solution)/shard_map/ppermute | solution.py:89
  59.8 11.1 %collective-permute-start.5 = (bf16[768,256]{1,0:T(8,128)(2,1)S(1)}, bf16[768,256]{1,0:T(8,128)(2,1)S(1)}, u32[]{:S(2)}, u32[]{:S(2)}) collective-permute-start(bf16[768,256]{1,0:T(8,128)(2,1)S(1)} %get-tuple-element.137.rest_0_.refs_2_), channel_id=1, source_target_pairs={{0,8},{4,12},{8,0},{12,4},{1,9},{5,13},{9,1},{13,5},{2,10},{6,14},... | collective-permute-start | bytes 1179656 | tf_op jit(solution)/shard_map/ppermute | solution.py:29
  74.9 136.8 %reduce-scatter.2.cloned.1.call-start = ((), (), s32[]{:S(2)}) async-start(), calls=%async_computation.3 | async-start | bytes 3194880 | tf_op jit(solution)/shard_map/reduce_scatter | solution.py:915
  94.6 12.0 %collective-permute-start.10 = (bf16[768,256]{1,0:T(8,128)(2,1)S(1)}, bf16[768,256]{1,0:T(8,128)(2,1)S(1)}, u32[]{:S(2)}, u32[]{:S(2)}) collective-permute-start(bf16[768,256]{1,0:T(8,128)(2,1)S(1)} %add_convert_fusion.3), channel_id=1, source_target_pairs={{0,8},{4,12},{8,0},{12,4},{1,9},{5,13},{9,1},{13,5},{2,10},{6,14},... | collective-permute-start | bytes 1179656 | tf_op jit(solution)/shard_map/ppermute | solution.py:29
  96.2 18.9 %collective-permute-start.13 = (bf16[768,256]{1,0:T(8,128)(2,1)S(1)}, bf16[768,256]{1,0:T(8,128)(2,1)S(1)}, u32[]{:S(2)}, u32[]{:S(2)}) collective-permute-start(bf16[768,256]{1,0:T(8,128)(2,1)S(1)} %branch_grad.1.rest_1_.refs_12_), channel_id=1, source_target_pairs={{0,8},{4,12},{8,0},{12,4},{1,9},{5,13},{9,1},{13,5},{2,10},{6,14},... | collective-permute-start | bytes 1179656 | tf_op jit(solution)/shard_map/ppermute | solution.py:29
  107.4 15.3 %collective-permute-start.12 = (bf16[768,256]{1,0:T(8,128)(2,1)S(1)}, bf16[768,256]{1,0:T(8,128)(2,1)S(1)}, u32[]{:S(2)}, u32[]{:S(2)}) collective-permute-start(bf16[768,256]{1,0:T(8,128)(2,1)S(1)} %get-tuple-element.152.rest_0_.refs_4_), channel_id=1, source_target_pairs={{0,8},{4,12},{8,0},{12,4},{1,9},{5,13},{9,1},{13,5},{2,10},{6,14},... | collective-permute-start | bytes 1179656 | tf_op jit(solution)/shard_map/ppermute | solution.py:29
  115.1 7.6 %collective-permute-start.15 = (bf16[768,256]{1,0:T(8,128)(2,1)S(1)}, bf16[768,256]{1,0:T(8,128)(2,1)S(1)}, u32[]{:S(2)}, u32[]{:S(2)}) collective-permute-start(bf16[768,256]{1,0:T(8,128)(2,1)S(1)} %collective-permute-done.13.rest_5_.refs_14_), channel_id=1, source_target_pairs={{0,4},{4,0},{8,12},{12,8},{1,5},{5,1},{9,13},{13,9},{2,6},{6,2},{1... | collective-permute-start | bytes 1179656 | tf_op jit(solution)/shard_map/ppermute | solution.py:29
  115.1 7.6 %collective-permute-start.11 = (bf16[768,256]{1,0:T(8,128)(2,1)S(1)}, bf16[768,256]{1,0:T(8,128)(2,1)S(1)}, u32[]{:S(2)}, u32[]{:S(2)}) collective-permute-start(bf16[768,256]{1,0:T(8,128)(2,1)S(1)} %get-tuple-element.152.rest_0_.refs_4_), channel_id=1, source_target_pairs={{0,4},{4,0},{8,12},{12,8},{1,5},{5,1},{9,13},{13,9},{2,6},{6,2},{1... | collective-permute-start | bytes 1179656 | tf_op jit(solution)/shard_map/ppermute | solution.py:29
  140.0 11.2 %collective-permute-start.17 = (bf16[768,256]{1,0:T(8,128)(2,1)S(1)}, bf16[768,256]{1,0:T(8,128)(2,1)S(1)}, u32[]{:S(2)}, u32[]{:S(2)}) collective-permute-start(bf16[768,256]{1,0:T(8,128)(2,1)S(1)} %add_convert_fusion.2), channel_id=1, source_target_pairs={{0,8},{4,12},{8,0},{12,4},{1,9},{5,13},{9,1},{13,5},{2,10},{6,14},... | collective-permute-start | bytes 1179656 | tf_op jit(solution)/shard_map/ppermute | solution.py:29
  151.2 14.5 %collective-permute-start.21 = (bf16[1536,256]{1,0:T(8,128)(2,1)}, bf16[1536,256]{1,0:T(8,128)(2,1)S(1)}, u32[]{:S(2)}, u32[]{:S(2)}) collective-permute-start(bf16[1536,256]{1,0:T(8,128)(2,1)} %get-tuple-element.189), channel_id=1, source_target_pairs={{0,4},{4,0},{8,12},{12,8},{1,5},{5,1},{9,13},{13,9},{2,6},{6,2},{1... | collective-permute-start | bytes 2359304 | tf_op jit(solution)/shard_map/ppermute | solution.py:29
  154.1 11.5 %collective-permute-start.18 = (bf16[768,256]{1,0:T(8,128)(2,1)S(1)}, bf16[768,256]{1,0:T(8,128)(2,1)S(1)}, u32[]{:S(2)}, u32[]{:S(2)}) collective-permute-start(bf16[768,256]{1,0:T(8,128)(2,1)S(1)} %get-tuple-element.174.first.refs_6_), channel_id=1, source_target_pairs={{0,8},{4,12},{8,0},{12,4},{1,9},{5,13},{9,1},{13,5},{2,10},{6,14},... | collective-permute-start | bytes 1179656 | tf_op jit(solution)/shard_map/ppermute | solution.py:29
  165.8 12.5 %collective-permute-start.22 = (bf16[768,256]{1,0:T(8,128)(2,1)S(1)}, bf16[768,256]{1,0:T(8,128)(2,1)S(1)}, u32[]{:S(2)}, u32[]{:S(2)}) collective-permute-start(bf16[768,256]{1,0:T(8,128)(2,1)S(1)} %add_convert_fusion.1), channel_id=1, source_target_pairs={{0,8},{4,12},{8,0},{12,4},{1,9},{5,13},{9,1},{13,5},{2,10},{6,14},... | collective-permute-start | bytes 1179656 | tf_op jit(solution)/shard_map/ppermute | solution.py:29
  182.0 11.3 %collective-permute-start.24 = (bf16[768,256]{1,0:T(8,128)(2,1)S(1)}, bf16[768,256]{1,0:T(8,128)(2,1)S(1)}, u32[]{:S(2)}, u32[]{:S(2)}) collective-permute-start(bf16[768,256]{1,0:T(8,128)(2,1)S(1)} %add_convert_fusion), channel_id=1, source_target_pairs={{0,8},{4,12},{8,0},{12,4},{1,9},{5,13},{9,1},{13,5},{2,10},{6,14},... | collective-permute-start | bytes 1179656 | tf_op jit(solution)/shard_map/ppermute | solution.py:29
  193.2 27.4 %collective-permute-start.40 = (bf16[4,96,768]{2,1,0:T(8,128)(2,1)S(1)}, bf16[4,96,768]{2,1,0:T(8,128)(2,1)S(1)}, u32[]{:S(2)}, u32[]{:S(2)}) collective-permute-start(bf16[4,96,768]{2,1,0:T(8,128)(2,1)S(1)} %copy-done.42), channel_id=1, source_target_pairs={{0,16},{16,0},{1,17},{17,1},{2,18},{18,2},{3,19},{19,3},{4,20},{20... | collective-permute-start | bytes 1769480 | tf_op jit(solution)/shard_map/ppermute | solution.py:29
  195.8 11.6 %collective-permute-start.25 = (bf16[192,384]{1,0:T(8,128)(2,1)S(1)}, bf16[192,384]{1,0:T(8,128)(2,1)S(1)}, u32[]{:S(2)}, u32[]{:S(2)}) collective-permute-start(bf16[192,384]{1,0:T(8,128)(2,1)S(1)} %get-tuple-element.208), channel_id=1, source_target_pairs={{0,0},{4,1},{8,2},{12,3},{2,4},{6,5},{10,6},{14,7},{1,8},{5,9},{9,... | collective-permute-start | bytes 442376 | tf_op jit(solution)/shard_map/ppermute | solution.py:89
  196.5 10.9 %collective-permute-start.26 = (bf16[192,384]{1,0:T(8,128)(2,1)S(1)}, bf16[192,384]{1,0:T(8,128)(2,1)S(1)}, u32[]{:S(2)}, u32[]{:S(2)}) collective-permute-start(bf16[192,384]{1,0:T(8,128)(2,1)S(1)} %get-tuple-element.209), channel_id=1, source_target_pairs={{4,0},{8,1},{12,2},{0,3},{6,4},{10,5},{14,6},{2,7},{5,8},{9,9},{13... | collective-permute-start | bytes 442376 | tf_op jit(solution)/shard_map/ppermute | solution.py:89
  203.5 8.2 %collective-permute-start.28 = (bf16[192,384]{1,0:T(8,128)(2,1)S(1)}, bf16[192,384]{1,0:T(8,128)(2,1)S(1)}, u32[]{:S(2)}, u32[]{:S(2)}) collective-permute-start(bf16[192,384]{1,0:T(8,128)(2,1)S(1)} %get-tuple-element.211), channel_id=1, source_target_pairs={{12,0},{0,1},{4,2},{8,3},{14,4},{2,5},{6,6},{10,7},{13,8},{1,9},{5... | collective-permute-start | bytes 442376 | tf_op jit(solution)/shard_map/ppermute | solution.py:89
  211.7 49.7 %collective-permute-start.45 = (bf16[208,1536]{1,0:T(8,128)(2,1)}, bf16[208,1536]{1,0:T(8,128)(2,1)S(1)}, u32[]{:S(2)}, u32[]{:S(2)}) collective-permute-start(bf16[208,1536]{1,0:T(8,128)(2,1)} %reduce-scatter.2.cloned.1.call-done.rest_0_), channel_id=1, source_target_pairs={{0,16},{16,0},{1,17},{17,1},{2,18},{18,2},{3,19},{19,3},{4,20},{20... | collective-permute-start | bytes 1916936 | tf_op jit(solution)/shard_map/ppermute | solution.py:29
  214.1 11.2 %collective-permute-start.33 = (f32[1,64,192]{2,1,0:T(8,128)S(1)}, f32[1,64,192]{2,1,0:T(8,128)S(1)}, u32[]{:S(2)}, u32[]{:S(2)}) collective-permute-start(f32[1,64,192]{2,1,0:T(8,128)S(1)} %get-tuple-element.217), channel_id=1, source_target_pairs={{0,4},{4,0},{8,12},{12,8},{1,5},{5,1},{9,13},{13,9},{2,6},{6,2},{1... | collective-permute-start | bytes 147464 | tf_op jit(solution)/shard_map/ppermute | solution.py:29
  220.9 16.3 %collective-permute-start.42 = (bf16[96,768]{1,0:T(8,128)(2,1)S(1)}, bf16[96,768]{1,0:T(8,128)(2,1)S(1)}, u32[]{:S(2)}, u32[]{:S(2)}) collective-permute-start(bf16[96,768]{1,0:T(8,128)(2,1)S(1)} %get-tuple-element.227), channel_id=1, source_target_pairs={{0,2},{1,3},{2,0},{3,1},{4,6},{5,7},{6,4},{7,5},{8,10},{9,11},{10,... | collective-permute-start | bytes 442376 | tf_op jit(solution)/shard_map/ppermute | solution.py:29
  221.0 16.8 %collective-permute-start.43 = (bf16[96,768]{1,0:T(8,128)(2,1)S(1)}, bf16[96,768]{1,0:T(8,128)(2,1)S(1)}, u32[]{:S(2)}, u32[]{:S(2)}) collective-permute-start(bf16[96,768]{1,0:T(8,128)(2,1)S(1)} %get-tuple-element.228), channel_id=1, source_target_pairs={{0,3},{1,2},{2,1},{3,0},{4,7},{5,6},{6,5},{7,4},{8,11},{9,10},{10,... | collective-permute-start | bytes 442376 | tf_op jit(solution)/shard_map/ppermute | solution.py:29
  225.3 12.5 %collective-permute-start.29 = (bf16[192,256]{1,0:T(8,128)(2,1)S(1)}, bf16[192,256]{1,0:T(8,128)(2,1)S(1)}, u32[]{:S(2)}, u32[]{:S(2)}) collective-permute-start(bf16[192,256]{1,0:T(8,128)(2,1)S(1)} %get-tuple-element.212), channel_id=1, source_target_pairs={{0,0},{4,1},{8,2},{12,3},{2,4},{6,5},{10,6},{14,7},{1,8},{5,9},{9,... | collective-permute-start | bytes 294920 | tf_op jit(solution)/shard_map/ppermute | solution.py:89
  228.0 11.4 %collective-permute-start.36 = (f32[2,64,192]{2,1,0:T(8,128)S(1)}, f32[2,64,192]{2,1,0:T(8,128)S(1)}, u32[]{:S(2)}, u32[]{:S(2)}) collective-permute-start(f32[2,64,192]{2,1,0:T(8,128)S(1)} %constant_dynamic-update-slice_fusion.rest_4_), channel_id=1, source_target_pairs={{0,24},{4,28},{8,16},{12,20},{16,8},{20,12},{24,0},{28,4},{1,25},{... | collective-permute-start | bytes 294920 | tf_op jit(solution)/shard_map/ppermute | solution.py:990
  237.8 22.6 %collective-permute-start.44 = (bf16[96,768]{1,0:T(8,128)(2,1)S(1)}, bf16[96,768]{1,0:T(8,128)(2,1)S(1)}, u32[]{:S(2)}, u32[]{:S(2)}) collective-permute-start(bf16[96,768]{1,0:T(8,128)(2,1)S(1)} %block_sum.1.own), channel_id=1, source_target_pairs={{0,16},{16,0},{1,17},{17,1},{2,18},{18,2},{3,19},{19,3},{4,20},{20... | collective-permute-start | bytes 442376 | tf_op jit(solution)/shard_map/ppermute | solution.py:29
  239.4 12.4 %collective-permute-start.30 = (bf16[192,256]{1,0:T(8,128)(2,1)S(1)}, bf16[192,256]{1,0:T(8,128)(2,1)S(1)}, u32[]{:S(2)}, u32[]{:S(2)}) collective-permute-start(bf16[192,256]{1,0:T(8,128)(2,1)S(1)} %get-tuple-element.213), channel_id=1, source_target_pairs={{4,0},{8,1},{12,2},{0,3},{6,4},{10,5},{14,6},{2,7},{5,8},{9,9},{13... | collective-permute-start | bytes 294920 | tf_op jit(solution)/shard_map/ppermute | solution.py:89
  243.7 9.4 %collective-permute-start.31 = (bf16[192,256]{1,0:T(8,128)(2,1)S(1)}, bf16[192,256]{1,0:T(8,128)(2,1)S(1)}, u32[]{:S(2)}, u32[]{:S(2)}) collective-permute-start(bf16[192,256]{1,0:T(8,128)(2,1)S(1)} %get-tuple-element.214), channel_id=1, source_target_pairs={{8,0},{12,1},{0,2},{4,3},{10,4},{14,5},{2,6},{6,7},{9,8},{13,9},{1... | collective-permute-start | bytes 294920 | tf_op jit(solution)/shard_map/ppermute | solution.py:89
  244.5 9.1 %collective-permute-start.32 = (bf16[192,256]{1,0:T(8,128)(2,1)S(1)}, bf16[192,256]{1,0:T(8,128)(2,1)S(1)}, u32[]{:S(2)}, u32[]{:S(2)}) collective-permute-start(bf16[192,256]{1,0:T(8,128)(2,1)S(1)} %get-tuple-element.215), channel_id=1, source_target_pairs={{12,0},{0,1},{4,2},{8,3},{14,4},{2,5},{6,6},{10,7},{13,8},{1,9},{5... | collective-permute-start | bytes 294920 | tf_op jit(solution)/shard_map/ppermute | solution.py:89
  (60 other events, 960.8 us)
Sparse Core Ops, SparseCore 0:
  14.3 58.8 all-gather.2
  75.3 50.6 all-gather.4
  151.3 49.6 reduce-scatter.1
